TPU v7x, 32 devices: a whole 2x2x4 slice. The times are simulated.
32 devices in a mesh: vec: 4 (over y, core), dom: 8 (over z, x).
Axes of the slice: x: 2, y: 2, z: 4, core: 2. Of those that a mesh axis runs over, the one named last changes fastest.
Arguments:
- probe: float32 [16, 1024, 256], P('vec', 'dom'), may hold values from -5 to 5
- cheb_prev: float32 [16, 1024, 256], P('vec', 'dom'), may hold values from -6 to 6
- cheb_cur: float32 [16, 1024, 256], P('vec', 'dom'), may hold values from -6 to 6
- prior_moments: float32 [124, 1024, 256], P(None, ('dom', 'vec')), may hold values from -3 to 3
- site_terms: float32 [3, 1024, 128], P(None, 'dom'), may hold values from -0.3 to 0.3
- hop_kinds: float32 [8, 256, 256], replicated, may hold values from -0.09375 to 0.09375
- tile_kind_ids: int32 [1024, 4], P('dom'), may hold values from 0 to 7
- send_lists: int32 [8, 2, 48], P('dom'), may hold values from -1 to 127, as said below
- tile_cols: int32 [1024, 4], P('dom'), may hold values from 0 to 223, as said below
Outputs:
- next_prev: float32 [16, 1024, 256], P('vec', 'dom')
- next_cur: float32 [16, 1024, 256], P('vec', 'dom')
- new_moments: float32 [4, 1024, 256], P(None, ('dom', 'vec'))
- energy_map: float32 [512, 1024, 256], P(None, ('dom', 'vec'))
Inputs may be any that keep to these rules, and one draw needn't show every extreme that they name: send_lists[d, 0] names local blocks of domain d sent to domain (d + 1) mod 8, send_lists[d, 1] those sent to domain (d - 1) mod 8; the valid entries come first and are distinct within the domain, the rest are -1; some domain sends 48 blocks one way. `tile_cols`: an entry e < 128 names the domain's own block e, 128 <= e < 176 names slot e - 128 of what the lower neighbour sends up, larger e slot e - 176 of what the upper neighbour sends down; only valid slots are named; link 0 of each block row is the block itself.
All inputs are finite; a program needn't handle non-finite values.
Results may differ from a plain program's by a relative error of at most 0.0001.
Values sent between devices are 32-bit elements; how exact they have to be, the bound alone decides.
No kernel may reach another device: no remote copies, remote signals or barrier semaphores. Data moves between devices by JAX's collectives and lax.ppermute only.
A program may use at most 128 MiB of HBM per device.

v0:
```python
import functools
import math

import jax
import jax.numpy as jnp
import numpy as np
from jax import lax
from jax.experimental import pallas as pl
from jax.experimental.pallas import tpu as pltpu
from jax.sharding import PartitionSpec as P

ENERGIES = 512
STEPS = 4
F32 = jnp.float32
BF16 = jnp.bfloat16
VMEM_LIMIT = 24 * 1024 * 1024


def split(x):
    high = x.astype(BF16)
    return high, (x - high.astype(F32)).astype(BF16)


def dot(a, b):
    return jnp.dot(a, b, preferred_element_type=F32)


def jackson_split(moment_count, energy_count):
    m = np.arange(moment_count, dtype=np.float64)
    step = math.pi / (moment_count + 1.0)
    damping = (
        (moment_count - m + 1.0) * np.cos(step * m) + np.sin(step * m) / math.tan(step)
    ) / (moment_count + 1.0)
    weights = np.where(m == 0, damping, 2.0 * damping)
    angles = math.pi * (np.arange(energy_count) + 0.5) / energy_count
    table = (weights[None, :] * np.cos(angles[:, None] * m[None, :])).astype(np.float32)
    high = table.astype(BF16)
    low = (table - high.astype(np.float32)).astype(BF16)
    return np.concatenate([high, low], axis=1), high


def vmem():
    return pl.BlockSpec(memory_space=pltpu.VMEM)


def smem():
    return pl.BlockSpec(memory_space=pltpu.SMEM)


def params(limit=VMEM_LIMIT):
    return pltpu.CompilerParams(vmem_limit_bytes=limit)


def cost(flops, size):
    return pl.CostEstimate(flops=int(flops), bytes_accessed=int(size), transcendentals=0)


def gather_rows(onehot, value):
    high, low = split(value)
    return dot(onehot, jnp.concatenate([high, low], axis=0))


def first_kernel(rim, vecs, parity_ref, lists_ref, cur_ref, pick_ref, *sends):
    blocks = cur_ref.shape[1]
    width = cur_ref.shape[2]
    lists = lists_ref[0]
    even = parity_ref[0] == 0
    rows = lax.broadcasted_iota(jnp.int32, (rim, rim), 0)
    lanes = lax.broadcasted_iota(jnp.int32, (rim, rim), 1)
    slots = lax.broadcasted_iota(jnp.int32, (rim, blocks), 1)
    for half in range(2):
        mine = lists[half : half + 1]
        other = lists[1 - half : 2 - half]
        chosen = jnp.where(even, mine, other)
        spread = jnp.where(rows == lanes, chosen, 0).astype(F32)
        column = jnp.sum(spread, axis=1, keepdims=True).astype(jnp.int32)
        onehot = jnp.where(slots == column, 1.0, 0.0).astype(BF16)
        pick_ref[pl.ds(half * rim, rim), 0:blocks] = onehot
        pick_ref[pl.ds(half * rim, rim), blocks : 2 * blocks] = onehot
    pick = pick_ref[...]
    for v in range(cur_ref.shape[0]):
        chunk, place = divmod(v, vecs)
        got = gather_rows(pick, cur_ref[v])
        for half in range(2):
            sends[2 * chunk + half][:, place * width : (place + 1) * width] = got[
                half * rim : (half + 1) * rim
            ]


def prep_kernel(rim, parity_ref, cols_ref, ids_ref, kinds_ref, mix_ref, high_ref, low_ref):
    blocks, links = cols_ref.shape
    kind_count, width = kinds_ref.shape[:2]
    padded = mix_ref.shape[1] // 2
    even = parity_ref[0] == 0
    lanes = lax.broadcasted_iota(jnp.int32, (blocks, padded), 1)
    hits = []
    for k in range(links):
        e = cols_ref[:, k : k + 1]
        crossed = jnp.where(e < blocks + rim, e + rim, e - rim)
        e = jnp.where(jnp.logical_and(even, e >= blocks), crossed, e)
        hits.append(jnp.where(lanes == e, 1.0, 0.0))
    for n in range(kind_count):
        total = jnp.zeros((blocks, padded), F32)
        for k in range(links):
            total += jnp.where(ids_ref[:, k : k + 1] == n, hits[k], 0.0)
        total = total.astype(BF16)
        mix_ref[n * blocks : (n + 1) * blocks, 0:padded] = total
        mix_ref[n * blocks : (n + 1) * blocks, padded : 2 * padded] = total
        high, low = split(2.0 * kinds_ref[n])
        high_ref[n * width : (n + 1) * width] = high
        low_ref[n * width : (n + 1) * width] = low


def step_kernel(
    cfg,
    index_ref,
    mix_ref,
    high_ref,
    low_ref,
    pick_ref,
    site_ref,
    cur_ref,
    prev_ref,
    probe_ref,
    recv_a,
    recv_b,
    *rest,
):
    chunk, last, add_partial, older, has_alias = cfg
    rest = list(rest)
    partial_in = rest.pop(0) if add_partial else None
    olders = [rest.pop(0) for _ in range(older)]
    if has_alias:
        rest.pop(0)
    out_ref = rest.pop(0)
    if last:
        partial_out = rest.pop(0)
        keep_ref = rest.pop(0) if older else None
        give_ref = rest.pop(0) if older else None
    else:
        send_a, send_b, partial_out = rest.pop(0), rest.pop(0), rest.pop(0)
    source, mixed = rest
    vecs, blocks, width = cur_ref.shape
    rim = recv_a.shape[0]
    padded = source.shape[1] // 2
    kind_count = mix_ref.shape[0] // blocks
    spin = width // 2
    for v in range(vecs):
        columns = slice(v * width, (v + 1) * width)
        pieces = [cur_ref[v], recv_a[:, columns], recv_b[:, columns]]
        used = blocks + 2 * rim
        if used < padded:
            pieces.append(jnp.zeros((padded - used, width), F32))
        high, low = split(jnp.concatenate(pieces, axis=0))
        source[v, 0:padded] = high
        source[v, padded : 2 * padded] = low
    for v in range(vecs):
        mixture = dot(mix_ref[...], source[v])
        high, low = split(mixture)
        for n in range(kind_count):
            columns = slice(n * width, (n + 1) * width)
            rows = slice(n * blocks, (n + 1) * blocks)
            mixed[v * blocks : (v + 1) * blocks, columns] = high[rows]
            mixed[(vecs + v) * blocks : (vecs + v + 1) * blocks, columns] = low[rows]
    count = vecs * blocks
    both = dot(mixed[...], high_ref[...])
    hopping = both[:count] + both[count:] + dot(mixed[:count], low_ref[...])
    diag_up = 2.0 * (site_ref[0] + site_ref[1])
    diag_down = 2.0 * (site_ref[0] - site_ref[1])
    cross = 2.0 * site_ref[2]
    partial = partial_in[...] if add_partial else None
    for v in range(vecs):
        here = cur_ref[v]
        up = here[:, :spin]
        down = here[:, spin:]
        onsite = jnp.concatenate(
            [diag_up * up + cross * down, diag_down * down + cross * up], axis=1
        )
        following = hopping[v * blocks : (v + 1) * blocks] + onsite - prev_ref[v]
        out_ref[v] = following
        term = probe_ref[v] * following
        partial = term if partial is None else partial + term
        if not last:
            got = gather_rows(pick_ref[...], following)
            send_a[:, v * width : (v + 1) * width] = got[:rim]
            send_b[:, v * width : (v + 1) * width] = got[rim:]
    partial_out[...] = partial
    if last and older:
        groups, cores = index_ref[2], 2
        quarter = keep_ref.shape[2]
        core = index_ref[1]
        for s in range(older + 1):
            ref = olders[s] if s < older else partial_out
            for y in range(keep_ref.shape[1]):
                base = y * cores * quarter
                keep_ref[s, y] = ref[pl.ds(pl.multiple_of(base + core * quarter, quarter), quarter)]
                give_ref[s, y] = ref[
                    pl.ds(pl.multiple_of(base + (1 - core) * quarter, quarter), quarter)
                ]


def fold_kernel(index_ref, keep_ref, got_ref, mine_ref, give_ref):
    y = index_ref[2]
    mine_ref[...] = keep_ref[:, y] + got_ref[:, y]
    give_ref[...] = keep_ref[:, 1 - y] + got_ref[:, 1 - y]


def energy_kernel(vector_total, both_ref, high_ref, prior_ref, mine_ref, got_ref, new_ref, map_ref, moments):
    prior_count, group, lanes = prior_ref.shape
    steps = mine_ref.shape[0]
    energies = both_ref.shape[0]
    new = (mine_ref[...] + got_ref[...]) * (1.0 / vector_total)
    new_ref[...] = new
    moments[0 : prior_count * group] = prior_ref[...].reshape(prior_count * group, lanes)
    moments[prior_count * group :] = new.reshape(steps * group, lanes)
    flat = map_ref.reshape(energies * group, lanes)
    for b in range(0, group, 2):
        pair = [moments[pl.ds(b + i, prior_count + steps, stride=group)] for i in range(2)]
        high, low = split(jnp.concatenate(pair, axis=1))
        value = dot(both_ref[...], jnp.concatenate([high, high], axis=0)) + dot(high_ref[...], low)
        for i in range(2):
            flat[pl.ds(b + i, energies, stride=group)] = value[:, i * lanes : (i + 1) * lanes]


def per_device(
    probe,
    cheb_prev,
    cheb_cur,
    prior_moments,
    site_terms,
    hop_kinds,
    tile_kind_ids,
    send_lists,
    tile_cols,
):
    vec_dev, blocks, width = cheb_cur.shape
    kind_count = hop_kinds.shape[0]
    groups = lax.axis_size("vec")
    domains = lax.axis_size("dom")
    rim = send_lists.shape[2]
    chunks = 2
    vecs = vec_dev // chunks
    quarter = blocks // groups
    padded = -(-(blocks + 2 * rim) // 256) * 256
    swap_a = [(i, i ^ 1) for i in range(domains)]
    swap_b = [(i, (i + 1) % domains if i % 2 else (i - 1) % domains) for i in range(domains)]
    vec_index = lax.axis_index("vec")
    index = jnp.stack([lax.axis_index("dom") % 2, vec_index % 2, vec_index // 2]).astype(jnp.int32)

    rows = jax.ShapeDtypeStruct((rim, vecs * width), F32)
    first = pl.pallas_call(
        functools.partial(first_kernel, rim, vecs),
        out_shape=[jax.ShapeDtypeStruct((2 * rim, 2 * blocks), BF16)] + [rows] * (2 * chunks),
        in_specs=[smem(), vmem(), vmem()],
        out_specs=[vmem()] * (1 + 2 * chunks),
        compiler_params=params(),
        cost_estimate=cost(1e8, 1e6),
        name="first_sends",
    )(index, send_lists, cheb_cur)
    pick, sends = first[0], list(first[1:])

    def exchange(a, b):
        got_b = lax.ppermute(b, "dom", swap_b)
        got_a = lax.ppermute(a, "dom", swap_a)
        return got_a, got_b

    received = [exchange(sends[2 * c], sends[2 * c + 1]) for c in range(chunks)]

    mix, high, low = pl.pallas_call(
        functools.partial(prep_kernel, rim),
        out_shape=[
            jax.ShapeDtypeStruct((kind_count * blocks, 2 * padded), BF16),
            jax.ShapeDtypeStruct((kind_count * width, width), BF16),
            jax.ShapeDtypeStruct((kind_count * width, width), BF16),
        ],
        in_specs=[smem()] + [vmem()] * 3,
        out_specs=[vmem()] * 3,
        compiler_params=params(),
        cost_estimate=cost(1e7, 8e6),
        name="tables",
    )(index, tile_cols, tile_kind_ids, hop_kinds)

    def chunk_spec(c):
        return pl.BlockSpec((vecs, blocks, width), lambda i: (c, 0, 0))

    whole = chunk_spec(0)
    partial_shape = jax.ShapeDtypeStruct((blocks, width), F32)
    rows_spec = pl.BlockSpec((rim, vecs * width), lambda i: (0, 0))
    partial_spec = pl.BlockSpec((blocks, width), lambda i: (0, 0))
    full_shape = jax.ShapeDtypeStruct((vec_dev, blocks, width), F32)
    chunk_shape = jax.ShapeDtypeStruct((vecs, blocks, width), F32)

    current = [(cheb_cur, c) for c in range(chunks)]
    previous = [(cheb_prev, c) for c in range(chunks)]
    partials = []
    keep = give = None
    for s in range(STEPS):
        last = s == STEPS - 1
        emit = s >= STEPS - 2
        partial = None
        buffer = None
        for c in range(chunks):
            final = last and c == chunks - 1
            args = [index, mix, high, low, pick, site_terms, current[c][0], previous[c][0], probe]
            specs = [
                smem(),
                pl.BlockSpec((kind_count * blocks, 2 * padded), lambda i: (0, 0)),
                pl.BlockSpec((kind_count * width, width), lambda i: (0, 0)),
                pl.BlockSpec((kind_count * width, width), lambda i: (0, 0)),
                pl.BlockSpec((2 * rim, 2 * blocks), lambda i: (0, 0)),
                pl.BlockSpec(site_terms.shape, lambda i: (0, 0, 0)),
                chunk_spec(current[c][1]),
                chunk_spec(previous[c][1]),
                chunk_spec(c),
                rows_spec,
                rows_spec,
            ]
            args += list(received[c])
            if partial is not None:
                args.append(partial)
                specs.append(partial_spec)
            older = len(partials) if final else 0
            if older:
                args += partials
                specs += [partial_spec] * older
            aliases = {}
            if emit and buffer is not None:
                aliases = {len(args): 0}
                args.append(buffer)
                specs.append(pl.BlockSpec(memory_space=pl.ANY))
            outs = [full_shape if emit else chunk_shape]
            out_specs = [chunk_spec(c) if emit else whole]
            if not last:
                outs += [rows, rows]
                out_specs += [rows_spec, rows_spec]
            outs.append(partial_shape)
            out_specs.append(partial_spec)
            if older:
                pair = jax.ShapeDtypeStruct((older + 1, groups // 2, quarter, width), F32)
                outs += [pair, pair]
                out_specs += [pl.BlockSpec(pair.shape, lambda i: (0, 0, 0, 0))] * 2
            result = pl.pallas_call(
                functools.partial(
                    step_kernel, (c, last, partial is not None, older, bool(aliases))
                ),
                out_shape=outs,
                grid=(1,),
                in_specs=specs,
                out_specs=out_specs,
                scratch_shapes=[
                    pltpu.VMEM((vecs, 2 * padded, width), BF16),
                    pltpu.VMEM((2 * vecs * blocks, kind_count * width), BF16),
                ],
                input_output_aliases=aliases,
                compiler_params=params(),
                cost_estimate=cost(1.5e9, 5e6),
                name=f"step{s}_{c}",
            )(*args)
            following = result[0]
            if emit:
                buffer = following
            partial = result[1] if last else result[3]
            previous[c] = current[c]
            current[c] = (following, c if emit else 0)
            if not last:
                received[c] = exchange(result[1], result[2])
            elif older:
                keep, give = result[2], result[3]
        if emit:
            for c in range(chunks):
                current[c] = (buffer, c)
        partials.append(partial)

    got = lax.ppermute(give, "vec", [(i, i ^ 1) for i in range(groups)])
    piece = jax.ShapeDtypeStruct((STEPS, quarter, width), F32)
    mine, give = pl.pallas_call(
        fold_kernel,
        out_shape=[piece, piece],
        in_specs=[smem(), vmem(), vmem()],
        out_specs=[vmem(), vmem()],
        compiler_params=params(),
        cost_estimate=cost(1e5, 1e6),
        name="fold",
    )(index, keep, got)
    got = lax.ppermute(give, "vec", [(i, i ^ 2) for i in range(groups)])

    prior_count = prior_moments.shape[0]
    moment_count = prior_count + STEPS
    both, top = jackson_split(moment_count, ENERGIES)
    group, lanes = 8, 128
    small = pl.BlockSpec((STEPS, group, lanes), lambda i, h: (0, i, h))
    new_moments, energy_map = pl.pallas_call(
        functools.partial(energy_kernel, vec_dev * groups),
        out_shape=[piece, jax.ShapeDtypeStruct((ENERGIES, quarter, width), F32)],
        grid=(quarter // group, width // lanes),
        in_specs=[
            pl.BlockSpec((ENERGIES, 2 * moment_count), lambda i, h: (0, 0)),
            pl.BlockSpec((ENERGIES, moment_count), lambda i, h: (0, 0)),
            pl.BlockSpec((prior_count, group, lanes), lambda i, h: (0, i, h)),
            small,
            small,
        ],
        out_specs=[small, pl.BlockSpec((ENERGIES, group, lanes), lambda i, h: (0, i, h))],
        scratch_shapes=[pltpu.VMEM((moment_count * group, lanes), F32)],
        compiler_params=params(),
        cost_estimate=cost(4e9, 2.2e7),
        name="energy",
    )(jnp.asarray(both), jnp.asarray(top), prior_moments, mine, got)
    return current_outputs(previous, current) + (new_moments, energy_map)


def current_outputs(previous, current):
    return previous[0][0], current[0][0]


def solution(mesh):
    return jax.shard_map(
        per_device,
        mesh=mesh,
        in_specs=(
            P("vec", "dom", None),
            P("vec", "dom", None),
            P("vec", "dom", None),
            P(None, ("dom", "vec"), None),
            P(None, "dom", None),
            P(),
            P("dom", None),
            P("dom", None, None),
            P("dom", None),
        ),
        out_specs=(
            P("vec", "dom", None),
            P("vec", "dom", None),
            P(None, ("dom", "vec"), None),
            P(None, ("dom", "vec"), None),
        ),
        check_vma=False,
    )
```

profile of v0, /device:TPU:0, one launch (start us, length us, event | category | flops | bytes accessed | tf_op | source)
XLA Modules:
  0.0 84.9 jit_solution(14895511789215071630)
XLA Ops:
  0.7 1.0 %copy-done.4 = f32[4,128,256]{2,1,0:T(8,128)S(1)} copy-done((f32[4,128,256]{2,1,0:T(8,128)S(1)}, f32[4,128,256]{2,1,0:T(8,128)}, u32[]{:S(2)}) %copy-start.4) | copy-done | bytes 524312
  2.5 0.8 first_sends.1
  3.3 3.0 %collective-permute-start.2 = (f32[48,512]{1,0:T(8,128)S(1)}, f32[48,512]{1,0:T(8,128)S(1)}, u32[]{:S(2)}, u32[]{:S(2)}) collective-permute-start(f32[48,512]{1,0:T(8,128)S(1)} %get-tuple-element.51), channel_id=1, source_target_pairs={{0,1},{1,0},{2,3},{3,2},{4,5},{5,4},{6,7},{7,6},{8,9},{9,8},{10,11... | collective-permute-start | bytes 294920 | tf_op jit(solution)/shard_map/ppermute | solution.py:264
  6.3 3.6 %collective-permute-start.3 = (f32[48,512]{1,0:T(8,128)S(1)}, f32[48,512]{1,0:T(8,128)S(1)}, u32[]{:S(2)}, u32[]{:S(2)}) collective-permute-start(f32[48,512]{1,0:T(8,128)S(1)} %get-tuple-element.52), channel_id=1, source_target_pairs={{0,7},{1,2},{2,1},{3,4},{4,3},{5,6},{6,5},{7,0},{8,15},{9,10},{10,... | collective-permute-start | bytes 294920 | tf_op jit(solution)/shard_map/ppermute | solution.py:263
  9.9 1.9 %collective-permute-start.1 = (f32[48,512]{1,0:T(8,128)S(1)}, f32[48,512]{1,0:T(8,128)S(1)}, u32[]{:S(2)}, u32[]{:S(2)}) collective-permute-start(f32[48,512]{1,0:T(8,128)S(1)} %get-tuple-element.50), channel_id=1, source_target_pairs={{0,7},{1,2},{2,1},{3,4},{4,3},{5,6},{6,5},{7,0},{8,15},{9,10},{10,... | collective-permute-start | bytes 294920 | tf_op jit(solution)/shard_map/ppermute | solution.py:263
  11.8 0.8 copy.18.ids_ref
  13.4 1.6 %copy-done = f32[8,256,256]{2,1,0:T(8,128)S(1)} copy-done((f32[8,256,256]{2,1,0:T(8,128)S(1)}, f32[8,256,256]{2,1,0:T(8,128)}, u32[]{:S(2)}) %copy-start) | copy-done | bytes 2097176
  15.0 1.9 %tables.1 = (bf16[1024,512]{1,0:T(8,128)(2,1)S(1)}, bf16[2048,256]{1,0:T(8,128)(2,1)S(1)}, bf16[2048,256]{1,0:T(8,128)(2,1)S(1)}) custom-call(s32[3]{0:T(128)S(1)} %pad_add_fusion.parity_ref.index_ref, s32[128,4]{1,0:T(8,128)S(1)} %copy.17.cols_ref, s32[128,4]{1,0:T(8,128)S(1)} %copy.18.ids_ref, f32[8,256,256]{2,1,0:T(8,128)S(1)} %copy-done), custom_call_target="tpu_custom_call" | custom-call | flops 10000000 | bytes 8000000 | tf_op jit(solution)/shard_map/tables/pallas_call | solution.py:269
  16.9 1.0 %copy-done.1 = f32[4,128,256]{2,1,0:T(8,128)S(1)} copy-done((f32[4,128,256]{2,1,0:T(8,128)S(1)}, f32[4,128,256]{2,1,0:T(8,128)}, u32[]{:S(2)}) %copy-start.1) | copy-done | bytes 524312
  17.9 1.0 %copy-done.5 = f32[4,128,256]{2,1,0:T(8,128)S(1)} copy-done((f32[4,128,256]{2,1,0:T(8,128)S(1)}, f32[4,128,256]{2,1,0:T(8,128)}, u32[]{:S(2)}) %copy-start.5) | copy-done | bytes 524312
  19.0 0.9 %copy-done.7 = f32[3,128,128]{2,1,0:T(8,128)S(1)} copy-done((f32[3,128,128]{2,1,0:T(8,128)S(1)}, f32[3,128,128]{2,1,0:T(8,128)}, u32[]{:S(2)}) %copy-start.7) | copy-done | bytes 196632
  19.9 1.0 %copy-done.11 = f32[4,128,256]{2,1,0:T(8,128)S(1)} copy-done((f32[4,128,256]{2,1,0:T(8,128)S(1)}, f32[4,128,256]{2,1,0:T(8,128)}, u32[]{:S(2)}) %copy-start.11) | copy-done | bytes 524312
  21.0 3.2 %step0_0.1 = (f32[2,128,256]{2,1,0:T(8,128)S(1)}, f32[48,512]{1,0:T(8,128)S(1)}, f32[48,512]{1,0:T(8,128)S(1)}, f32[128,256]{1,0:T(8,128)S(1)}) custom-call(s32[3]{0:T(128)S(1)} %pad_add_fusion.parity_ref.index_ref, bf16[1024,512]{1,0:T(8,128)(2,1)S(1)} %get-tuple-element.45.mix_ref, bf16[2048,256]{1,0:T(8,128)(2,1)S(1)} %get-tuple-element.46.high_ref, ...), custom_call_target="tpu_custom_call" | custom-call | flops 1500000000 | bytes 5000000 | tf_op jit(solution)/shard_map/step0_0/pallas_call | solution.py:342
  24.8 2.3 %collective-permute-start.7 = (f32[48,512]{1,0:T(8,128)S(1)}, f32[48,512]{1,0:T(8,128)S(1)}, u32[]{:S(2)}, u32[]{:S(2)}) collective-permute-start(f32[48,512]{1,0:T(8,128)S(1)} %get-tuple-element.59), channel_id=1, source_target_pairs={{0,7},{1,2},{2,1},{3,4},{4,3},{5,6},{6,5},{7,0},{8,15},{9,10},{10,... | collective-permute-start | bytes 294920 | tf_op jit(solution)/shard_map/ppermute | solution.py:263
  27.1 3.2 %step0_1.1 = (f32[2,128,256]{2,1,0:T(8,128)S(1)}, f32[48,512]{1,0:T(8,128)S(1)}, f32[48,512]{1,0:T(8,128)S(1)}, f32[128,256]{1,0:T(8,128)S(1)}) custom-call(s32[3]{0:T(128)S(1)} %pad_add_fusion.parity_ref.index_ref, bf16[1024,512]{1,0:T(8,128)(2,1)S(1)} %get-tuple-element.45.mix_ref, bf16[2048,256]{1,0:T(8,128)(2,1)S(1)} %get-tuple-element.46.high_ref, ...), custom_call_target="tpu_custom_call" | custom-call | flops 1500000000 | bytes 5000000 | tf_op jit(solution)/shard_map/step0_1/pallas_call | solution.py:342
  30.3 0.8 collective-permute-start.4
  31.1 1.8 %collective-permute-start.5 = (f32[48,512]{1,0:T(8,128)S(1)}, f32[48,512]{1,0:T(8,128)S(1)}, u32[]{:S(2)}, u32[]{:S(2)}) collective-permute-start(f32[48,512]{1,0:T(8,128)S(1)} %get-tuple-element.56), channel_id=1, source_target_pairs={{0,7},{1,2},{2,1},{3,4},{4,3},{5,6},{6,5},{7,0},{8,15},{9,10},{10,... | collective-permute-start | bytes 294920 | tf_op jit(solution)/shard_map/ppermute | solution.py:263
  32.9 3.2 %step1_0.1 = (f32[2,128,256]{2,1,0:T(8,128)S(1)}, f32[48,512]{1,0:T(8,128)S(1)}, f32[48,512]{1,0:T(8,128)S(1)}, f32[128,256]{1,0:T(8,128)S(1)}) custom-call(s32[3]{0:T(128)S(1)} %pad_add_fusion.parity_ref.index_ref, bf16[1024,512]{1,0:T(8,128)(2,1)S(1)} %get-tuple-element.45.mix_ref, bf16[2048,256]{1,0:T(8,128)(2,1)S(1)} %get-tuple-element.46.high_ref, ...), custom_call_target="tpu_custom_call" | custom-call | flops 1500000000 | bytes 5000000 | tf_op jit(solution)/shard_map/step1_0/pallas_call | solution.py:342
  36.2 3.5 %collective-permute-start.11 = (f32[48,512]{1,0:T(8,128)S(1)}, f32[48,512]{1,0:T(8,128)S(1)}, u32[]{:S(2)}, u32[]{:S(2)}) collective-permute-start(f32[48,512]{1,0:T(8,128)S(1)} %get-tuple-element.66), channel_id=1, source_target_pairs={{0,7},{1,2},{2,1},{3,4},{4,3},{5,6},{6,5},{7,0},{8,15},{9,10},{10,... | collective-permute-start | bytes 294920 | tf_op jit(solution)/shard_map/ppermute | solution.py:263
  39.7 3.2 %step1_1.1 = (f32[2,128,256]{2,1,0:T(8,128)S(1)}, f32[48,512]{1,0:T(8,128)S(1)}, f32[48,512]{1,0:T(8,128)S(1)}, f32[128,256]{1,0:T(8,128)S(1)}) custom-call(s32[3]{0:T(128)S(1)} %pad_add_fusion.parity_ref.index_ref, bf16[1024,512]{1,0:T(8,128)(2,1)S(1)} %get-tuple-element.45.mix_ref, bf16[2048,256]{1,0:T(8,128)(2,1)S(1)} %get-tuple-element.46.high_ref, ...), custom_call_target="tpu_custom_call" | custom-call | flops 1500000000 | bytes 5000000 | tf_op jit(solution)/shard_map/step1_1/pallas_call | solution.py:342
  43.0 1.9 %collective-permute-start.9 = (f32[48,512]{1,0:T(8,128)S(1)}, f32[48,512]{1,0:T(8,128)S(1)}, u32[]{:S(2)}, u32[]{:S(2)}) collective-permute-start(f32[48,512]{1,0:T(8,128)S(1)} %get-tuple-element.63), channel_id=1, source_target_pairs={{0,7},{1,2},{2,1},{3,4},{4,3},{5,6},{6,5},{7,0},{8,15},{9,10},{10,... | collective-permute-start | bytes 294920 | tf_op jit(solution)/shard_map/ppermute | solution.py:263
  44.9 3.7 %step2_0.1 = (f32[4,128,256]{2,1,0:T(8,128)}, f32[48,512]{1,0:T(8,128)S(1)}, f32[48,512]{1,0:T(8,128)S(1)}, f32[128,256]{1,0:T(8,128)S(1)}) custom-call(s32[3]{0:T(128)S(1)} %pad_add_fusion.parity_ref.index_ref, bf16[1024,512]{1,0:T(8,128)(2,1)S(1)} %get-tuple-element.45.mix_ref, bf16[2048,256]{1,0:T(8,128)(2,1)S(1)} %get-tuple-element.46.high_ref, ...), custom_call_target="tpu_custom_call" | custom-call | flops 1500000000 | bytes 5000000 | tf_op jit(solution)/shard_map/step2_0/pallas_call | solution.py:342
  49.2 2.3 %collective-permute-start.15 = (f32[48,512]{1,0:T(8,128)S(1)}, f32[48,512]{1,0:T(8,128)S(1)}, u32[]{:S(2)}, u32[]{:S(2)}) collective-permute-start(f32[48,512]{1,0:T(8,128)S(1)} %get-tuple-element.73), channel_id=1, source_target_pairs={{0,7},{1,2},{2,1},{3,4},{4,3},{5,6},{6,5},{7,0},{8,15},{9,10},{10,... | collective-permute-start | bytes 294920 | tf_op jit(solution)/shard_map/ppermute | solution.py:263
  51.5 3.9 %step2_1.1 = (f32[4,128,256]{2,1,0:T(8,128)}, f32[48,512]{1,0:T(8,128)S(1)}, f32[48,512]{1,0:T(8,128)S(1)}, f32[128,256]{1,0:T(8,128)S(1)}) custom-call(s32[3]{0:T(128)S(1)} %pad_add_fusion.parity_ref.index_ref, bf16[1024,512]{1,0:T(8,128)(2,1)S(1)} %get-tuple-element.45.mix_ref, ...), custom_call_target="tpu_custom_call", output_to_operand_aliasing={{0}: (12, {})} | custom-call | flops 1500000000 | bytes 5000000 | tf_op jit(solution)/shard_map/step2_1/pallas_call | solution.py:342
  56.2 1.8 %collective-permute-start.13 = (f32[48,512]{1,0:T(8,128)S(1)}, f32[48,512]{1,0:T(8,128)S(1)}, u32[]{:S(2)}, u32[]{:S(2)}) collective-permute-start(f32[48,512]{1,0:T(8,128)S(1)} %get-tuple-element.71), channel_id=1, source_target_pairs={{0,7},{1,2},{2,1},{3,4},{4,3},{5,6},{6,5},{7,0},{8,15},{9,10},{10,... | collective-permute-start | bytes 294920 | tf_op jit(solution)/shard_map/ppermute | solution.py:263
  57.9 1.0 %copy-done.3 = f32[4,128,256]{2,1,0:T(8,128)S(1)} copy-done((f32[4,128,256]{2,1,0:T(8,128)S(1)}, f32[4,128,256]{2,1,0:T(8,128)}, u32[]{:S(2)}) %copy-start.3) | copy-done | bytes 524312
  59.0 3.7 %step3_0.1 = (f32[4,128,256]{2,1,0:T(8,128)}, f32[128,256]{1,0:T(8,128)S(1)}) custom-call(s32[3]{0:T(128)S(1)} %pad_add_fusion.parity_ref.index_ref, bf16[1024,512]{1,0:T(8,128)(2,1)S(1)} %get-tuple-element.45.mix_ref, bf16[2048,256]{1,0:T(8,128)(2,1)S(1)} %get-tuple-element.46.high_ref, bf16[2048,256]{1,0:T(8,128)(2,1)S(1)} %get-tuple-element.47.low_ref, ...), custom_call_target="tpu_custom_call" | custom-call | flops 1500000000 | bytes 5000000 | tf_op jit(solution)/shard_map/step3_0/pallas_call | solution.py:342
  63.5 3.8 %step3_1.1 = (f32[4,128,256]{2,1,0:T(8,128)}, f32[128,256]{1,0:T(8,128)}, f32[4,2,32,256]{3,2,1,0:T(8,128)S(1)}, f32[4,2,32,256]{3,2,1,0:T(8,128)S(1)}) custom-call(s32[3]{0:T(128)S(1)} %pad_add_fusion.parity_ref.index_ref, bf16[1024,512]{1,0:T(8,128)(2,1)S(1)} %get-tuple-element.45.mix_ref, ...), custom_call_target="tpu_custom_call", output_to_operand_aliasing={{0}: (15, {})} | custom-call | flops 1500000000 | bytes 5000000 | tf_op jit(solution)/shard_map/step3_1/pallas_call | solution.py:342
  67.3 1.5 %collective-permute-done.16.got_ref = f32[4,2,32,256]{3,2,1,0:T(8,128)S(1)} collective-permute-done((f32[4,2,32,256]{3,2,1,0:T(8,128)S(1)}, f32[4,2,32,256]{3,2,1,0:T(8,128)S(1)}, u32[]{:S(2)}, u32[]{:S(2)}) %collective-permute-start.16) | collective-permute-done | bytes 262176 | tf_op jit(solution)/shard_map/ppermute | solution.py:374
  69.4 1.6 %collective-permute-start.17 = (f32[4,32,256]{2,1,0:T(8,128)S(1)}, f32[4,32,256]{2,1,0:T(8,128)S(1)}, u32[]{:S(2)}, u32[]{:S(2)}) collective-permute-start(f32[4,32,256]{2,1,0:T(8,128)S(1)} %get-tuple-element.83), channel_id=1, source_target_pairs={{0,16},{8,24},{16,0},{24,8},{1,17},{9,25},{17,1},{25,9},{2,18},{10... | collective-permute-start | bytes 393224 | tf_op jit(solution)/shard_map/ppermute | solution.py:385
  71.0 4.0 %collective-permute-done.17.got_ref = f32[4,32,256]{2,1,0:T(8,128)S(1)} collective-permute-done((f32[4,32,256]{2,1,0:T(8,128)S(1)}, f32[4,32,256]{2,1,0:T(8,128)S(1)}, u32[]{:S(2)}, u32[]{:S(2)}) %collective-permute-start.17) | collective-permute-done | bytes 131104 | tf_op jit(solution)/shard_map/ppermute | solution.py:385
  75.0 9.9 %energy.1 = (f32[4,32,256]{2,1,0:T(8,128)}, f32[512,32,256]{2,1,0:T(8,128)}) custom-call(bf16[512,256]{1,0:T(8,128)(2,1)S(1)} %copy-done.12, bf16[512,128]{1,0:T(8,128)(2,1)S(1)} %copy-done.13, f32[124,32,256]{2,1,0:T(8,128)S(1)} %copy-done.10, f32[4,32,256]{2,1,0:T(8,128)S(1)} %get-tuple-element.82.mine_ref, f32[4,32,256]{2,1,0:T(8,128)S(1)} %collective-permute-done.17.got_ref), custom_call_target="tpu_custom_call" | custom-call | flops 4000000000 | bytes 22000000 | tf_op jit(solution)/shard_map/energy/pallas_call | solution.py:392
  (47 shorter events, 5.1 us)
Async XLA Ops:
  0.7 1.0 %copy-start.4 = (f32[4,128,256]{2,1,0:T(8,128)S(1)}, f32[4,128,256]{2,1,0:T(8,128)}, u32[]{:S(2)}) copy-start(f32[4,128,256]{2,1,0:T(8,128)} %prev_ref.7) | copy-start | bytes 1572868
  1.8 0.7 copy-start.9
  2.5 24.7 %copy-start.6 = (f32[4,128,256]{2,1,0:T(8,128)S(1)}, f32[4,128,256]{2,1,0:T(8,128)}, u32[]{:S(2)}) copy-start(f32[4,128,256]{2,1,0:T(8,128)} %prev_ref.7) | copy-start | bytes 1572868
  3.3 13.6 %collective-permute-start.2 = (f32[48,512]{1,0:T(8,128)S(1)}, f32[48,512]{1,0:T(8,128)S(1)}, u32[]{:S(2)}, u32[]{:S(2)}) collective-permute-start(f32[48,512]{1,0:T(8,128)S(1)} %get-tuple-element.51), channel_id=1, source_target_pairs={{0,1},{1,0},{2,3},{3,2},{4,5},{5,4},{6,7},{7,6},{8,9},{9,8},{10,11... | collective-permute-start | bytes 294920 | tf_op jit(solution)/shard_map/ppermute | solution.py:264
  6.3 10.6 %collective-permute-start.3 = (f32[48,512]{1,0:T(8,128)S(1)}, f32[48,512]{1,0:T(8,128)S(1)}, u32[]{:S(2)}, u32[]{:S(2)}) collective-permute-start(f32[48,512]{1,0:T(8,128)S(1)} %get-tuple-element.52), channel_id=1, source_target_pairs={{0,7},{1,2},{2,1},{3,4},{4,3},{5,6},{6,5},{7,0},{8,15},{9,10},{10,... | collective-permute-start | bytes 294920 | tf_op jit(solution)/shard_map/ppermute | solution.py:263
  9.9 17.2 %collective-permute-start = (f32[48,512]{1,0:T(8,128)S(1)}, f32[48,512]{1,0:T(8,128)S(1)}, u32[]{:S(2)}, u32[]{:S(2)}) collective-permute-start(f32[48,512]{1,0:T(8,128)S(1)} %get-tuple-element.49), channel_id=1, source_target_pairs={{0,1},{1,0},{2,3},{3,2},{4,5},{5,4},{6,7},{7,6},{8,9},{9,8},{10,11... | collective-permute-start | bytes 294920 | tf_op jit(solution)/shard_map/ppermute | solution.py:264
  9.9 17.2 %collective-permute-start.1 = (f32[48,512]{1,0:T(8,128)S(1)}, f32[48,512]{1,0:T(8,128)S(1)}, u32[]{:S(2)}, u32[]{:S(2)}) collective-permute-start(f32[48,512]{1,0:T(8,128)S(1)} %get-tuple-element.50), channel_id=1, source_target_pairs={{0,7},{1,2},{2,1},{3,4},{4,3},{5,6},{6,5},{7,0},{8,15},{9,10},{10,... | collective-permute-start | bytes 294920 | tf_op jit(solution)/shard_map/ppermute | solution.py:263
  13.4 1.6 %copy-start = (f32[8,256,256]{2,1,0:T(8,128)S(1)}, f32[8,256,256]{2,1,0:T(8,128)}, u32[]{:S(2)}) copy-start(f32[8,256,256]{2,1,0:T(8,128)} %kinds_ref.1) | copy-start | bytes 6291460
  16.9 1.0 %copy-start.1 = (f32[4,128,256]{2,1,0:T(8,128)S(1)}, f32[4,128,256]{2,1,0:T(8,128)}, u32[]{:S(2)}) copy-start(f32[4,128,256]{2,1,0:T(8,128)} %probe_ref.15) | copy-start | bytes 1572868
  17.9 1.0 %copy-start.5 = (f32[4,128,256]{2,1,0:T(8,128)S(1)}, f32[4,128,256]{2,1,0:T(8,128)}, u32[]{:S(2)}) copy-start(f32[4,128,256]{2,1,0:T(8,128)} %prev_ref.7) | copy-start | bytes 1572868
  19.0 0.9 %copy-start.7 = (f32[3,128,128]{2,1,0:T(8,128)S(1)}, f32[3,128,128]{2,1,0:T(8,128)}, u32[]{:S(2)}) copy-start(f32[3,128,128]{2,1,0:T(8,128)} %site_ref.15) | copy-start | bytes 589828
  19.9 1.0 %copy-start.11 = (f32[4,128,256]{2,1,0:T(8,128)S(1)}, f32[4,128,256]{2,1,0:T(8,128)}, u32[]{:S(2)}) copy-start(f32[4,128,256]{2,1,0:T(8,128)} %prev_ref.5) | copy-start | bytes 1572868
  24.1 8.8 %copy-start.2 = (f32[4,128,256]{2,1,0:T(8,128)S(1)}, f32[4,128,256]{2,1,0:T(8,128)}, u32[]{:S(2)}) copy-start(f32[4,128,256]{2,1,0:T(8,128)} %probe_ref.15) | copy-start | bytes 1572868
  24.2 8.7 %collective-permute-start.6 = (f32[48,512]{1,0:T(8,128)S(1)}, f32[48,512]{1,0:T(8,128)S(1)}, u32[]{:S(2)}, u32[]{:S(2)}) collective-permute-start(f32[48,512]{1,0:T(8,128)S(1)} %get-tuple-element.58), channel_id=1, source_target_pairs={{0,1},{1,0},{2,3},{3,2},{4,5},{5,4},{6,7},{7,6},{8,9},{9,8},{10,11... | collective-permute-start | bytes 294920 | tf_op jit(solution)/shard_map/ppermute | solution.py:264
  24.8 8.1 %collective-permute-start.7 = (f32[48,512]{1,0:T(8,128)S(1)}, f32[48,512]{1,0:T(8,128)S(1)}, u32[]{:S(2)}, u32[]{:S(2)}) collective-permute-start(f32[48,512]{1,0:T(8,128)S(1)} %get-tuple-element.59), channel_id=1, source_target_pairs={{0,7},{1,2},{2,1},{3,4},{4,3},{5,6},{6,5},{7,0},{8,15},{9,10},{10,... | collective-permute-start | bytes 294920 | tf_op jit(solution)/shard_map/ppermute | solution.py:263
  30.3 9.3 %collective-permute-start.4 = (f32[48,512]{1,0:T(8,128)S(1)}, f32[48,512]{1,0:T(8,128)S(1)}, u32[]{:S(2)}, u32[]{:S(2)}) collective-permute-start(f32[48,512]{1,0:T(8,128)S(1)} %get-tuple-element.55), channel_id=1, source_target_pairs={{0,1},{1,0},{2,3},{3,2},{4,5},{5,4},{6,7},{7,6},{8,9},{9,8},{10,11... | collective-permute-start | bytes 294920 | tf_op jit(solution)/shard_map/ppermute | solution.py:264
  31.1 8.5 %collective-permute-start.5 = (f32[48,512]{1,0:T(8,128)S(1)}, f32[48,512]{1,0:T(8,128)S(1)}, u32[]{:S(2)}, u32[]{:S(2)}) collective-permute-start(f32[48,512]{1,0:T(8,128)S(1)} %get-tuple-element.56), channel_id=1, source_target_pairs={{0,7},{1,2},{2,1},{3,4},{4,3},{5,6},{6,5},{7,0},{8,15},{9,10},{10,... | collective-permute-start | bytes 294920 | tf_op jit(solution)/shard_map/ppermute | solution.py:263
  36.1 8.7 %collective-permute-start.10 = (f32[48,512]{1,0:T(8,128)S(1)}, f32[48,512]{1,0:T(8,128)S(1)}, u32[]{:S(2)}, u32[]{:S(2)}) collective-permute-start(f32[48,512]{1,0:T(8,128)S(1)} %get-tuple-element.65), channel_id=1, source_target_pairs={{0,1},{1,0},{2,3},{3,2},{4,5},{5,4},{6,7},{7,6},{8,9},{9,8},{10,11... | collective-permute-start | bytes 294920 | tf_op jit(solution)/shard_map/ppermute | solution.py:264
  36.2 8.7 %collective-permute-start.11 = (f32[48,512]{1,0:T(8,128)S(1)}, f32[48,512]{1,0:T(8,128)S(1)}, u32[]{:S(2)}, u32[]{:S(2)}) collective-permute-start(f32[48,512]{1,0:T(8,128)S(1)} %get-tuple-element.66), channel_id=1, source_target_pairs={{0,7},{1,2},{2,1},{3,4},{4,3},{5,6},{6,5},{7,0},{8,15},{9,10},{10,... | collective-permute-start | bytes 294920 | tf_op jit(solution)/shard_map/ppermute | solution.py:263
  42.9 8.6 %collective-permute-start.8 = (f32[48,512]{1,0:T(8,128)S(1)}, f32[48,512]{1,0:T(8,128)S(1)}, u32[]{:S(2)}, u32[]{:S(2)}) collective-permute-start(f32[48,512]{1,0:T(8,128)S(1)} %get-tuple-element.62), channel_id=1, source_target_pairs={{0,1},{1,0},{2,3},{3,2},{4,5},{5,4},{6,7},{7,6},{8,9},{9,8},{10,11... | collective-permute-start | bytes 294920 | tf_op jit(solution)/shard_map/ppermute | solution.py:264
  43.0 8.6 %collective-permute-start.9 = (f32[48,512]{1,0:T(8,128)S(1)}, f32[48,512]{1,0:T(8,128)S(1)}, u32[]{:S(2)}, u32[]{:S(2)}) collective-permute-start(f32[48,512]{1,0:T(8,128)S(1)} %get-tuple-element.63), channel_id=1, source_target_pairs={{0,7},{1,2},{2,1},{3,4},{4,3},{5,6},{6,5},{7,0},{8,15},{9,10},{10,... | collective-permute-start | bytes 294920 | tf_op jit(solution)/shard_map/ppermute | solution.py:263
  48.6 9.3 %copy-start.8 = (f32[3,128,128]{2,1,0:T(8,128)S(1)}, f32[3,128,128]{2,1,0:T(8,128)}, u32[]{:S(2)}) copy-start(f32[3,128,128]{2,1,0:T(8,128)} %site_ref.15) | copy-start | bytes 589828
  48.6 9.3 %collective-permute-start.14 = (f32[48,512]{1,0:T(8,128)S(1)}, f32[48,512]{1,0:T(8,128)S(1)}, u32[]{:S(2)}, u32[]{:S(2)}) collective-permute-start(f32[48,512]{1,0:T(8,128)S(1)} %get-tuple-element.72), channel_id=1, source_target_pairs={{0,1},{1,0},{2,3},{3,2},{4,5},{5,4},{6,7},{7,6},{8,9},{9,8},{10,11... | collective-permute-start | bytes 294920 | tf_op jit(solution)/shard_map/ppermute | solution.py:264
  49.2 8.7 %collective-permute-start.15 = (f32[48,512]{1,0:T(8,128)S(1)}, f32[48,512]{1,0:T(8,128)S(1)}, u32[]{:S(2)}, u32[]{:S(2)}) collective-permute-start(f32[48,512]{1,0:T(8,128)S(1)} %get-tuple-element.73), channel_id=1, source_target_pairs={{0,7},{1,2},{2,1},{3,4},{4,3},{5,6},{6,5},{7,0},{8,15},{9,10},{10,... | collective-permute-start | bytes 294920 | tf_op jit(solution)/shard_map/ppermute | solution.py:263
  55.4 7.3 %collective-permute-start.12 = (f32[48,512]{1,0:T(8,128)S(1)}, f32[48,512]{1,0:T(8,128)S(1)}, u32[]{:S(2)}, u32[]{:S(2)}) collective-permute-start(f32[48,512]{1,0:T(8,128)S(1)} %get-tuple-element.70), channel_id=1, source_target_pairs={{0,1},{1,0},{2,3},{3,2},{4,5},{5,4},{6,7},{7,6},{8,9},{9,8},{10,11... | collective-permute-start | bytes 294920 | tf_op jit(solution)/shard_map/ppermute | solution.py:264
  56.2 7.3 %collective-permute-start.13 = (f32[48,512]{1,0:T(8,128)S(1)}, f32[48,512]{1,0:T(8,128)S(1)}, u32[]{:S(2)}, u32[]{:S(2)}) collective-permute-start(f32[48,512]{1,0:T(8,128)S(1)} %get-tuple-element.71), channel_id=1, source_target_pairs={{0,7},{1,2},{2,1},{3,4},{4,3},{5,6},{6,5},{7,0},{8,15},{9,10},{10,... | collective-permute-start | bytes 294920 | tf_op jit(solution)/shard_map/ppermute | solution.py:263
  57.9 1.0 %copy-start.3 = (f32[4,128,256]{2,1,0:T(8,128)S(1)}, f32[4,128,256]{2,1,0:T(8,128)}, u32[]{:S(2)}) copy-start(f32[4,128,256]{2,1,0:T(8,128)} %get-tuple-element.41.cur_ref) | copy-start | bytes 1572868
  62.7 12.3 %copy-start.10 = (f32[124,32,256]{2,1,0:T(8,128)S(1)}, f32[124,32,256]{2,1,0:T(8,128)}, u32[]{:S(2)}) copy-start(f32[124,32,256]{2,1,0:T(8,128)} %prior_ref.1) | copy-start | bytes 12189700
  62.7 12.3 %copy-start.12 = (bf16[512,256]{1,0:T(8,128)(2,1)S(1)}, bf16[512,256]{1,0:T(8,128)(2,1)}, u32[]{:S(2)}) copy-start(bf16[512,256]{1,0:T(8,128)(2,1)} %constant.40.clone.both_ref) | copy-start | bytes 786436
  62.7 12.3 %copy-start.13 = (bf16[512,128]{1,0:T(8,128)(2,1)S(1)}, bf16[512,128]{1,0:T(8,128)(2,1)}, u32[]{:S(2)}) copy-start(bf16[512,128]{1,0:T(8,128)(2,1)} %constant.41.clone.high_ref) | copy-start | bytes 393220
  67.3 1.5 %collective-permute-start.16 = (f32[4,2,32,256]{3,2,1,0:T(8,128)S(1)}, f32[4,2,32,256]{3,2,1,0:T(8,128)S(1)}, u32[]{:S(2)}, u32[]{:S(2)}) collective-permute-start(f32[4,2,32,256]{3,2,1,0:T(8,128)S(1)} %get-tuple-element.81), channel_id=1, source_target_pairs={{0,8},{8,0},{16,24},{24,16},{1,9},{9,1},{17,25},{25,17},{2,10},{10... | collective-permute-start | bytes 786440 | tf_op jit(solution)/shard_map/ppermute | solution.py:374
  69.4 5.6 %collective-permute-start.17 = (f32[4,32,256]{2,1,0:T(8,128)S(1)}, f32[4,32,256]{2,1,0:T(8,128)S(1)}, u32[]{:S(2)}, u32[]{:S(2)}) collective-permute-start(f32[4,32,256]{2,1,0:T(8,128)S(1)} %get-tuple-element.83), channel_id=1, source_target_pairs={{0,16},{8,24},{16,0},{24,8},{1,17},{9,25},{17,1},{25,9},{2,18},{10... | collective-permute-start | bytes 393224 | tf_op jit(solution)/shard_map/ppermute | solution.py:385
where the time goes:
time: 85.3 us; the launch traced here: 84.9 us
  Pallas kernels  41.1 us (48%)
  starting transfers between devices  26.5 us (31%)
  local copies, waits for them, and re-layouts  9.99 us (12%)
  waiting for transfers between devices  6.35 us (7%)
    pallas_call x8, Pallas kernels, per_device(): pl.pallas_call(functools.partial(step_kernel, (c, last, partial is not No...  27.9 us
    ppermute x8, starting transfers between devices, exchange(): got_b = lax.ppermute(b, 'dom', swap_b)  19 us
    unnamed x30, local copies, waits for them, and re-layouts  9.99 us
    pallas_call x1, Pallas kernels, per_device(): pl.pallas_call(functools.partial(energy_kernel, vec_dev * groups), out_sh...  9.87 us
    ppermute x8, starting transfers between devices, exchange(): got_a = lax.ppermute(a, 'dom', swap_a)  5.98 us
    ppermute x1, waiting for transfers between devices, per_device(): got = lax.ppermute(give, 'vec', [(i, i ^ 2) for i in range(groups)])  4.02 us
    pallas_call x1, Pallas kernels, per_device(): pl.pallas_call(functools.partial(prep_kernel, rim), out_shape=[jax.ShapeD...  1.9 us
  transfers between devices with their start and end apart: 18, of which 3 were waited for; matrix products, arithmetic and copies ran while one was open for 2% of the time, Pallas kernels for 31%

commit v1 on v0

v1 whole, which is shorter than its diff:
```python
import functools
import math

import jax
import jax.numpy as jnp
import numpy as np
from jax import lax
from jax.experimental import pallas as pl
from jax.experimental.pallas import tpu as pltpu
from jax.sharding import PartitionSpec as P

ENERGIES = 512
STEPS = 4
F32 = jnp.float32
BF16 = jnp.bfloat16
VMEM_LIMIT = 24 * 1024 * 1024


def split(x):
    high = x.astype(BF16)
    return high, (x - high.astype(F32)).astype(BF16)


def dot(a, b):
    return jnp.dot(a, b, preferred_element_type=F32)


def jackson_split(moment_count, energy_count):
    m = np.arange(moment_count, dtype=np.float64)
    step = math.pi / (moment_count + 1.0)
    damping = (
        (moment_count - m + 1.0) * np.cos(step * m) + np.sin(step * m) / math.tan(step)
    ) / (moment_count + 1.0)
    weights = np.where(m == 0, damping, 2.0 * damping)
    angles = math.pi * (np.arange(energy_count // 2) + 0.5) / energy_count
    table = (weights[None, :] * np.cos(angles[:, None] * m[None, :])).astype(np.float32)
    halves = []
    for parity in range(2):
        part = table[:, parity::2]
        high = part.astype(BF16)
        low = (part - high.astype(np.float32)).astype(BF16)
        halves.append(np.concatenate([high, low, high, low], axis=1))
    return halves


def vmem():
    return pl.BlockSpec(memory_space=pltpu.VMEM)


def smem():
    return pl.BlockSpec(memory_space=pltpu.SMEM)


def params(limit=VMEM_LIMIT):
    return pltpu.CompilerParams(vmem_limit_bytes=limit)


def cost(flops, size):
    return pl.CostEstimate(flops=int(flops), bytes_accessed=int(size), transcendentals=0)


def gather_rows(onehot, value):
    high, low = split(value)
    return dot(onehot, jnp.concatenate([high, low], axis=0))


def any_space():
    return pl.BlockSpec(memory_space=pl.ANY)


def first_kernel(rim, vecs, index_ref, lists_hbm, cur_hbm, pick_ref, cur_ref, *rest):
    sends, (lists_ref, sems) = rest[:-2], rest[-2:]
    count, blocks, width = cur_ref.shape
    list_copy = pltpu.make_async_copy(lists_hbm, lists_ref, sems.at[count])
    list_copy.start()
    copies = [pltpu.make_async_copy(cur_hbm.at[v], cur_ref.at[v], sems.at[v]) for v in range(count)]
    for copy in copies:
        copy.start()
    list_copy.wait()
    lists = lists_ref[0]
    even = index_ref[0] == 0
    rows = lax.broadcasted_iota(jnp.int32, (rim, rim), 0)
    lanes = lax.broadcasted_iota(jnp.int32, (rim, rim), 1)
    slots = lax.broadcasted_iota(jnp.int32, (rim, blocks), 1)
    for half in range(2):
        mine = lists[half : half + 1]
        other = lists[1 - half : 2 - half]
        chosen = jnp.where(even, mine, other)
        spread = jnp.where(rows == lanes, chosen, 0).astype(F32)
        column = jnp.sum(spread, axis=1, keepdims=True).astype(jnp.int32)
        onehot = jnp.where(slots == column, 1.0, 0.0).astype(BF16)
        pick_ref[pl.ds(half * rim, rim), 0:blocks] = onehot
        pick_ref[pl.ds(half * rim, rim), blocks : 2 * blocks] = onehot
    pick = pick_ref[...]
    for v in range(count):
        chunk, place = divmod(v, vecs)
        copies[v].wait()
        got = gather_rows(pick, cur_ref[v])
        for half in range(2):
            sends[2 * chunk + half][:, place * width : (place + 1) * width] = got[
                half * rim : (half + 1) * rim
            ]


def prep_kernel(
    rim,
    index_ref,
    cols_ref,
    ids_ref,
    kinds_hbm,
    prev_hbm,
    probe_hbm,
    site_hbm,
    mix_ref,
    high_ref,
    low_ref,
    prev_ref,
    probe_ref,
    site_ref,
    kinds,
    sems,
):
    links, blocks = cols_ref.shape
    kind_count, width = kinds.shape[:2]
    padded = mix_ref.shape[1] // 2
    copies = [
        pltpu.make_async_copy(kinds_hbm.at[n], kinds.at[n], sems.at[n]) for n in range(kind_count)
    ]
    fetched = ((prev_hbm, prev_ref), (probe_hbm, probe_ref), (site_hbm, site_ref))
    for i, (source, target) in enumerate(fetched):
        copies.append(pltpu.make_async_copy(source, target, sems.at[kind_count + i]))
    for copy in copies:
        copy.start()
    even = index_ref[0] == 0
    rows = lax.broadcasted_iota(jnp.int32, (padded, blocks), 0)
    corner = lax.broadcasted_iota(jnp.int32, (blocks, blocks), 0)
    diagonal = corner == lax.broadcasted_iota(jnp.int32, (blocks, blocks), 1)
    identity = jnp.where(diagonal, 1.0, 0.0).astype(BF16)
    e = cols_ref[...]
    crossed = jnp.where(e < blocks + rim, e + rim, e - rim)
    e = jnp.where(jnp.logical_and(even, e >= blocks), crossed, e)
    ids = ids_ref[...]
    for n in range(kind_count):
        mine = jnp.where(ids == n, e, -1)
        total = jnp.zeros((padded, blocks), F32)
        for k in range(links):
            total += jnp.where(rows == mine[k : k + 1], 1.0, 0.0)
        turned = lax.dot_general(
            identity, total.astype(BF16), (((1,), (1,)), ((), ())), preferred_element_type=F32
        ).astype(BF16)
        mix_ref[n * blocks : (n + 1) * blocks, 0:padded] = turned
        mix_ref[n * blocks : (n + 1) * blocks, padded : 2 * padded] = turned
    for n in range(kind_count):
        copies[n].wait()
        high, low = split(2.0 * kinds[n])
        high_ref[n * width : (n + 1) * width] = high
        low_ref[n * width : (n + 1) * width] = low
    for copy in copies[kind_count:]:
        copy.wait()


def step_kernel(
    cfg,
    index_ref,
    mix_ref,
    high_ref,
    low_ref,
    pick_ref,
    site_ref,
    cur_ref,
    prev_ref,
    probe_ref,
    recv_a,
    recv_b,
    *rest,
):
    vecs, cur_at, prev_at, own_at, last, add_partial, older, aliased = cfg
    rest = list(rest)
    partial_in = rest.pop(0) if add_partial else None
    olders = [rest.pop(0) for _ in range(older)]
    rest = rest[aliased:]
    if last:
        prev_out, out_hbm, partial_out = rest.pop(0), rest.pop(0), rest.pop(0)
        keep_ref = rest.pop(0) if older else None
        give_ref = rest.pop(0) if older else None
        source, mixed, out_ref, sems = rest
    else:
        out_ref, send_a, send_b, partial_out = rest[:4]
        source, mixed = rest[4:]
    blocks, width = cur_ref.shape[1:]
    rim = recv_a.shape[0]
    padded = source.shape[1] // 2
    kind_count = mix_ref.shape[0] // blocks
    spin = width // 2
    copies = []
    if last:
        copies.append(
            pltpu.make_async_copy(
                cur_ref.at[pl.ds(cur_at, vecs)], prev_out.at[pl.ds(own_at, vecs)], sems.at[vecs]
            )
        )
        copies[0].start()
    for v in range(vecs):
        columns = slice(v * width, (v + 1) * width)
        pieces = [cur_ref[cur_at + v], recv_a[:, columns], recv_b[:, columns]]
        used = blocks + 2 * rim
        if used < padded:
            pieces.append(jnp.zeros((padded - used, width), F32))
        high, low = split(jnp.concatenate(pieces, axis=0))
        source[v, 0:padded] = high
        source[v, padded : 2 * padded] = low
    for v in range(vecs):
        mixture = dot(mix_ref[...], source[v])
        high, low = split(mixture)
        for n in range(kind_count):
            columns = slice(n * width, (n + 1) * width)
            rows = slice(n * blocks, (n + 1) * blocks)
            mixed[v * blocks : (v + 1) * blocks, columns] = high[rows]
            mixed[(vecs + v) * blocks : (vecs + v + 1) * blocks, columns] = low[rows]
    count = vecs * blocks
    both = dot(mixed[...], high_ref[...])
    hopping = both[:count] + both[count:] + dot(mixed[:count], low_ref[...])
    diag_up = 2.0 * (site_ref[0] + site_ref[1])
    diag_down = 2.0 * (site_ref[0] - site_ref[1])
    cross = 2.0 * site_ref[2]
    partial = partial_in[...] if add_partial else None
    for v in range(vecs):
        here = cur_ref[cur_at + v]
        up = here[:, :spin]
        down = here[:, spin:]
        onsite = jnp.concatenate(
            [diag_up * up + cross * down, diag_down * down + cross * up], axis=1
        )
        following = hopping[v * blocks : (v + 1) * blocks] + onsite - prev_ref[prev_at + v]
        out_ref[v] = following
        if last:
            copies.append(pltpu.make_async_copy(out_ref.at[v], out_hbm.at[own_at + v], sems.at[v]))
            copies[-1].start()
        term = probe_ref[own_at + v] * following
        partial = term if partial is None else partial + term
        if not last:
            got = gather_rows(pick_ref[...], following)
            send_a[:, v * width : (v + 1) * width] = got[:rim]
            send_b[:, v * width : (v + 1) * width] = got[rim:]
    partial_out[...] = partial
    if last and older:
        cores = 2
        quarter = keep_ref.shape[2]
        core = index_ref[1]
        for s in range(older + 1):
            ref = olders[s] if s < older else partial_out
            for y in range(keep_ref.shape[1]):
                base = y * cores * quarter
                keep_ref[s, y] = ref[pl.ds(pl.multiple_of(base + core * quarter, quarter), quarter)]
                give_ref[s, y] = ref[
                    pl.ds(pl.multiple_of(base + (1 - core) * quarter, quarter), quarter)
                ]
    for copy in copies:
        copy.wait()


def fold_kernel(index_ref, keep_ref, got_ref, mine_ref, give_ref):
    y = index_ref[2]
    mine_ref[...] = keep_ref[:, y] + got_ref[:, y]
    give_ref[...] = keep_ref[:, 1 - y] + got_ref[:, 1 - y]


def energy_kernel(vector_total, even_ref, odd_ref, prior_ref, mine_ref, got_ref, new_ref, map_ref, moments):
    prior_count, group, lanes = prior_ref.shape
    steps = mine_ref.shape[0]
    half = even_ref.shape[0]
    pairs = (prior_count + steps) // 2
    new = (mine_ref[...] + got_ref[...]) * (1.0 / vector_total)
    new_ref[...] = new
    moments[0 : prior_count * group] = prior_ref[...].reshape(prior_count * group, lanes)
    moments[prior_count * group :] = new.reshape(steps * group, lanes)
    flat = map_ref.reshape(2 * half * group, lanes)
    flip = 7 - lax.broadcasted_iota(jnp.int32, (8, lanes), 0)
    for b in range(0, group, 2):
        sums = []
        for parity, table in ((0, even_ref), (1, odd_ref)):
            pair = [
                moments[pl.ds(parity * group + b + i, pairs, stride=2 * group)] for i in range(2)
            ]
            high, low = split(jnp.concatenate(pair, axis=1))
            sums.append(dot(table[...], jnp.concatenate([high, high, low, low], axis=0)))
        plus = sums[0] + sums[1]
        minus = sums[0] - sums[1]
        for i in range(2):
            columns = slice(i * lanes, (i + 1) * lanes)
            flat[pl.ds(b + i, half, stride=group)] = plus[:, columns]
            for r in range(0, half, 8):
                turned = jnp.take_along_axis(minus[r : r + 8, columns], flip, axis=0)
                top = 2 * half - 8 - r
                flat[pl.ds(top * group + b + i, 8, stride=group)] = turned


def per_device(
    probe,
    cheb_prev,
    cheb_cur,
    prior_moments,
    site_terms,
    hop_kinds,
    tile_kind_ids,
    send_lists,
    tile_cols,
):
    vec_dev, blocks, width = cheb_cur.shape
    kind_count = hop_kinds.shape[0]
    groups = lax.axis_size("vec")
    domains = lax.axis_size("dom")
    rim = send_lists.shape[2]
    chunks = 2
    vecs = vec_dev // chunks
    quarter = blocks // groups
    padded = -(-(blocks + 2 * rim) // 256) * 256
    swap_a = [(i, i ^ 1) for i in range(domains)]
    swap_b = [(i, (i + 1) % domains if i % 2 else (i - 1) % domains) for i in range(domains)]
    vec_index = lax.axis_index("vec")
    index = jnp.stack([lax.axis_index("dom") % 2, vec_index % 2, vec_index // 2]).astype(jnp.int32)

    rows = jax.ShapeDtypeStruct((rim, vecs * width), F32)
    full_shape = jax.ShapeDtypeStruct((vec_dev, blocks, width), F32)
    chunk_shape = jax.ShapeDtypeStruct((vecs, blocks, width), F32)
    first = pl.pallas_call(
        functools.partial(first_kernel, rim, vecs),
        out_shape=[jax.ShapeDtypeStruct((2 * rim, 2 * blocks), BF16), full_shape]
        + [rows] * (2 * chunks),
        in_specs=[smem(), any_space(), any_space()],
        out_specs=[vmem()] * (2 + 2 * chunks),
        scratch_shapes=[
            pltpu.VMEM(send_lists.shape, jnp.int32),
            pltpu.SemaphoreType.DMA((vec_dev + 1,)),
        ],
        compiler_params=params(),
        cost_estimate=cost(1e8, 1e6),
        name="first_sends",
    )(index, send_lists, cheb_cur)
    pick, cur_held, sends = first[0], first[1], list(first[2:])

    def exchange(a, b):
        got_b = lax.ppermute(b, "dom", swap_b)
        got_a = lax.ppermute(a, "dom", swap_a)
        return got_a, got_b

    received = [exchange(sends[2 * c], sends[2 * c + 1]) for c in range(chunks)]

    mix, high, low, prev_held, probe_held, site_held = pl.pallas_call(
        functools.partial(prep_kernel, rim),
        out_shape=[
            jax.ShapeDtypeStruct((kind_count * blocks, 2 * padded), BF16),
            jax.ShapeDtypeStruct((kind_count * width, width), BF16),
            jax.ShapeDtypeStruct((kind_count * width, width), BF16),
            full_shape,
            full_shape,
            jax.ShapeDtypeStruct(site_terms.shape, F32),
        ],
        in_specs=[smem(), vmem(), vmem()] + [any_space()] * 4,
        out_specs=[vmem()] * 6,
        scratch_shapes=[
            pltpu.VMEM(hop_kinds.shape, F32),
            pltpu.SemaphoreType.DMA((kind_count + 3,)),
        ],
        compiler_params=params(),
        cost_estimate=cost(1e7, 8e6),
        name="tables",
    )(index, tile_cols.T, tile_kind_ids.T, hop_kinds, cheb_prev, probe, site_terms)

    partial_shape = jax.ShapeDtypeStruct((blocks, width), F32)
    current = [(cur_held, c * vecs) for c in range(chunks)]
    previous = [(prev_held, c * vecs) for c in range(chunks)]
    partials = []
    buffers = []
    for s in range(STEPS):
        last = s == STEPS - 1
        partial = None
        for c in range(chunks):
            args = [index, mix, high, low, pick, site_held]
            args += [current[c][0], previous[c][0], probe_held, *received[c]]
            specs = [smem()] + [vmem()] * (len(args) - 1)
            older = len(partials) if last and c == chunks - 1 else 0
            extra = ([] if partial is None else [partial]) + (partials if older else [])
            args += extra
            specs += [vmem()] * len(extra)
            aliases = {len(args) + i: i for i in range(len(buffers))}
            args += buffers
            specs += [any_space()] * len(buffers)
            scratch = [
                pltpu.VMEM((vecs, 2 * padded, width), BF16),
                pltpu.VMEM((2 * vecs * blocks, kind_count * width), BF16),
            ]
            if last:
                outs, out_specs = [full_shape, full_shape], [any_space(), any_space()]
                scratch += [
                    pltpu.VMEM((vecs, blocks, width), F32),
                    pltpu.SemaphoreType.DMA((vecs + 1,)),
                ]
            else:
                outs, out_specs = [chunk_shape, rows, rows], [vmem()] * 3
            outs.append(partial_shape)
            if older:
                outs += [jax.ShapeDtypeStruct((older + 1, groups // 2, quarter, width), F32)] * 2
            out_specs += [vmem()] * (len(outs) - len(out_specs))
            cfg = (
                vecs,
                current[c][1],
                previous[c][1],
                c * vecs,
                last,
                partial is not None,
                older,
                len(buffers),
            )
            result = pl.pallas_call(
                functools.partial(step_kernel, cfg),
                out_shape=outs,
                in_specs=specs,
                out_specs=out_specs,
                scratch_shapes=scratch,
                input_output_aliases=aliases,
                compiler_params=params(),
                cost_estimate=cost(1.5e9, 5e6),
                name=f"step{s}_{c}",
            )(*args)
            if last:
                buffers = list(result[:2])
                partial = result[2]
                rest = result[3:]
            else:
                previous[c], current[c] = current[c], (result[0], 0)
                received[c] = exchange(result[1], result[2])
                partial = result[3]
        partials.append(partial)

    keep, give = rest
    got = lax.ppermute(give, "vec", [(i, i ^ 1) for i in range(groups)])
    piece = jax.ShapeDtypeStruct((STEPS, quarter, width), F32)
    mine, give = pl.pallas_call(
        fold_kernel,
        out_shape=[piece, piece],
        in_specs=[smem(), vmem(), vmem()],
        out_specs=[vmem(), vmem()],
        compiler_params=params(),
        cost_estimate=cost(1e5, 1e6),
        name="fold",
    )(index, keep, got)
    got = lax.ppermute(give, "vec", [(i, i ^ 2) for i in range(groups)])

    prior_count = prior_moments.shape[0]
    moment_count = prior_count + STEPS
    even_table, odd_table = jackson_split(moment_count, ENERGIES)
    group, lanes = 8, 128
    small = pl.BlockSpec((STEPS, group, lanes), lambda i, h: (0, i, h))
    new_moments, energy_map = pl.pallas_call(
        functools.partial(energy_kernel, vec_dev * groups),
        out_shape=[piece, jax.ShapeDtypeStruct((ENERGIES, quarter, width), F32)],
        grid=(quarter // group, width // lanes),
        in_specs=[
            pl.BlockSpec(even_table.shape, lambda i, h: (0, 0)),
            pl.BlockSpec(odd_table.shape, lambda i, h: (0, 0)),
            pl.BlockSpec((prior_count, group, lanes), lambda i, h: (0, i, h)),
            small,
            small,
        ],
        out_specs=[small, pl.BlockSpec((ENERGIES, group, lanes), lambda i, h: (0, i, h))],
        scratch_shapes=[pltpu.VMEM((moment_count * group, lanes), F32)],
        compiler_params=params(),
        cost_estimate=cost(4e9, 2.2e7),
        name="energy",
    )(jnp.asarray(even_table), jnp.asarray(odd_table), prior_moments, mine, got)
    return buffers[0], buffers[1], new_moments, energy_map


def solution(mesh):
    return jax.shard_map(
        per_device,
        mesh=mesh,
        in_specs=(
            P("vec", "dom", None),
            P("vec", "dom", None),
            P("vec", "dom", None),
            P(None, ("dom", "vec"), None),
            P(None, "dom", None),
            P(),
            P("dom", None),
            P("dom", None, None),
            P("dom", None),
        ),
        out_specs=(
            P("vec", "dom", None),
            P("vec", "dom", None),
            P(None, ("dom", "vec"), None),
            P(None, ("dom", "vec"), None),
        ),
        check_vma=False,
    )
```

time: 85.3 us -> 84.2 us (0.987)
  local copies, waits for them, and re-layouts: 9.99 us -> 7.7 us
    unnamed x30 -> x22, local copies, waits for them, and re-layouts: 9.99 us -> 7.7 us
    pallas_call x1, Pallas kernels: 0.82 us -> 2.07 us  [per_device(): pl.pallas_call(functools.partial(first_kernel, rim, vecs), out_shape=[jax...]
    pallas_call x1, Pallas kernels: 9.87 us -> 8.91 us  [per_device(): pl.pallas_call(functools.partial(energy_kernel, vec_dev * groups), out_sh...]
  transfers between devices with their start and end apart: 18 -> 18, of which waited for: 3 -> 3; matrix products, arithmetic and copies ran while one was open for 2% -> 0% of each run, Pallas kernels for 31% -> 30%
where the time goes in v1:
time: 84.2 us; the launch traced here: 83.8 us
  Pallas kernels  41.2 us (49%)
  starting transfers between devices  26.7 us (32%)
  local copies, waits for them, and re-layouts  7.7 us (9%)
  waiting for transfers between devices  7.17 us (9%)
    pallas_call x8, Pallas kernels, per_device(): pl.pallas_call(functools.partial(step_kernel, cfg), out_shape=outs, in_sp...  27.5 us
    ppermute x8, starting transfers between devices, exchange(): got_b = lax.ppermute(b, 'dom', swap_b)  19 us
    pallas_call x1, Pallas kernels, per_device(): pl.pallas_call(functools.partial(energy_kernel, vec_dev * groups), out_sh...  8.91 us
    unnamed x22, local copies, waits for them, and re-layouts  7.7 us
    ppermute x8, starting transfers between devices, exchange(): got_a = lax.ppermute(a, 'dom', swap_a)  6.05 us
    ppermute x1, waiting for transfers between devices, per_device(): got = lax.ppermute(give, 'vec', [(i, i ^ 2) for i in range(groups)])  4.02 us
    pallas_call x1, Pallas kernels, per_device(): pl.pallas_call(functools.partial(prep_kernel, rim), out_shape=[jax.ShapeD...  2.22 us
    pallas_call x1, Pallas kernels, per_device(): pl.pallas_call(functools.partial(first_kernel, rim, vecs), out_shape=[jax...  2.07 us
  transfers between devices with their start and end apart: 18, of which 3 were waited for; matrix products, arithmetic and copies ran while one was open for 0% of the time, Pallas kernels for 30%

profile of v1, /device:TPU:0, one launch (start us, length us, event | category | flops | bytes accessed | tf_op | source)
XLA Modules:
  0.0 83.8 jit_solution(11248659564716309823)
XLA Ops:
  0.7 1.0 %copy-done.1 = f32[4,128,256]{2,1,0:T(8,128)S(1)} copy-done((f32[4,128,256]{2,1,0:T(8,128)S(1)}, f32[4,128,256]{2,1,0:T(8,128)}, u32[]{:S(2)}) %copy-start.1) | copy-done | bytes 524312
  2.5 2.1 %first_sends.1 = (bf16[96,256]{1,0:T(8,128)(2,1)S(1)}, f32[4,128,256]{2,1,0:T(8,128)S(1)}, f32[48,512]{1,0:T(8,128)S(1)}, f32[48,512]{1,0:T(8,128)S(1)}, f32[48,512]{1,0:T(8,128)S(1)}, /*index=5*/f32[48,512]{1,0:T(8,128)S(1)}) custom-call(s32[3]{0:T(128)S(1)} %pad_add_fusion.index_ref, s32[1,2,48]{2,1,0:T(2,128)S(1)} %copy-done.7, f32[4,128,256]{2,1,0:T(8,128)S(1)} %copy-done.1), custom_call_target="tpu_custom_call" | custom-call | flops 100000000 | bytes 1000000 | tf_op jit(solution)/shard_map/first_sends/pallas_call | solution.py:326
  4.5 3.0 %collective-permute-start.2 = (f32[48,512]{1,0:T(8,128)S(1)}, f32[48,512]{1,0:T(8,128)S(1)}, u32[]{:S(2)}, u32[]{:S(2)}) collective-permute-start(f32[48,512]{1,0:T(8,128)S(1)} %get-tuple-element.61), channel_id=1, source_target_pairs={{0,1},{1,0},{2,3},{3,2},{4,5},{5,4},{6,7},{7,6},{8,9},{9,8},{10,11... | collective-permute-start | bytes 294920 | tf_op jit(solution)/shard_map/ppermute | solution.py:344
  7.6 3.6 %collective-permute-start.3 = (f32[48,512]{1,0:T(8,128)S(1)}, f32[48,512]{1,0:T(8,128)S(1)}, u32[]{:S(2)}, u32[]{:S(2)}) collective-permute-start(f32[48,512]{1,0:T(8,128)S(1)} %get-tuple-element.62), channel_id=1, source_target_pairs={{0,7},{1,2},{2,1},{3,4},{4,3},{5,6},{6,5},{7,0},{8,15},{9,10},{10,... | collective-permute-start | bytes 294920 | tf_op jit(solution)/shard_map/ppermute | solution.py:343
  11.1 1.9 %collective-permute-start.1 = (f32[48,512]{1,0:T(8,128)S(1)}, f32[48,512]{1,0:T(8,128)S(1)}, u32[]{:S(2)}, u32[]{:S(2)}) collective-permute-start(f32[48,512]{1,0:T(8,128)S(1)} %get-tuple-element.60), channel_id=1, source_target_pairs={{0,7},{1,2},{2,1},{3,4},{4,3},{5,6},{6,5},{7,0},{8,15},{9,10},{10,... | collective-permute-start | bytes 294920 | tf_op jit(solution)/shard_map/ppermute | solution.py:343
  13.1 1.6 %copy-done = f32[8,256,256]{2,1,0:T(8,128)S(1)} copy-done((f32[8,256,256]{2,1,0:T(8,128)S(1)}, f32[8,256,256]{2,1,0:T(8,128)}, u32[]{:S(2)}) %copy-start) | copy-done | bytes 2097176
  14.7 1.0 %copy-done.2 = f32[4,128,256]{2,1,0:T(8,128)S(1)} copy-done((f32[4,128,256]{2,1,0:T(8,128)S(1)}, f32[4,128,256]{2,1,0:T(8,128)}, u32[]{:S(2)}) %copy-start.2) | copy-done | bytes 524312
  15.7 1.0 %copy-done.3 = f32[4,128,256]{2,1,0:T(8,128)S(1)} copy-done((f32[4,128,256]{2,1,0:T(8,128)S(1)}, f32[4,128,256]{2,1,0:T(8,128)}, u32[]{:S(2)}) %copy-start.3) | copy-done | bytes 524312
  16.7 0.9 %copy-done.4 = f32[3,128,128]{2,1,0:T(8,128)S(1)} copy-done((f32[3,128,128]{2,1,0:T(8,128)S(1)}, f32[3,128,128]{2,1,0:T(8,128)}, u32[]{:S(2)}) %copy-start.4) | copy-done | bytes 196632
  18.3 0.7 copy-done.6
  19.0 2.2 %tables.1 = (bf16[1024,512]{1,0:T(8,128)(2,1)S(1)}, bf16[2048,256]{1,0:T(8,128)(2,1)S(1)}, bf16[2048,256]{1,0:T(8,128)(2,1)S(1)}, f32[4,128,256]{2,1,0:T(8,128)S...) custom-call(s32[3]{0:T(128)S(1)} %pad_add_fusion.index_ref, s32[4,128]{1,0:T(4,128)S(1)} %bitcast.5, ...), custom_call_target="tpu_custom_call" | custom-call | flops 10000000 | bytes 8000000 | tf_op jit(solution)/shard_map/tables/pallas_call | solution.py:349
  21.3 3.2 %step0_0.1 = (f32[2,128,256]{2,1,0:T(8,128)S(1)}, f32[48,512]{1,0:T(8,128)S(1)}, f32[48,512]{1,0:T(8,128)S(1)}, f32[128,256]{1,0:T(8,128)S(1)}) custom-call(s32[3]{0:T(128)S(1)} %pad_add_fusion.index_ref, bf16[1024,512]{1,0:T(8,128)(2,1)S(1)} %get-tuple-element.51.mix_ref, bf16[2048,256]{1,0:T(8,128)(2,1)S(1)} %get-tuple-element.52.high_ref, ...), custom_call_target="tpu_custom_call" | custom-call | flops 1500000000 | bytes 5000000 | tf_op jit(solution)/shard_map/step0_0/pallas_call | solution.py:415
  25.1 2.3 %collective-permute-start.7 = (f32[48,512]{1,0:T(8,128)S(1)}, f32[48,512]{1,0:T(8,128)S(1)}, u32[]{:S(2)}, u32[]{:S(2)}) collective-permute-start(f32[48,512]{1,0:T(8,128)S(1)} %get-tuple-element.69), channel_id=1, source_target_pairs={{0,7},{1,2},{2,1},{3,4},{4,3},{5,6},{6,5},{7,0},{8,15},{9,10},{10,... | collective-permute-start | bytes 294920 | tf_op jit(solution)/shard_map/ppermute | solution.py:343
  27.4 3.2 %step0_1.1 = (f32[2,128,256]{2,1,0:T(8,128)S(1)}, f32[48,512]{1,0:T(8,128)S(1)}, f32[48,512]{1,0:T(8,128)S(1)}, f32[128,256]{1,0:T(8,128)S(1)}) custom-call(s32[3]{0:T(128)S(1)} %pad_add_fusion.index_ref, bf16[1024,512]{1,0:T(8,128)(2,1)S(1)} %get-tuple-element.51.mix_ref, bf16[2048,256]{1,0:T(8,128)(2,1)S(1)} %get-tuple-element.52.high_ref, ...), custom_call_target="tpu_custom_call" | custom-call | flops 1500000000 | bytes 5000000 | tf_op jit(solution)/shard_map/step0_1/pallas_call | solution.py:415
  30.6 0.8 collective-permute-start.4
  31.5 1.8 %collective-permute-start.5 = (f32[48,512]{1,0:T(8,128)S(1)}, f32[48,512]{1,0:T(8,128)S(1)}, u32[]{:S(2)}, u32[]{:S(2)}) collective-permute-start(f32[48,512]{1,0:T(8,128)S(1)} %get-tuple-element.66), channel_id=1, source_target_pairs={{0,7},{1,2},{2,1},{3,4},{4,3},{5,6},{6,5},{7,0},{8,15},{9,10},{10,... | collective-permute-start | bytes 294920 | tf_op jit(solution)/shard_map/ppermute | solution.py:343
  33.2 3.2 %step1_0.1 = (f32[2,128,256]{2,1,0:T(8,128)S(1)}, f32[48,512]{1,0:T(8,128)S(1)}, f32[48,512]{1,0:T(8,128)S(1)}, f32[128,256]{1,0:T(8,128)S(1)}) custom-call(s32[3]{0:T(128)S(1)} %pad_add_fusion.index_ref, bf16[1024,512]{1,0:T(8,128)(2,1)S(1)} %get-tuple-element.51.mix_ref, bf16[2048,256]{1,0:T(8,128)(2,1)S(1)} %get-tuple-element.52.high_ref, ...), custom_call_target="tpu_custom_call" | custom-call | flops 1500000000 | bytes 5000000 | tf_op jit(solution)/shard_map/step1_0/pallas_call | solution.py:415
  36.5 3.5 %collective-permute-start.11 = (f32[48,512]{1,0:T(8,128)S(1)}, f32[48,512]{1,0:T(8,128)S(1)}, u32[]{:S(2)}, u32[]{:S(2)}) collective-permute-start(f32[48,512]{1,0:T(8,128)S(1)} %get-tuple-element.76), channel_id=1, source_target_pairs={{0,7},{1,2},{2,1},{3,4},{4,3},{5,6},{6,5},{7,0},{8,15},{9,10},{10,... | collective-permute-start | bytes 294920 | tf_op jit(solution)/shard_map/ppermute | solution.py:343
  40.0 3.2 %step1_1.1 = (f32[2,128,256]{2,1,0:T(8,128)S(1)}, f32[48,512]{1,0:T(8,128)S(1)}, f32[48,512]{1,0:T(8,128)S(1)}, f32[128,256]{1,0:T(8,128)S(1)}) custom-call(s32[3]{0:T(128)S(1)} %pad_add_fusion.index_ref, bf16[1024,512]{1,0:T(8,128)(2,1)S(1)} %get-tuple-element.51.mix_ref, bf16[2048,256]{1,0:T(8,128)(2,1)S(1)} %get-tuple-element.52.high_ref, ...), custom_call_target="tpu_custom_call" | custom-call | flops 1500000000 | bytes 5000000 | tf_op jit(solution)/shard_map/step1_1/pallas_call | solution.py:415
  43.3 1.9 %collective-permute-start.9 = (f32[48,512]{1,0:T(8,128)S(1)}, f32[48,512]{1,0:T(8,128)S(1)}, u32[]{:S(2)}, u32[]{:S(2)}) collective-permute-start(f32[48,512]{1,0:T(8,128)S(1)} %get-tuple-element.73), channel_id=1, source_target_pairs={{0,7},{1,2},{2,1},{3,4},{4,3},{5,6},{6,5},{7,0},{8,15},{9,10},{10,... | collective-permute-start | bytes 294920 | tf_op jit(solution)/shard_map/ppermute | solution.py:343
  45.2 3.2 %step2_0.1 = (f32[2,128,256]{2,1,0:T(8,128)S(1)}, f32[48,512]{1,0:T(8,128)S(1)}, f32[48,512]{1,0:T(8,128)S(1)}, f32[128,256]{1,0:T(8,128)S(1)}) custom-call(s32[3]{0:T(128)S(1)} %pad_add_fusion.index_ref, bf16[1024,512]{1,0:T(8,128)(2,1)S(1)} %get-tuple-element.51.mix_ref, bf16[2048,256]{1,0:T(8,128)(2,1)S(1)} %get-tuple-element.52.high_ref, ...), custom_call_target="tpu_custom_call" | custom-call | flops 1500000000 | bytes 5000000 | tf_op jit(solution)/shard_map/step2_0/pallas_call | solution.py:415
  49.0 2.4 %collective-permute-start.15 = (f32[48,512]{1,0:T(8,128)S(1)}, f32[48,512]{1,0:T(8,128)S(1)}, u32[]{:S(2)}, u32[]{:S(2)}) collective-permute-start(f32[48,512]{1,0:T(8,128)S(1)} %get-tuple-element.83), channel_id=1, source_target_pairs={{0,7},{1,2},{2,1},{3,4},{4,3},{5,6},{6,5},{7,0},{8,15},{9,10},{10,... | collective-permute-start | bytes 294920 | tf_op jit(solution)/shard_map/ppermute | solution.py:343
  51.4 3.2 %step2_1.1 = (f32[2,128,256]{2,1,0:T(8,128)S(1)}, f32[48,512]{1,0:T(8,128)S(1)}, f32[48,512]{1,0:T(8,128)S(1)}, f32[128,256]{1,0:T(8,128)S(1)}) custom-call(s32[3]{0:T(128)S(1)} %pad_add_fusion.index_ref, bf16[1024,512]{1,0:T(8,128)(2,1)S(1)} %get-tuple-element.51.mix_ref, bf16[2048,256]{1,0:T(8,128)(2,1)S(1)} %get-tuple-element.52.high_ref, ...), custom_call_target="tpu_custom_call" | custom-call | flops 1500000000 | bytes 5000000 | tf_op jit(solution)/shard_map/step2_1/pallas_call | solution.py:415
  54.6 0.7 collective-permute-start.12
  55.4 1.8 %collective-permute-start.13 = (f32[48,512]{1,0:T(8,128)S(1)}, f32[48,512]{1,0:T(8,128)S(1)}, u32[]{:S(2)}, u32[]{:S(2)}) collective-permute-start(f32[48,512]{1,0:T(8,128)S(1)} %get-tuple-element.80), channel_id=1, source_target_pairs={{0,7},{1,2},{2,1},{3,4},{4,3},{5,6},{6,5},{7,0},{8,15},{9,10},{10,... | collective-permute-start | bytes 294920 | tf_op jit(solution)/shard_map/ppermute | solution.py:343
  57.1 3.9 %step3_0.1 = (f32[4,128,256]{2,1,0:T(8,128)}, f32[4,128,256]{2,1,0:T(8,128)}, f32[128,256]{1,0:T(8,128)S(1)}) custom-call(s32[3]{0:T(128)S(1)} %pad_add_fusion.index_ref, bf16[1024,512]{1,0:T(8,128)(2,1)S(1)} %get-tuple-element.51.mix_ref, bf16[2048,256]{1,0:T(8,128)(2,1)S(1)} %get-tuple-element.52.high_ref, ...), custom_call_target="tpu_custom_call" | custom-call | flops 1500000000 | bytes 5000000 | tf_op jit(solution)/shard_map/step3_0/pallas_call | solution.py:415
  61.1 1.6 %collective-permute-done.13.recv_b = f32[48,512]{1,0:T(8,128)S(1)} collective-permute-done((f32[48,512]{1,0:T(8,128)S(1)}, f32[48,512]{1,0:T(8,128)S(1)}, u32[]{:S(2)}, u32[]{:S(2)}) %collective-permute-start.13) | collective-permute-done | bytes 98336 | tf_op jit(solution)/shard_map/ppermute | solution.py:343
  62.7 4.4 %step3_1.1 = (f32[4,128,256]{2,1,0:T(8,128)}, f32[4,128,256]{2,1,0:T(8,128)}, f32[128,256]{1,0:T(8,128)}, f32[4,2,32,256]{3,2,1,0:T(8,128)S(1)}, f32[4,2,32,256]{3,2,1,0:T(8,128)S(1)}) custom-call(s32[3]{0:T(128)S(1)} %pad_add_fusion.index_ref, bf16[1024,512]{1,0:T(8,128)(2,1)S(1)} %get-tuple-element.51.mix_ref, ...), custom_call_target="tpu_custom_call", output_to_operand_aliasing={{0}: (15, {}), {1}: (16, {})} | custom-call | flops 1500000000 | bytes 5000000 | tf_op jit(solution)/shard_map/step3_1/pallas_call | solution.py:415
  67.1 1.5 %collective-permute-done.16.got_ref = f32[4,2,32,256]{3,2,1,0:T(8,128)S(1)} collective-permute-done((f32[4,2,32,256]{3,2,1,0:T(8,128)S(1)}, f32[4,2,32,256]{3,2,1,0:T(8,128)S(1)}, u32[]{:S(2)}, u32[]{:S(2)}) %collective-permute-start.16) | collective-permute-done | bytes 262176 | tf_op jit(solution)/shard_map/ppermute | solution.py:437
  69.2 1.6 %collective-permute-start.17 = (f32[4,32,256]{2,1,0:T(8,128)S(1)}, f32[4,32,256]{2,1,0:T(8,128)S(1)}, u32[]{:S(2)}, u32[]{:S(2)}) collective-permute-start(f32[4,32,256]{2,1,0:T(8,128)S(1)} %get-tuple-element.95), channel_id=1, source_target_pairs={{0,16},{8,24},{16,0},{24,8},{1,17},{9,25},{17,1},{25,9},{2,18},{10... | collective-permute-start | bytes 393224 | tf_op jit(solution)/shard_map/ppermute | solution.py:448
  70.8 4.0 %collective-permute-done.17.got_ref = f32[4,32,256]{2,1,0:T(8,128)S(1)} collective-permute-done((f32[4,32,256]{2,1,0:T(8,128)S(1)}, f32[4,32,256]{2,1,0:T(8,128)S(1)}, u32[]{:S(2)}, u32[]{:S(2)}) %collective-permute-start.17) | collective-permute-done | bytes 131104 | tf_op jit(solution)/shard_map/ppermute | solution.py:448
  74.9 8.9 %energy.1 = (f32[4,32,256]{2,1,0:T(8,128)}, f32[512,32,256]{2,1,0:T(8,128)}) custom-call(bf16[256,256]{1,0:T(8,128)(2,1)S(1)} %copy-done.10, bf16[256,256]{1,0:T(8,128)(2,1)S(1)} %copy-done.9, f32[124,32,256]{2,1,0:T(8,128)S(1)} %copy-done.8, f32[4,32,256]{2,1,0:T(8,128)S(1)} %get-tuple-element.94.mine_ref, f32[4,32,256]{2,1,0:T(8,128)S(1)} %collective-permute-done.17.got_ref), custom_call_target="tpu_custom_call" | custom-call | flops 4000000000 | bytes 22000000 | tf_op jit(solution)/shard_map/energy/pallas_call | solution.py:455
  (39 shorter events, 3.6 us)
Async XLA Ops:
  0.7 1.0 %copy-start.1 = (f32[4,128,256]{2,1,0:T(8,128)S(1)}, f32[4,128,256]{2,1,0:T(8,128)}, u32[]{:S(2)}) copy-start(f32[4,128,256]{2,1,0:T(8,128)} %cur_hbm.1) | copy-start | bytes 1572868
  1.8 0.7 copy-start.7
  4.5 16.7 %collective-permute-start.2 = (f32[48,512]{1,0:T(8,128)S(1)}, f32[48,512]{1,0:T(8,128)S(1)}, u32[]{:S(2)}, u32[]{:S(2)}) collective-permute-start(f32[48,512]{1,0:T(8,128)S(1)} %get-tuple-element.61), channel_id=1, source_target_pairs={{0,1},{1,0},{2,3},{3,2},{4,5},{5,4},{6,7},{7,6},{8,9},{9,8},{10,11... | collective-permute-start | bytes 294920 | tf_op jit(solution)/shard_map/ppermute | solution.py:344
  7.6 13.7 %collective-permute-start.3 = (f32[48,512]{1,0:T(8,128)S(1)}, f32[48,512]{1,0:T(8,128)S(1)}, u32[]{:S(2)}, u32[]{:S(2)}) collective-permute-start(f32[48,512]{1,0:T(8,128)S(1)} %get-tuple-element.62), channel_id=1, source_target_pairs={{0,7},{1,2},{2,1},{3,4},{4,3},{5,6},{6,5},{7,0},{8,15},{9,10},{10,... | collective-permute-start | bytes 294920 | tf_op jit(solution)/shard_map/ppermute | solution.py:343
  11.1 16.3 %collective-permute-start = (f32[48,512]{1,0:T(8,128)S(1)}, f32[48,512]{1,0:T(8,128)S(1)}, u32[]{:S(2)}, u32[]{:S(2)}) collective-permute-start(f32[48,512]{1,0:T(8,128)S(1)} %get-tuple-element.59), channel_id=1, source_target_pairs={{0,1},{1,0},{2,3},{3,2},{4,5},{5,4},{6,7},{7,6},{8,9},{9,8},{10,11... | collective-permute-start | bytes 294920 | tf_op jit(solution)/shard_map/ppermute | solution.py:344
  11.1 16.3 %collective-permute-start.1 = (f32[48,512]{1,0:T(8,128)S(1)}, f32[48,512]{1,0:T(8,128)S(1)}, u32[]{:S(2)}, u32[]{:S(2)}) collective-permute-start(f32[48,512]{1,0:T(8,128)S(1)} %get-tuple-element.60), channel_id=1, source_target_pairs={{0,7},{1,2},{2,1},{3,4},{4,3},{5,6},{6,5},{7,0},{8,15},{9,10},{10,... | collective-permute-start | bytes 294920 | tf_op jit(solution)/shard_map/ppermute | solution.py:343
  13.1 1.6 %copy-start = (f32[8,256,256]{2,1,0:T(8,128)S(1)}, f32[8,256,256]{2,1,0:T(8,128)}, u32[]{:S(2)}) copy-start(f32[8,256,256]{2,1,0:T(8,128)} %kinds_hbm.1) | copy-start | bytes 6291460
  14.6 1.0 %copy-start.2 = (f32[4,128,256]{2,1,0:T(8,128)S(1)}, f32[4,128,256]{2,1,0:T(8,128)}, u32[]{:S(2)}) copy-start(f32[4,128,256]{2,1,0:T(8,128)} %prev_hbm.1) | copy-start | bytes 1572868
  15.7 1.0 %copy-start.3 = (f32[4,128,256]{2,1,0:T(8,128)S(1)}, f32[4,128,256]{2,1,0:T(8,128)}, u32[]{:S(2)}) copy-start(f32[4,128,256]{2,1,0:T(8,128)} %probe_hbm.1) | copy-start | bytes 1572868
  16.7 0.9 %copy-start.4 = (f32[3,128,128]{2,1,0:T(8,128)S(1)}, f32[3,128,128]{2,1,0:T(8,128)}, u32[]{:S(2)}) copy-start(f32[3,128,128]{2,1,0:T(8,128)} %site_hbm.1) | copy-start | bytes 589828
  17.7 0.7 copy-start.5
  18.3 0.7 copy-start.6
  24.5 8.7 %collective-permute-start.6 = (f32[48,512]{1,0:T(8,128)S(1)}, f32[48,512]{1,0:T(8,128)S(1)}, u32[]{:S(2)}, u32[]{:S(2)}) collective-permute-start(f32[48,512]{1,0:T(8,128)S(1)} %get-tuple-element.68), channel_id=1, source_target_pairs={{0,1},{1,0},{2,3},{3,2},{4,5},{5,4},{6,7},{7,6},{8,9},{9,8},{10,11... | collective-permute-start | bytes 294920 | tf_op jit(solution)/shard_map/ppermute | solution.py:344
  25.1 8.1 %collective-permute-start.7 = (f32[48,512]{1,0:T(8,128)S(1)}, f32[48,512]{1,0:T(8,128)S(1)}, u32[]{:S(2)}, u32[]{:S(2)}) collective-permute-start(f32[48,512]{1,0:T(8,128)S(1)} %get-tuple-element.69), channel_id=1, source_target_pairs={{0,7},{1,2},{2,1},{3,4},{4,3},{5,6},{6,5},{7,0},{8,15},{9,10},{10,... | collective-permute-start | bytes 294920 | tf_op jit(solution)/shard_map/ppermute | solution.py:343
  30.6 9.3 %collective-permute-start.4 = (f32[48,512]{1,0:T(8,128)S(1)}, f32[48,512]{1,0:T(8,128)S(1)}, u32[]{:S(2)}, u32[]{:S(2)}) collective-permute-start(f32[48,512]{1,0:T(8,128)S(1)} %get-tuple-element.65), channel_id=1, source_target_pairs={{0,1},{1,0},{2,3},{3,2},{4,5},{5,4},{6,7},{7,6},{8,9},{9,8},{10,11... | collective-permute-start | bytes 294920 | tf_op jit(solution)/shard_map/ppermute | solution.py:344
  31.5 8.5 %collective-permute-start.5 = (f32[48,512]{1,0:T(8,128)S(1)}, f32[48,512]{1,0:T(8,128)S(1)}, u32[]{:S(2)}, u32[]{:S(2)}) collective-permute-start(f32[48,512]{1,0:T(8,128)S(1)} %get-tuple-element.66), channel_id=1, source_target_pairs={{0,7},{1,2},{2,1},{3,4},{4,3},{5,6},{6,5},{7,0},{8,15},{9,10},{10,... | collective-permute-start | bytes 294920 | tf_op jit(solution)/shard_map/ppermute | solution.py:343
  36.4 8.8 %collective-permute-start.10 = (f32[48,512]{1,0:T(8,128)S(1)}, f32[48,512]{1,0:T(8,128)S(1)}, u32[]{:S(2)}, u32[]{:S(2)}) collective-permute-start(f32[48,512]{1,0:T(8,128)S(1)} %get-tuple-element.75), channel_id=1, source_target_pairs={{0,1},{1,0},{2,3},{3,2},{4,5},{5,4},{6,7},{7,6},{8,9},{9,8},{10,11... | collective-permute-start | bytes 294920 | tf_op jit(solution)/shard_map/ppermute | solution.py:344
  36.5 8.7 %collective-permute-start.11 = (f32[48,512]{1,0:T(8,128)S(1)}, f32[48,512]{1,0:T(8,128)S(1)}, u32[]{:S(2)}, u32[]{:S(2)}) collective-permute-start(f32[48,512]{1,0:T(8,128)S(1)} %get-tuple-element.76), channel_id=1, source_target_pairs={{0,7},{1,2},{2,1},{3,4},{4,3},{5,6},{6,5},{7,0},{8,15},{9,10},{10,... | collective-permute-start | bytes 294920 | tf_op jit(solution)/shard_map/ppermute | solution.py:343
  43.2 8.2 %collective-permute-start.8 = (f32[48,512]{1,0:T(8,128)S(1)}, f32[48,512]{1,0:T(8,128)S(1)}, u32[]{:S(2)}, u32[]{:S(2)}) collective-permute-start(f32[48,512]{1,0:T(8,128)S(1)} %get-tuple-element.72), channel_id=1, source_target_pairs={{0,1},{1,0},{2,3},{3,2},{4,5},{5,4},{6,7},{7,6},{8,9},{9,8},{10,11... | collective-permute-start | bytes 294920 | tf_op jit(solution)/shard_map/ppermute | solution.py:344
  43.3 8.1 %collective-permute-start.9 = (f32[48,512]{1,0:T(8,128)S(1)}, f32[48,512]{1,0:T(8,128)S(1)}, u32[]{:S(2)}, u32[]{:S(2)}) collective-permute-start(f32[48,512]{1,0:T(8,128)S(1)} %get-tuple-element.73), channel_id=1, source_target_pairs={{0,7},{1,2},{2,1},{3,4},{4,3},{5,6},{6,5},{7,0},{8,15},{9,10},{10,... | collective-permute-start | bytes 294920 | tf_op jit(solution)/shard_map/ppermute | solution.py:343
  48.4 8.7 %collective-permute-start.14 = (f32[48,512]{1,0:T(8,128)S(1)}, f32[48,512]{1,0:T(8,128)S(1)}, u32[]{:S(2)}, u32[]{:S(2)}) collective-permute-start(f32[48,512]{1,0:T(8,128)S(1)} %get-tuple-element.82), channel_id=1, source_target_pairs={{0,1},{1,0},{2,3},{3,2},{4,5},{5,4},{6,7},{7,6},{8,9},{9,8},{10,11... | collective-permute-start | bytes 294920 | tf_op jit(solution)/shard_map/ppermute | solution.py:344
  49.0 8.1 %collective-permute-start.15 = (f32[48,512]{1,0:T(8,128)S(1)}, f32[48,512]{1,0:T(8,128)S(1)}, u32[]{:S(2)}, u32[]{:S(2)}) collective-permute-start(f32[48,512]{1,0:T(8,128)S(1)} %get-tuple-element.83), channel_id=1, source_target_pairs={{0,7},{1,2},{2,1},{3,4},{4,3},{5,6},{6,5},{7,0},{8,15},{9,10},{10,... | collective-permute-start | bytes 294920 | tf_op jit(solution)/shard_map/ppermute | solution.py:343
  54.6 6.5 %collective-permute-start.12 = (f32[48,512]{1,0:T(8,128)S(1)}, f32[48,512]{1,0:T(8,128)S(1)}, u32[]{:S(2)}, u32[]{:S(2)}) collective-permute-start(f32[48,512]{1,0:T(8,128)S(1)} %get-tuple-element.79), channel_id=1, source_target_pairs={{0,1},{1,0},{2,3},{3,2},{4,5},{5,4},{6,7},{7,6},{8,9},{9,8},{10,11... | collective-permute-start | bytes 294920 | tf_op jit(solution)/shard_map/ppermute | solution.py:344
  55.4 7.3 %collective-permute-start.13 = (f32[48,512]{1,0:T(8,128)S(1)}, f32[48,512]{1,0:T(8,128)S(1)}, u32[]{:S(2)}, u32[]{:S(2)}) collective-permute-start(f32[48,512]{1,0:T(8,128)S(1)} %get-tuple-element.80), channel_id=1, source_target_pairs={{0,7},{1,2},{2,1},{3,4},{4,3},{5,6},{6,5},{7,0},{8,15},{9,10},{10,... | collective-permute-start | bytes 294920 | tf_op jit(solution)/shard_map/ppermute | solution.py:343
  61.0 13.8 %copy-start.8 = (f32[124,32,256]{2,1,0:T(8,128)S(1)}, f32[124,32,256]{2,1,0:T(8,128)}, u32[]{:S(2)}) copy-start(f32[124,32,256]{2,1,0:T(8,128)} %prior_ref.1) | copy-start | bytes 12189700
  61.0 13.8 %copy-start.9 = (bf16[256,256]{1,0:T(8,128)(2,1)S(1)}, bf16[256,256]{1,0:T(8,128)(2,1)}, u32[]{:S(2)}) copy-start(bf16[256,256]{1,0:T(8,128)(2,1)} %constant.41.clone.odd_ref) | copy-start | bytes 393220
  61.1 13.8 %copy-start.10 = (bf16[256,256]{1,0:T(8,128)(2,1)S(1)}, bf16[256,256]{1,0:T(8,128)(2,1)}, u32[]{:S(2)}) copy-start(bf16[256,256]{1,0:T(8,128)(2,1)} %constant.40.clone.even_ref) | copy-start | bytes 393220
  67.1 1.6 %collective-permute-start.16 = (f32[4,2,32,256]{3,2,1,0:T(8,128)S(1)}, f32[4,2,32,256]{3,2,1,0:T(8,128)S(1)}, u32[]{:S(2)}, u32[]{:S(2)}) collective-permute-start(f32[4,2,32,256]{3,2,1,0:T(8,128)S(1)} %get-tuple-element.93), channel_id=1, source_target_pairs={{0,8},{8,0},{16,24},{24,16},{1,9},{9,1},{17,25},{25,17},{2,10},{10... | collective-permute-start | bytes 786440 | tf_op jit(solution)/shard_map/ppermute | solution.py:437
  69.2 5.6 %collective-permute-start.17 = (f32[4,32,256]{2,1,0:T(8,128)S(1)}, f32[4,32,256]{2,1,0:T(8,128)S(1)}, u32[]{:S(2)}, u32[]{:S(2)}) collective-permute-start(f32[4,32,256]{2,1,0:T(8,128)S(1)} %get-tuple-element.95), channel_id=1, source_target_pairs={{0,16},{8,24},{16,0},{24,8},{1,17},{9,25},{17,1},{25,9},{2,18},{10... | collective-permute-start | bytes 393224 | tf_op jit(solution)/shard_map/ppermute | solution.py:448

commit v2 on v1

--- a/solution.py
+++ b/solution.py
@@ -8,6 +8,7 @@
 from jax.experimental import pallas as pl
 from jax.experimental.pallas import tpu as pltpu
 from jax.sharding import PartitionSpec as P
+
 
 ENERGIES = 512
 STEPS = 4
@@ -66,6 +67,14 @@
 
 def any_space():
     return pl.BlockSpec(memory_space=pl.ANY)
+
+
+def hbm():
+    return pl.BlockSpec(memory_space=pltpu.HBM)
+
+
+def stay(x):
+    return pltpu.with_memory_space_constraint(x, pltpu.HBM)
 
 
 def first_kernel(rim, vecs, index_ref, lists_hbm, cur_hbm, pick_ref, cur_ref, *rest):
@@ -105,8 +114,8 @@
 def prep_kernel(
     rim,
     index_ref,
-    cols_ref,
-    ids_ref,
+    cols_hbm,
+    ids_hbm,
     kinds_hbm,
     prev_hbm,
     probe_hbm,
@@ -117,6 +126,8 @@
     prev_ref,
     probe_ref,
     site_ref,
+    cols_ref,
+    ids_ref,
     kinds,
     sems,
 ):
@@ -127,6 +138,12 @@
         pltpu.make_async_copy(kinds_hbm.at[n], kinds.at[n], sems.at[n]) for n in range(kind_count)
     ]
     fetched = ((prev_hbm, prev_ref), (probe_hbm, probe_ref), (site_hbm, site_ref))
+    small = [
+        pltpu.make_async_copy(cols_hbm, cols_ref, sems.at[kind_count + 3]),
+        pltpu.make_async_copy(ids_hbm, ids_ref, sems.at[kind_count + 4]),
+    ]
+    for copy in small:
+        copy.start()
     for i, (source, target) in enumerate(fetched):
         copies.append(pltpu.make_async_copy(source, target, sems.at[kind_count + i]))
     for copy in copies:
@@ -136,6 +153,8 @@
     corner = lax.broadcasted_iota(jnp.int32, (blocks, blocks), 0)
     diagonal = corner == lax.broadcasted_iota(jnp.int32, (blocks, blocks), 1)
     identity = jnp.where(diagonal, 1.0, 0.0).astype(BF16)
+    for copy in small:
+        copy.wait()
     e = cols_ref[...]
     crossed = jnp.where(e < blocks + rim, e + rim, e - rim)
     e = jnp.where(jnp.logical_and(even, e >= blocks), crossed, e)
@@ -174,32 +193,30 @@
     recv_b,
     *rest,
 ):
-    vecs, cur_at, prev_at, own_at, last, add_partial, older, aliased = cfg
+    vecs, cur_at, prev_at, own_at, last, add_partial, older, fold, aliased = cfg
     rest = list(rest)
     partial_in = rest.pop(0) if add_partial else None
     olders = [rest.pop(0) for _ in range(older)]
     rest = rest[aliased:]
+    out_ref, partial_out = rest[:2]
+    rest = rest[2:]
     if last:
-        prev_out, out_hbm, partial_out = rest.pop(0), rest.pop(0), rest.pop(0)
-        keep_ref = rest.pop(0) if older else None
-        give_ref = rest.pop(0) if older else None
-        source, mixed, out_ref, sems = rest
+        prev_out = rest.pop(0)
     else:
-        out_ref, send_a, send_b, partial_out = rest[:4]
-        source, mixed = rest[4:]
+        send_a, send_b = rest.pop(0), rest.pop(0)
+    if fold:
+        keep_ref, give_ref = rest.pop(0), rest.pop(0)
+    source, mixed = rest[:2]
     blocks, width = cur_ref.shape[1:]
     rim = recv_a.shape[0]
     padded = source.shape[1] // 2
     kind_count = mix_ref.shape[0] // blocks
     spin = width // 2
-    copies = []
     if last:
-        copies.append(
-            pltpu.make_async_copy(
-                cur_ref.at[pl.ds(cur_at, vecs)], prev_out.at[pl.ds(own_at, vecs)], sems.at[vecs]
-            )
+        copy = pltpu.make_async_copy(
+            cur_ref.at[pl.ds(cur_at, vecs)], prev_out.at[pl.ds(own_at, vecs)], rest[2]
         )
-        copies[0].start()
+        copy.start()
     for v in range(vecs):
         columns = slice(v * width, (v + 1) * width)
         pieces = [cur_ref[cur_at + v], recv_a[:, columns], recv_b[:, columns]]
@@ -233,9 +250,6 @@
         )
         following = hopping[v * blocks : (v + 1) * blocks] + onsite - prev_ref[prev_at + v]
         out_ref[v] = following
-        if last:
-            copies.append(pltpu.make_async_copy(out_ref.at[v], out_hbm.at[own_at + v], sems.at[v]))
-            copies[-1].start()
         term = probe_ref[own_at + v] * following
         partial = term if partial is None else partial + term
         if not last:
@@ -243,7 +257,7 @@
             send_a[:, v * width : (v + 1) * width] = got[:rim]
             send_b[:, v * width : (v + 1) * width] = got[rim:]
     partial_out[...] = partial
-    if last and older:
+    if fold:
         cores = 2
         quarter = keep_ref.shape[2]
         core = index_ref[1]
@@ -255,7 +269,7 @@
                 give_ref[s, y] = ref[
                     pl.ds(pl.multiple_of(base + (1 - core) * quarter, quarter), quarter)
                 ]
-    for copy in copies:
+    if last:
         copy.wait()
 
 
@@ -265,15 +279,41 @@
     give_ref[...] = keep_ref[:, 1 - y] + got_ref[:, 1 - y]
 
 
-def energy_kernel(vector_total, even_ref, odd_ref, prior_ref, mine_ref, got_ref, new_ref, map_ref, moments):
+def energy_kernel(
+    vector_total,
+    chunks,
+    even_ref,
+    odd_ref,
+    prior_ref,
+    early_mine,
+    early_got,
+    late_mine,
+    late_got,
+    *rest,
+):
+    finals = rest[:chunks]
+    new_ref, map_ref, cur_out, moments, sems = rest[chunks:]
+    vecs = finals[0].shape[0]
+    copies = [
+        pltpu.make_async_copy(finals[c], cur_out.at[pl.ds(c * vecs, vecs)], sems.at[c])
+        for c in range(chunks)
+    ]
+    step = pl.program_id(0) * pl.num_programs(1) + pl.program_id(1)
+
+    @pl.when(step == 0)
+    def _():
+        for copy in copies:
+            copy.start()
+
     prior_count, group, lanes = prior_ref.shape
-    steps = mine_ref.shape[0]
+    early, late = early_mine.shape[0], late_mine.shape[0]
+    steps = early + late
     half = even_ref.shape[0]
     pairs = (prior_count + steps) // 2
-    new = (mine_ref[...] + got_ref[...]) * (1.0 / vector_total)
-    new_ref[...] = new
+    new_ref[0:early] = (early_mine[...] + early_got[...]) * (1.0 / vector_total)
+    new_ref[early:steps] = (late_mine[...] + late_got[...]) * (1.0 / vector_total)
     moments[0 : prior_count * group] = prior_ref[...].reshape(prior_count * group, lanes)
-    moments[prior_count * group :] = new.reshape(steps * group, lanes)
+    moments[prior_count * group :] = new_ref[...].reshape(steps * group, lanes)
     flat = map_ref.reshape(2 * half * group, lanes)
     flip = 7 - lax.broadcasted_iota(jnp.int32, (8, lanes), 0)
     for b in range(0, group, 2):
@@ -293,6 +333,11 @@
                 turned = jnp.take_along_axis(minus[r : r + 8, columns], flip, axis=0)
                 top = 2 * half - 8 - r
                 flat[pl.ds(top * group + b + i, 8, stride=group)] = turned
+
+    @pl.when(step == pl.num_programs(0) * pl.num_programs(1) - 1)
+    def _():
+        for copy in copies:
+            copy.wait()
 
 
 def per_device(
@@ -327,7 +372,7 @@
         functools.partial(first_kernel, rim, vecs),
         out_shape=[jax.ShapeDtypeStruct((2 * rim, 2 * blocks), BF16), full_shape]
         + [rows] * (2 * chunks),
-        in_specs=[smem(), any_space(), any_space()],
+        in_specs=[smem(), hbm(), hbm()],
         out_specs=[vmem()] * (2 + 2 * chunks),
         scratch_shapes=[
             pltpu.VMEM(send_lists.shape, jnp.int32),
@@ -336,7 +381,7 @@
         compiler_params=params(),
         cost_estimate=cost(1e8, 1e6),
         name="first_sends",
-    )(index, send_lists, cheb_cur)
+    )(index, stay(send_lists), stay(cheb_cur))
     pick, cur_held, sends = first[0], first[1], list(first[2:])
 
     def exchange(a, b):
@@ -356,22 +401,46 @@
             full_shape,
             jax.ShapeDtypeStruct(site_terms.shape, F32),
         ],
-        in_specs=[smem(), vmem(), vmem()] + [any_space()] * 4,
+        in_specs=[smem()] + [hbm()] * 6,
         out_specs=[vmem()] * 6,
         scratch_shapes=[
+            pltpu.VMEM(tile_cols.shape[::-1], jnp.int32),
+            pltpu.VMEM(tile_cols.shape[::-1], jnp.int32),
             pltpu.VMEM(hop_kinds.shape, F32),
-            pltpu.SemaphoreType.DMA((kind_count + 3,)),
+            pltpu.SemaphoreType.DMA((kind_count + 5,)),
         ],
         compiler_params=params(),
         cost_estimate=cost(1e7, 8e6),
         name="tables",
-    )(index, tile_cols.T, tile_kind_ids.T, hop_kinds, cheb_prev, probe, site_terms)
+    )(
+        index,
+        *[
+            stay(x)
+            for x in (tile_cols.T, tile_kind_ids.T, hop_kinds, cheb_prev, probe, site_terms)
+        ],
+    )
 
     partial_shape = jax.ShapeDtypeStruct((blocks, width), F32)
     current = [(cur_held, c * vecs) for c in range(chunks)]
     previous = [(prev_held, c * vecs) for c in range(chunks)]
+
+    def reduce(keep, give):
+        got = lax.ppermute(give, "vec", [(i, i ^ 1) for i in range(groups)])
+        piece = jax.ShapeDtypeStruct((keep.shape[0], quarter, width), F32)
+        mine, give = pl.pallas_call(
+            fold_kernel,
+            out_shape=[piece, piece],
+            in_specs=[smem(), vmem(), vmem()],
+            out_specs=[vmem(), vmem()],
+            compiler_params=params(),
+            cost_estimate=cost(1e5, 1e6),
+            name="fold",
+        )(index, keep, got)
+        return mine, lax.ppermute(give, "vec", [(i, i ^ 2) for i in range(groups)])
+
     partials = []
     buffers = []
+    reduced = []
     for s in range(STEPS):
         last = s == STEPS - 1
         partial = None
@@ -379,27 +448,26 @@
             args = [index, mix, high, low, pick, site_held]
             args += [current[c][0], previous[c][0], probe_held, *received[c]]
             specs = [smem()] + [vmem()] * (len(args) - 1)
-            older = len(partials) if last and c == chunks - 1 else 0
-            extra = ([] if partial is None else [partial]) + (partials if older else [])
+            fold = c == chunks - 1 and s >= STEPS - 2
+            older = len(partials) if fold else 0
+            extra = ([] if partial is None else [partial]) + (partials if fold else [])
             args += extra
             specs += [vmem()] * len(extra)
-            aliases = {len(args) + i: i for i in range(len(buffers))}
+            aliases = {len(args) + i: 2 + i for i in range(len(buffers))}
             args += buffers
             specs += [any_space()] * len(buffers)
             scratch = [
                 pltpu.VMEM((vecs, 2 * padded, width), BF16),
                 pltpu.VMEM((2 * vecs * blocks, kind_count * width), BF16),
             ]
+            outs, out_specs = [chunk_shape, partial_shape], [vmem(), vmem()]
             if last:
-                outs, out_specs = [full_shape, full_shape], [any_space(), any_space()]
-                scratch += [
-                    pltpu.VMEM((vecs, blocks, width), F32),
-                    pltpu.SemaphoreType.DMA((vecs + 1,)),
-                ]
+                outs.append(full_shape)
+                out_specs.append(any_space())
+                scratch.append(pltpu.SemaphoreType.DMA)
             else:
-                outs, out_specs = [chunk_shape, rows, rows], [vmem()] * 3
-            outs.append(partial_shape)
-            if older:
+                outs += [rows, rows]
+            if fold:
                 outs += [jax.ShapeDtypeStruct((older + 1, groups // 2, quarter, width), F32)] * 2
             out_specs += [vmem()] * (len(outs) - len(out_specs))
             cfg = (
@@ -410,66 +478,77 @@
                 last,
                 partial is not None,
                 older,
+                fold,
                 len(buffers),
             )
-            result = pl.pallas_call(
-                functools.partial(step_kernel, cfg),
-                out_shape=outs,
-                in_specs=specs,
-                out_specs=out_specs,
-                scratch_shapes=scratch,
-                input_output_aliases=aliases,
-                compiler_params=params(),
-                cost_estimate=cost(1.5e9, 5e6),
-                name=f"step{s}_{c}",
-            )(*args)
+            result = list(
+                pl.pallas_call(
+                    functools.partial(step_kernel, cfg),
+                    out_shape=outs,
+                    in_specs=specs,
+                    out_specs=out_specs,
+                    scratch_shapes=scratch,
+                    input_output_aliases=aliases,
+                    compiler_params=params(),
+                    cost_estimate=cost(1.5e9, 5e6),
+                )(*args)
+            )
+            previous[c], current[c] = current[c], (result.pop(0), 0)
+            partial = result.pop(0)
             if last:
-                buffers = list(result[:2])
-                partial = result[2]
-                rest = result[3:]
+                buffers = [result.pop(0)]
             else:
-                previous[c], current[c] = current[c], (result[0], 0)
-                received[c] = exchange(result[1], result[2])
-                partial = result[3]
+                received[c] = exchange(result.pop(0), result.pop(0))
+            if fold:
+                reduced.append(reduce(*result))
         partials.append(partial)
-
-    keep, give = rest
-    got = lax.ppermute(give, "vec", [(i, i ^ 1) for i in range(groups)])
-    piece = jax.ShapeDtypeStruct((STEPS, quarter, width), F32)
-    mine, give = pl.pallas_call(
-        fold_kernel,
-        out_shape=[piece, piece],
-        in_specs=[smem(), vmem(), vmem()],
-        out_specs=[vmem(), vmem()],
-        compiler_params=params(),
-        cost_estimate=cost(1e5, 1e6),
-        name="fold",
-    )(index, keep, got)
-    got = lax.ppermute(give, "vec", [(i, i ^ 2) for i in range(groups)])
+        if fold:
+            partials = []
 
     prior_count = prior_moments.shape[0]
     moment_count = prior_count + STEPS
     even_table, odd_table = jackson_split(moment_count, ENERGIES)
     group, lanes = 8, 128
-    small = pl.BlockSpec((STEPS, group, lanes), lambda i, h: (0, i, h))
-    new_moments, energy_map = pl.pallas_call(
-        functools.partial(energy_kernel, vec_dev * groups),
-        out_shape=[piece, jax.ShapeDtypeStruct((ENERGIES, quarter, width), F32)],
+
+    def small(count):
+        return pl.BlockSpec((count, group, lanes), lambda i, h: (0, i, h))
+
+    terms = [x for pair in reduced for x in pair]
+    new_moments, energy_map, next_cur = pl.pallas_call(
+        functools.partial(energy_kernel, vec_dev * groups, chunks),
+        out_shape=[
+            jax.ShapeDtypeStruct((STEPS, quarter, width), F32),
+            jax.ShapeDtypeStruct((ENERGIES, quarter, width), F32),
+            full_shape,
+        ],
         grid=(quarter // group, width // lanes),
         in_specs=[
             pl.BlockSpec(even_table.shape, lambda i, h: (0, 0)),
             pl.BlockSpec(odd_table.shape, lambda i, h: (0, 0)),
             pl.BlockSpec((prior_count, group, lanes), lambda i, h: (0, i, h)),
-            small,
-            small,
-        ],
-        out_specs=[small, pl.BlockSpec((ENERGIES, group, lanes), lambda i, h: (0, i, h))],
-        scratch_shapes=[pltpu.VMEM((moment_count * group, lanes), F32)],
+            *[small(x.shape[0]) for x in terms],
+            *[vmem()] * chunks,
+        ],
+        out_specs=[
+            small(STEPS),
+            pl.BlockSpec((ENERGIES, group, lanes), lambda i, h: (0, i, h)),
+            any_space(),
+        ],
+        scratch_shapes=[
+            pltpu.VMEM((moment_count * group, lanes), F32),
+            pltpu.SemaphoreType.DMA((chunks,)),
+        ],
         compiler_params=params(),
         cost_estimate=cost(4e9, 2.2e7),
         name="energy",
-    )(jnp.asarray(even_table), jnp.asarray(odd_table), prior_moments, mine, got)
-    return buffers[0], buffers[1], new_moments, energy_map
+    )(
+        jnp.asarray(even_table),
+        jnp.asarray(odd_table),
+        prior_moments,
+        *terms,
+        *[current[c][0] for c in range(chunks)],
+    )
+    return buffers[0], next_cur, new_moments, energy_map
 
 
 def solution(mesh):

time: 84.2 us -> 77.5 us (0.920)
  local copies, waits for them, and re-layouts: 7.7 us -> 0.02 us
  starting transfers between devices: 26.7 us -> 28.6 us
  waiting for transfers between devices: 7.17 us -> 6.11 us
    unnamed x22 -> x6, local copies, waits for them, and re-layouts: 7.7 us -> 0.02 us
    ppermute x2 -> x4, waiting for transfers between devices: 5.54 us -> 3.34 us  [the longest x2 3.33 us: reduce(): lax.ppermute(give, 'vec', [(i, i ^ 2) for i in range(groups)])]
    ppermute x8, starting transfers between devices: 19 us -> 20.9 us  [exchange(): got_b = lax.ppermute(b, 'dom', swap_b)]
    ppermute x8, waiting for transfers between devices: 1.61 us -> 2.75 us  [exchange(): got_b = lax.ppermute(b, 'dom', swap_b)]
    pallas_call x8, Pallas kernels: 27.5 us -> 26.6 us  [per_device(): pl.pallas_call(functools.partial(step_kernel, cfg), out_shape=outs, in_sp...]
    pallas_call x2 -> x3, Pallas kernels: 9.48 us -> 10.2 us  [the longest x1 9.07 us: per_device(): pl.pallas_call(functools.partial(energy_kernel, vec_dev * groups, chunks)...]
    ppermute x2 -> x4, starting transfers between devices: 1.65 us -> 2.31 us  [the longest x2 2.24 us: reduce(): lax.ppermute(give, 'vec', [(i, i ^ 2) for i in range(groups)])]
  transfers between devices with their start and end apart: 18 -> 20, of which waited for: 3 -> 2; matrix products, arithmetic and copies ran while one was open for 0% -> 0% of each run, Pallas kernels for 30% -> 39%
where the time goes in v2:
time: 77.5 us; the launch traced here: 77.4 us
  Pallas kernels  41.5 us (54%)
  starting transfers between devices  28.6 us (37%)
  waiting for transfers between devices  6.11 us (8%)
  between operations  1.01 us (1%)
    pallas_call x8, Pallas kernels, per_device(): pl.pallas_call(functools.partial(step_kernel, cfg), out_shape=outs, in_sp...  26.6 us
    ppermute x8, starting transfers between devices, exchange(): got_b = lax.ppermute(b, 'dom', swap_b)  20.9 us
    pallas_call x1, Pallas kernels, per_device(): pl.pallas_call(functools.partial(energy_kernel, vec_dev * groups, chunks)...  9.07 us
    ppermute x8, starting transfers between devices, exchange(): got_a = lax.ppermute(a, 'dom', swap_a)  5.45 us
    ppermute x2, waiting for transfers between devices, reduce(): lax.ppermute(give, 'vec', [(i, i ^ 2) for i in range(groups)])  3.33 us
    ppermute x8, waiting for transfers between devices, exchange(): got_b = lax.ppermute(b, 'dom', swap_b)  2.75 us
    pallas_call x1, Pallas kernels, per_device(): pl.pallas_call(functools.partial(prep_kernel, rim), out_shape=[jax.ShapeD...  2.56 us
    ppermute x2, starting transfers between devices, reduce(): lax.ppermute(give, 'vec', [(i, i ^ 2) for i in range(groups)])  2.24 us
  transfers between devices with their start and end apart: 20, of which 2 were waited for; matrix products, arithmetic and copies ran while one was open for 0% of the time, Pallas kernels for 39%

profile of v2, /device:TPU:0, one launch (start us, length us, event | category | flops | bytes accessed | tf_op | source)
XLA Modules:
  0.0 77.4 jit_solution(16386248204451560787)
XLA Ops:
  0.7 0.1 pad_add_fusion.index_ref
  0.7 2.2 %first_sends.1 = (bf16[96,256]{1,0:T(8,128)(2,1)S(1)}, f32[4,128,256]{2,1,0:T(8,128)S(1)}, f32[48,512]{1,0:T(8,128)S(1)}, f32[48,512]{1,0:T(8,128)S(1)}, f32[48,512]{1,0:T(8,128)S(1)}, /*index=5*/f32[48,512]{1,0:T(8,128)S(1)}) custom-call(s32[3]{0:T(128)S(1)} %pad_add_fusion.index_ref, s32[1,2,48]{2,1,0:T(2,128)} %lists_hbm.1, f32[4,128,256]{2,1,0:T(8,128)} %cur_hbm.1), custom_call_target="tpu_custom_call" | custom-call | flops 100000000 | bytes 1000000 | tf_op jit(solution)/shard_map/first_sends/pallas_call | solution.py:371
  2.9 3.0 %collective-permute-start.2 = (f32[48,512]{1,0:T(8,128)S(1)}, f32[48,512]{1,0:T(8,128)S(1)}, u32[]{:S(2)}, u32[]{:S(2)}) collective-permute-start(f32[48,512]{1,0:T(8,128)S(1)} %get-tuple-element.65), channel_id=1, source_target_pairs={{0,1},{1,0},{2,3},{3,2},{4,5},{5,4},{6,7},{7,6},{8,9},{9,8},{10,11... | collective-permute-start | bytes 294920 | tf_op jit(solution)/shard_map/ppermute | solution.py:389
  6.0 3.6 %collective-permute-start.3 = (f32[48,512]{1,0:T(8,128)S(1)}, f32[48,512]{1,0:T(8,128)S(1)}, u32[]{:S(2)}, u32[]{:S(2)}) collective-permute-start(f32[48,512]{1,0:T(8,128)S(1)} %get-tuple-element.66), channel_id=1, source_target_pairs={{0,7},{1,2},{2,1},{3,4},{4,3},{5,6},{6,5},{7,0},{8,15},{9,10},{10,... | collective-permute-start | bytes 294920 | tf_op jit(solution)/shard_map/ppermute | solution.py:388
  9.6 1.9 %collective-permute-start.1 = (f32[48,512]{1,0:T(8,128)S(1)}, f32[48,512]{1,0:T(8,128)S(1)}, u32[]{:S(2)}, u32[]{:S(2)}) collective-permute-start(f32[48,512]{1,0:T(8,128)S(1)} %get-tuple-element.64), channel_id=1, source_target_pairs={{0,7},{1,2},{2,1},{3,4},{4,3},{5,6},{6,5},{7,0},{8,15},{9,10},{10,... | collective-permute-start | bytes 294920 | tf_op jit(solution)/shard_map/ppermute | solution.py:388
  11.5 2.6 %tables.1 = (bf16[1024,512]{1,0:T(8,128)(2,1)S(1)}, bf16[2048,256]{1,0:T(8,128)(2,1)S(1)}, bf16[2048,256]{1,0:T(8,128)(2,1)S(1)}, f32[4,128,256]{2,1,0:T(8,128)S...) custom-call(s32[3]{0:T(128)S(1)} %pad_add_fusion.index_ref, s32[4,128]{1,0:T(4,128)} %bitcast.5, ...), custom_call_target="tpu_custom_call" | custom-call | flops 10000000 | bytes 8000000 | tf_op jit(solution)/shard_map/tables/pallas_call | solution.py:394
  14.1 3.2 %shard_map.138 = (f32[2,128,256]{2,1,0:T(8,128)S(1)}, f32[128,256]{1,0:T(8,128)S(1)}, f32[48,512]{1,0:T(8,128)S(1)}, f32[48,512]{1,0:T(8,128)S(1)}) custom-call(s32[3]{0:T(128)S(1)} %pad_add_fusion.index_ref, bf16[1024,512]{1,0:T(8,128)(2,1)S(1)} %get-tuple-element.55.mix_ref, bf16[2048,256]{1,0:T(8,128)(2,1)S(1)} %get-tuple-element.56.high_ref, ...), custom_call_target="tpu_custom_call" | custom-call | flops 1500000000 | bytes 5000000 | tf_op jit(solution)/shard_map/pallas_call | solution.py:485
  17.2 0.7 collective-permute-start.6
  17.9 4.6 %collective-permute-start.7 = (f32[48,512]{1,0:T(8,128)S(1)}, f32[48,512]{1,0:T(8,128)S(1)}, u32[]{:S(2)}, u32[]{:S(2)}) collective-permute-start(f32[48,512]{1,0:T(8,128)S(1)} %get-tuple-element.73), channel_id=1, source_target_pairs={{0,7},{1,2},{2,1},{3,4},{4,3},{5,6},{6,5},{7,0},{8,15},{9,10},{10,... | collective-permute-start | bytes 294920 | tf_op jit(solution)/shard_map/ppermute | solution.py:388
  22.5 3.2 %shard_map.139 = (f32[2,128,256]{2,1,0:T(8,128)S(1)}, f32[128,256]{1,0:T(8,128)S(1)}, f32[48,512]{1,0:T(8,128)S(1)}, f32[48,512]{1,0:T(8,128)S(1)}) custom-call(s32[3]{0:T(128)S(1)} %pad_add_fusion.index_ref, bf16[1024,512]{1,0:T(8,128)(2,1)S(1)} %get-tuple-element.55.mix_ref, bf16[2048,256]{1,0:T(8,128)(2,1)S(1)} %get-tuple-element.56.high_ref, ...), custom_call_target="tpu_custom_call" | custom-call | flops 1500000000 | bytes 5000000 | tf_op jit(solution)/shard_map/pallas_call | solution.py:485
  25.7 0.1 collective-permute-start.4
  25.8 1.4 %collective-permute-start.5 = (f32[48,512]{1,0:T(8,128)S(1)}, f32[48,512]{1,0:T(8,128)S(1)}, u32[]{:S(2)}, u32[]{:S(2)}) collective-permute-start(f32[48,512]{1,0:T(8,128)S(1)} %get-tuple-element.70), channel_id=1, source_target_pairs={{0,7},{1,2},{2,1},{3,4},{4,3},{5,6},{6,5},{7,0},{8,15},{9,10},{10,... | collective-permute-start | bytes 294920 | tf_op jit(solution)/shard_map/ppermute | solution.py:388
  27.1 3.2 %shard_map.140 = (f32[2,128,256]{2,1,0:T(8,128)S(1)}, f32[128,256]{1,0:T(8,128)S(1)}, f32[48,512]{1,0:T(8,128)S(1)}, f32[48,512]{1,0:T(8,128)S(1)}) custom-call(s32[3]{0:T(128)S(1)} %pad_add_fusion.index_ref, bf16[1024,512]{1,0:T(8,128)(2,1)S(1)} %get-tuple-element.55.mix_ref, bf16[2048,256]{1,0:T(8,128)(2,1)S(1)} %get-tuple-element.56.high_ref, ...), custom_call_target="tpu_custom_call" | custom-call | flops 1500000000 | bytes 5000000 | tf_op jit(solution)/shard_map/pallas_call | solution.py:485
  30.3 1.1 %collective-permute-start.10 = (f32[48,512]{1,0:T(8,128)S(1)}, f32[48,512]{1,0:T(8,128)S(1)}, u32[]{:S(2)}, u32[]{:S(2)}) collective-permute-start(f32[48,512]{1,0:T(8,128)S(1)} %get-tuple-element.79), channel_id=1, source_target_pairs={{0,1},{1,0},{2,3},{3,2},{4,5},{5,4},{6,7},{7,6},{8,9},{9,8},{10,11... | collective-permute-start | bytes 294920 | tf_op jit(solution)/shard_map/ppermute | solution.py:389
  31.4 2.4 %collective-permute-start.11 = (f32[48,512]{1,0:T(8,128)S(1)}, f32[48,512]{1,0:T(8,128)S(1)}, u32[]{:S(2)}, u32[]{:S(2)}) collective-permute-start(f32[48,512]{1,0:T(8,128)S(1)} %get-tuple-element.80), channel_id=1, source_target_pairs={{0,7},{1,2},{2,1},{3,4},{4,3},{5,6},{6,5},{7,0},{8,15},{9,10},{10,... | collective-permute-start | bytes 294920 | tf_op jit(solution)/shard_map/ppermute | solution.py:388
  33.9 3.2 %shard_map.141 = (f32[2,128,256]{2,1,0:T(8,128)S(1)}, f32[128,256]{1,0:T(8,128)S(1)}, f32[48,512]{1,0:T(8,128)S(1)}, f32[48,512]{1,0:T(8,128)S(1)}) custom-call(s32[3]{0:T(128)S(1)} %pad_add_fusion.index_ref, bf16[1024,512]{1,0:T(8,128)(2,1)S(1)} %get-tuple-element.55.mix_ref, bf16[2048,256]{1,0:T(8,128)(2,1)S(1)} %get-tuple-element.56.high_ref, ...), custom_call_target="tpu_custom_call" | custom-call | flops 1500000000 | bytes 5000000 | tf_op jit(solution)/shard_map/pallas_call | solution.py:485
  37.1 0.4 collective-permute-start.8
  37.5 2.0 %collective-permute-start.9 = (f32[48,512]{1,0:T(8,128)S(1)}, f32[48,512]{1,0:T(8,128)S(1)}, u32[]{:S(2)}, u32[]{:S(2)}) collective-permute-start(f32[48,512]{1,0:T(8,128)S(1)} %get-tuple-element.77), channel_id=1, source_target_pairs={{0,7},{1,2},{2,1},{3,4},{4,3},{5,6},{6,5},{7,0},{8,15},{9,10},{10,... | collective-permute-start | bytes 294920 | tf_op jit(solution)/shard_map/ppermute | solution.py:388
  39.5 3.2 %shard_map.142 = (f32[2,128,256]{2,1,0:T(8,128)S(1)}, f32[128,256]{1,0:T(8,128)S(1)}, f32[48,512]{1,0:T(8,128)S(1)}, f32[48,512]{1,0:T(8,128)S(1)}) custom-call(s32[3]{0:T(128)S(1)} %pad_add_fusion.index_ref, bf16[1024,512]{1,0:T(8,128)(2,1)S(1)} %get-tuple-element.55.mix_ref, bf16[2048,256]{1,0:T(8,128)(2,1)S(1)} %get-tuple-element.56.high_ref, ...), custom_call_target="tpu_custom_call" | custom-call | flops 1500000000 | bytes 5000000 | tf_op jit(solution)/shard_map/pallas_call | solution.py:485
  42.8 3.5 %collective-permute-start.15 = (f32[48,512]{1,0:T(8,128)S(1)}, f32[48,512]{1,0:T(8,128)S(1)}, u32[]{:S(2)}, u32[]{:S(2)}) collective-permute-start(f32[48,512]{1,0:T(8,128)S(1)} %get-tuple-element.89), channel_id=1, source_target_pairs={{0,7},{1,2},{2,1},{3,4},{4,3},{5,6},{6,5},{7,0},{8,15},{9,10},{10,... | collective-permute-start | bytes 294920 | tf_op jit(solution)/shard_map/ppermute | solution.py:388
  46.3 3.9 %shard_map.143 = (f32[2,128,256]{2,1,0:T(8,128)S(1)}, f32[128,256]{1,0:T(8,128)}, f32[48,512]{1,0:T(8,128)S(1)}, f32[48,512]{1,0:T(8,128)S(1)}, f32[3,2,32,256]{...) custom-call(s32[3]{0:T(128)S(1)} %pad_add_fusion.index_ref, bf16[1024,512]{1,0:T(8,128)(2,1)S(1)} %get-tuple-element.55.mix_ref, ...), custom_call_target="tpu_custom_call" | custom-call | flops 1500000000 | bytes 5000000 | tf_op jit(solution)/shard_map/pallas_call | solution.py:485
  50.2 0.1 collective-permute-start.12
  50.3 1.5 %collective-permute-start.13 = (f32[48,512]{1,0:T(8,128)S(1)}, f32[48,512]{1,0:T(8,128)S(1)}, u32[]{:S(2)}, u32[]{:S(2)}) collective-permute-start(f32[48,512]{1,0:T(8,128)S(1)} %get-tuple-element.86), channel_id=1, source_target_pairs={{0,7},{1,2},{2,1},{3,4},{4,3},{5,6},{6,5},{7,0},{8,15},{9,10},{10,... | collective-permute-start | bytes 294920 | tf_op jit(solution)/shard_map/ppermute | solution.py:388
  51.8 3.0 %shard_map.144 = (f32[2,128,256]{2,1,0:T(8,128)S(1)}, f32[128,256]{1,0:T(8,128)S(1)}, f32[4,128,256]{2,1,0:T(8,128)}) custom-call(s32[3]{0:T(128)S(1)} %pad_add_fusion.index_ref, bf16[1024,512]{1,0:T(8,128)(2,1)S(1)} %get-tuple-element.55.mix_ref, bf16[2048,256]{1,0:T(8,128)(2,1)S(1)} %get-tuple-element.56.high_ref, ...), custom_call_target="tpu_custom_call" | custom-call | flops 1500000000 | bytes 5000000 | tf_op jit(solution)/shard_map/pallas_call | solution.py:485
  54.9 2.7 %collective-permute-done.13.recv_b = f32[48,512]{1,0:T(8,128)S(1)} collective-permute-done((f32[48,512]{1,0:T(8,128)S(1)}, f32[48,512]{1,0:T(8,128)S(1)}, u32[]{:S(2)}, u32[]{:S(2)}) %collective-permute-start.13) | collective-permute-done | bytes 98336 | tf_op jit(solution)/shard_map/ppermute | solution.py:388
  57.6 3.7 %shard_map.145 = (f32[2,128,256]{2,1,0:T(8,128)S(1)}, f32[128,256]{1,0:T(8,128)}, f32[4,128,256]{2,1,0:T(8,128)}, f32[1,2,32,256]{3,2,1,0:T(8,128)S(1)}, f32[1,2,32,256]{3,2,1,0:T(8,128)S(1)}) custom-call(s32[3]{0:T(128)S(1)} %pad_add_fusion.index_ref, bf16[1024,512]{1,0:T(8,128)(2,1)S(1)} %get-tuple-element.55.mix_ref, ...), custom_call_target="tpu_custom_call", output_to_operand_aliasing={{2}: (12, {})} | custom-call | flops 1500000000 | bytes 5000000 | tf_op jit(solution)/shard_map/pallas_call | solution.py:485
  61.4 0.6 fold.2
  62.0 1.6 %collective-permute-start.17 = (f32[3,32,256]{2,1,0:T(8,128)S(1)}, f32[3,32,256]{2,1,0:T(8,128)S(1)}, u32[]{:S(2)}, u32[]{:S(2)}) collective-permute-start(f32[3,32,256]{2,1,0:T(8,128)S(1)} %get-tuple-element.96), channel_id=1, source_target_pairs={{0,16},{8,24},{16,0},{24,8},{1,17},{9,25},{17,1},{25,9},{2,18},{10... | collective-permute-start | bytes 294920 | tf_op jit(solution)/shard_map/ppermute | solution.py:439
  63.6 0.6 fold.3
  64.1 0.7 collective-permute-start.19
  64.8 3.3 %collective-permute-done.19.late_got = f32[1,32,256]{2,1,0:T(8,128)S(1)} collective-permute-done((f32[1,32,256]{2,1,0:T(8,128)S(1)}, f32[1,32,256]{2,1,0:T(8,128)S(1)}, u32[]{:S(2)}, u32[]{:S(2)}) %collective-permute-start.19) | collective-permute-done | bytes 32800 | tf_op jit(solution)/shard_map/ppermute | solution.py:439
  68.1 9.1 %energy.1 = (f32[4,32,256]{2,1,0:T(8,128)}, f32[512,32,256]{2,1,0:T(8,128)}, f32[4,128,256]{2,1,0:T(8,128)}) custom-call(bf16[256,256]{1,0:T(8,128)(2,1)S(1)} %copy-done.2, bf16[256,256]{1,0:T(8,128)(2,1)S(1)} %copy-done.1, f32[124,32,256]{2,1,0:T(8,128)S(1)} %copy-done, f32[3,32,256]{2,1,0:T(8,128)S(1)} %get-tuple-element.95.early_mine, ...), custom_call_target="tpu_custom_call" | custom-call | flops 4000000000 | bytes 22000000 | tf_op jit(solution)/shard_map/energy/pallas_call | solution.py:517
  (28 shorter events, 0.2 us)
Async XLA Ops:
  2.9 11.1 %collective-permute-start.2 = (f32[48,512]{1,0:T(8,128)S(1)}, f32[48,512]{1,0:T(8,128)S(1)}, u32[]{:S(2)}, u32[]{:S(2)}) collective-permute-start(f32[48,512]{1,0:T(8,128)S(1)} %get-tuple-element.65), channel_id=1, source_target_pairs={{0,1},{1,0},{2,3},{3,2},{4,5},{5,4},{6,7},{7,6},{8,9},{9,8},{10,11... | collective-permute-start | bytes 294920 | tf_op jit(solution)/shard_map/ppermute | solution.py:389
  6.0 8.1 %collective-permute-start.3 = (f32[48,512]{1,0:T(8,128)S(1)}, f32[48,512]{1,0:T(8,128)S(1)}, u32[]{:S(2)}, u32[]{:S(2)}) collective-permute-start(f32[48,512]{1,0:T(8,128)S(1)} %get-tuple-element.66), channel_id=1, source_target_pairs={{0,7},{1,2},{2,1},{3,4},{4,3},{5,6},{6,5},{7,0},{8,15},{9,10},{10,... | collective-permute-start | bytes 294920 | tf_op jit(solution)/shard_map/ppermute | solution.py:388
  9.6 12.9 %collective-permute-start = (f32[48,512]{1,0:T(8,128)S(1)}, f32[48,512]{1,0:T(8,128)S(1)}, u32[]{:S(2)}, u32[]{:S(2)}) collective-permute-start(f32[48,512]{1,0:T(8,128)S(1)} %get-tuple-element.63), channel_id=1, source_target_pairs={{0,1},{1,0},{2,3},{3,2},{4,5},{5,4},{6,7},{7,6},{8,9},{9,8},{10,11... | collective-permute-start | bytes 294920 | tf_op jit(solution)/shard_map/ppermute | solution.py:389
  9.6 12.9 %collective-permute-start.1 = (f32[48,512]{1,0:T(8,128)S(1)}, f32[48,512]{1,0:T(8,128)S(1)}, u32[]{:S(2)}, u32[]{:S(2)}) collective-permute-start(f32[48,512]{1,0:T(8,128)S(1)} %get-tuple-element.64), channel_id=1, source_target_pairs={{0,7},{1,2},{2,1},{3,4},{4,3},{5,6},{6,5},{7,0},{8,15},{9,10},{10,... | collective-permute-start | bytes 294920 | tf_op jit(solution)/shard_map/ppermute | solution.py:388
  17.2 9.9 %collective-permute-start.6 = (f32[48,512]{1,0:T(8,128)S(1)}, f32[48,512]{1,0:T(8,128)S(1)}, u32[]{:S(2)}, u32[]{:S(2)}) collective-permute-start(f32[48,512]{1,0:T(8,128)S(1)} %get-tuple-element.72), channel_id=1, source_target_pairs={{0,1},{1,0},{2,3},{3,2},{4,5},{5,4},{6,7},{7,6},{8,9},{9,8},{10,11... | collective-permute-start | bytes 294920 | tf_op jit(solution)/shard_map/ppermute | solution.py:389
  17.9 9.2 %collective-permute-start.7 = (f32[48,512]{1,0:T(8,128)S(1)}, f32[48,512]{1,0:T(8,128)S(1)}, u32[]{:S(2)}, u32[]{:S(2)}) collective-permute-start(f32[48,512]{1,0:T(8,128)S(1)} %get-tuple-element.73), channel_id=1, source_target_pairs={{0,7},{1,2},{2,1},{3,4},{4,3},{5,6},{6,5},{7,0},{8,15},{9,10},{10,... | collective-permute-start | bytes 294920 | tf_op jit(solution)/shard_map/ppermute | solution.py:388
  25.7 8.2 %collective-permute-start.4 = (f32[48,512]{1,0:T(8,128)S(1)}, f32[48,512]{1,0:T(8,128)S(1)}, u32[]{:S(2)}, u32[]{:S(2)}) collective-permute-start(f32[48,512]{1,0:T(8,128)S(1)} %get-tuple-element.69), channel_id=1, source_target_pairs={{0,1},{1,0},{2,3},{3,2},{4,5},{5,4},{6,7},{7,6},{8,9},{9,8},{10,11... | collective-permute-start | bytes 294920 | tf_op jit(solution)/shard_map/ppermute | solution.py:389
  25.8 8.1 %collective-permute-start.5 = (f32[48,512]{1,0:T(8,128)S(1)}, f32[48,512]{1,0:T(8,128)S(1)}, u32[]{:S(2)}, u32[]{:S(2)}) collective-permute-start(f32[48,512]{1,0:T(8,128)S(1)} %get-tuple-element.70), channel_id=1, source_target_pairs={{0,7},{1,2},{2,1},{3,4},{4,3},{5,6},{6,5},{7,0},{8,15},{9,10},{10,... | collective-permute-start | bytes 294920 | tf_op jit(solution)/shard_map/ppermute | solution.py:388
  30.3 9.2 %collective-permute-start.10 = (f32[48,512]{1,0:T(8,128)S(1)}, f32[48,512]{1,0:T(8,128)S(1)}, u32[]{:S(2)}, u32[]{:S(2)}) collective-permute-start(f32[48,512]{1,0:T(8,128)S(1)} %get-tuple-element.79), channel_id=1, source_target_pairs={{0,1},{1,0},{2,3},{3,2},{4,5},{5,4},{6,7},{7,6},{8,9},{9,8},{10,11... | collective-permute-start | bytes 294920 | tf_op jit(solution)/shard_map/ppermute | solution.py:389
  31.4 8.1 %collective-permute-start.11 = (f32[48,512]{1,0:T(8,128)S(1)}, f32[48,512]{1,0:T(8,128)S(1)}, u32[]{:S(2)}, u32[]{:S(2)}) collective-permute-start(f32[48,512]{1,0:T(8,128)S(1)} %get-tuple-element.80), channel_id=1, source_target_pairs={{0,7},{1,2},{2,1},{3,4},{4,3},{5,6},{6,5},{7,0},{8,15},{9,10},{10,... | collective-permute-start | bytes 294920 | tf_op jit(solution)/shard_map/ppermute | solution.py:388
  37.1 9.3 %collective-permute-start.8 = (f32[48,512]{1,0:T(8,128)S(1)}, f32[48,512]{1,0:T(8,128)S(1)}, u32[]{:S(2)}, u32[]{:S(2)}) collective-permute-start(f32[48,512]{1,0:T(8,128)S(1)} %get-tuple-element.76), channel_id=1, source_target_pairs={{0,1},{1,0},{2,3},{3,2},{4,5},{5,4},{6,7},{7,6},{8,9},{9,8},{10,11... | collective-permute-start | bytes 294920 | tf_op jit(solution)/shard_map/ppermute | solution.py:389
  37.5 8.8 %collective-permute-start.9 = (f32[48,512]{1,0:T(8,128)S(1)}, f32[48,512]{1,0:T(8,128)S(1)}, u32[]{:S(2)}, u32[]{:S(2)}) collective-permute-start(f32[48,512]{1,0:T(8,128)S(1)} %get-tuple-element.77), channel_id=1, source_target_pairs={{0,7},{1,2},{2,1},{3,4},{4,3},{5,6},{6,5},{7,0},{8,15},{9,10},{10,... | collective-permute-start | bytes 294920 | tf_op jit(solution)/shard_map/ppermute | solution.py:388
  42.7 9.1 %collective-permute-start.14 = (f32[48,512]{1,0:T(8,128)S(1)}, f32[48,512]{1,0:T(8,128)S(1)}, u32[]{:S(2)}, u32[]{:S(2)}) collective-permute-start(f32[48,512]{1,0:T(8,128)S(1)} %get-tuple-element.88), channel_id=1, source_target_pairs={{0,1},{1,0},{2,3},{3,2},{4,5},{5,4},{6,7},{7,6},{8,9},{9,8},{10,11... | collective-permute-start | bytes 294920 | tf_op jit(solution)/shard_map/ppermute | solution.py:389
  42.8 9.0 %collective-permute-start.15 = (f32[48,512]{1,0:T(8,128)S(1)}, f32[48,512]{1,0:T(8,128)S(1)}, u32[]{:S(2)}, u32[]{:S(2)}) collective-permute-start(f32[48,512]{1,0:T(8,128)S(1)} %get-tuple-element.89), channel_id=1, source_target_pairs={{0,7},{1,2},{2,1},{3,4},{4,3},{5,6},{6,5},{7,0},{8,15},{9,10},{10,... | collective-permute-start | bytes 294920 | tf_op jit(solution)/shard_map/ppermute | solution.py:388
  50.2 4.7 %collective-permute-start.12 = (f32[48,512]{1,0:T(8,128)S(1)}, f32[48,512]{1,0:T(8,128)S(1)}, u32[]{:S(2)}, u32[]{:S(2)}) collective-permute-start(f32[48,512]{1,0:T(8,128)S(1)} %get-tuple-element.85), channel_id=1, source_target_pairs={{0,1},{1,0},{2,3},{3,2},{4,5},{5,4},{6,7},{7,6},{8,9},{9,8},{10,11... | collective-permute-start | bytes 294920 | tf_op jit(solution)/shard_map/ppermute | solution.py:389
  50.3 7.3 %collective-permute-start.13 = (f32[48,512]{1,0:T(8,128)S(1)}, f32[48,512]{1,0:T(8,128)S(1)}, u32[]{:S(2)}, u32[]{:S(2)}) collective-permute-start(f32[48,512]{1,0:T(8,128)S(1)} %get-tuple-element.86), channel_id=1, source_target_pairs={{0,7},{1,2},{2,1},{3,4},{4,3},{5,6},{6,5},{7,0},{8,15},{9,10},{10,... | collective-permute-start | bytes 294920 | tf_op jit(solution)/shard_map/ppermute | solution.py:388
  51.8 9.6 %collective-permute-start.16 = (f32[3,2,32,256]{3,2,1,0:T(8,128)S(1)}, f32[3,2,32,256]{3,2,1,0:T(8,128)S(1)}, u32[]{:S(2)}, u32[]{:S(2)}) collective-permute-start(f32[3,2,32,256]{3,2,1,0:T(8,128)S(1)} %get-tuple-element.94), channel_id=1, source_target_pairs={{0,8},{8,0},{16,24},{24,16},{1,9},{9,1},{17,25},{25,17},{2,10},{10... | collective-permute-start | bytes 589832 | tf_op jit(solution)/shard_map/ppermute | solution.py:428
  54.8 13.3 %copy-start = (f32[124,32,256]{2,1,0:T(8,128)S(1)}, f32[124,32,256]{2,1,0:T(8,128)}, u32[]{:S(2)}) copy-start(f32[124,32,256]{2,1,0:T(8,128)} %prior_ref.1) | copy-start | bytes 12189700
  54.8 13.3 %copy-start.1 = (bf16[256,256]{1,0:T(8,128)(2,1)S(1)}, bf16[256,256]{1,0:T(8,128)(2,1)}, u32[]{:S(2)}) copy-start(bf16[256,256]{1,0:T(8,128)(2,1)} %constant.41.clone.odd_ref) | copy-start | bytes 393220
  54.9 13.3 %copy-start.2 = (bf16[256,256]{1,0:T(8,128)(2,1)S(1)}, bf16[256,256]{1,0:T(8,128)(2,1)}, u32[]{:S(2)}) copy-start(bf16[256,256]{1,0:T(8,128)(2,1)} %constant.40.clone.even_ref) | copy-start | bytes 393220
  61.3 2.3 %collective-permute-start.18 = (f32[1,2,32,256]{3,2,1,0:T(8,128)S(1)}, f32[1,2,32,256]{3,2,1,0:T(8,128)S(1)}, u32[]{:S(2)}, u32[]{:S(2)}) collective-permute-start(f32[1,2,32,256]{3,2,1,0:T(8,128)S(1)} %get-tuple-element.98), channel_id=1, source_target_pairs={{0,8},{8,0},{16,24},{24,16},{1,9},{9,1},{17,25},{25,17},{2,10},{10... | collective-permute-start | bytes 196616 | tf_op jit(solution)/shard_map/ppermute | solution.py:428
  62.0 6.1 %collective-permute-start.17 = (f32[3,32,256]{2,1,0:T(8,128)S(1)}, f32[3,32,256]{2,1,0:T(8,128)S(1)}, u32[]{:S(2)}, u32[]{:S(2)}) collective-permute-start(f32[3,32,256]{2,1,0:T(8,128)S(1)} %get-tuple-element.96), channel_id=1, source_target_pairs={{0,16},{8,24},{16,0},{24,8},{1,17},{9,25},{17,1},{25,9},{2,18},{10... | collective-permute-start | bytes 294920 | tf_op jit(solution)/shard_map/ppermute | solution.py:439
  64.1 4.0 %collective-permute-start.19 = (f32[1,32,256]{2,1,0:T(8,128)S(1)}, f32[1,32,256]{2,1,0:T(8,128)S(1)}, u32[]{:S(2)}, u32[]{:S(2)}) collective-permute-start(f32[1,32,256]{2,1,0:T(8,128)S(1)} %get-tuple-element.100), channel_id=1, source_target_pairs={{0,16},{8,24},{16,0},{24,8},{1,17},{9,25},{17,1},{25,9},{2,18},{10... | collective-permute-start | bytes 98312 | tf_op jit(solution)/shard_map/ppermute | solution.py:439

commit v3 on v2

--- a/solution.py
+++ b/solution.py
@@ -193,10 +193,11 @@
     recv_b,
     *rest,
 ):
-    vecs, cur_at, prev_at, own_at, last, add_partial, older, fold, aliased = cfg
+    vecs, cur_at, prev_at, own_at, last, add_partial, older, fold, fetch, aliased = cfg
     rest = list(rest)
     partial_in = rest.pop(0) if add_partial else None
     olders = [rest.pop(0) for _ in range(older)]
+    prior_hbm = rest.pop(0) if fetch else None
     rest = rest[aliased:]
     out_ref, partial_out = rest[:2]
     rest = rest[2:]
@@ -204,19 +205,41 @@
         prev_out = rest.pop(0)
     else:
         send_a, send_b = rest.pop(0), rest.pop(0)
-    if fold:
+    if fold and last:
+        pieces_out = [rest.pop(0) for _ in range(4)]
+    elif fold:
         keep_ref, give_ref = rest.pop(0), rest.pop(0)
+    if fetch:
+        prior_ref = rest.pop(0)
     source, mixed = rest[:2]
     blocks, width = cur_ref.shape[1:]
     rim = recv_a.shape[0]
     padded = source.shape[1] // 2
     kind_count = mix_ref.shape[0] // blocks
     spin = width // 2
+    copies = []
     if last:
-        copy = pltpu.make_async_copy(
-            cur_ref.at[pl.ds(cur_at, vecs)], prev_out.at[pl.ds(own_at, vecs)], rest[2]
-        )
+        copies = [
+            pltpu.make_async_copy(
+                cur_ref.at[pl.ds(cur_at, vecs)], prev_out.at[pl.ds(own_at, vecs)], rest[2]
+            )
+        ]
+    if fetch:
+        count, halves, moments, group, lanes = prior_ref.shape
+        known = prior_hbm.shape[0]
+        copies = [
+            pltpu.make_async_copy(
+                prior_hbm.at[:, pl.ds(i * group, group), pl.ds(h * lanes, lanes)],
+                prior_ref.at[i, h, pl.ds(0, known)],
+                rest[2].at[i * halves + h],
+            )
+            for i in range(count)
+            for h in range(halves)
+        ]
+    for copy in copies:
         copy.start()
+    if fetch:
+        prior_ref[:, :, known:] = jnp.zeros((count, halves, moments - known, group, lanes), F32)
     for v in range(vecs):
         columns = slice(v * width, (v + 1) * width)
         pieces = [cur_ref[cur_at + v], recv_a[:, columns], recv_b[:, columns]]
@@ -257,7 +280,14 @@
             send_a[:, v * width : (v + 1) * width] = got[:rim]
             send_b[:, v * width : (v + 1) * width] = got[rim:]
     partial_out[...] = partial
-    if fold:
+    if fold and last:
+        quarter = pieces_out[0].shape[0]
+        for flip, piece in enumerate(pieces_out):
+            core = index_ref[1] if flip % 2 == 0 else 1 - index_ref[1]
+            chip = index_ref[2] if flip < 2 else 1 - index_ref[2]
+            at = pl.multiple_of((2 * chip + core) * quarter, quarter)
+            piece[...] = partial_out[pl.ds(at, quarter)]
+    elif fold:
         cores = 2
         quarter = keep_ref.shape[2]
         core = index_ref[1]
@@ -269,7 +299,7 @@
                 give_ref[s, y] = ref[
                     pl.ds(pl.multiple_of(base + (1 - core) * quarter, quarter), quarter)
                 ]
-    if last:
+    for copy in copies:
         copy.wait()
 
 
@@ -279,65 +309,68 @@
     give_ref[...] = keep_ref[:, 1 - y] + got_ref[:, 1 - y]
 
 
-def energy_kernel(
-    vector_total,
-    chunks,
-    even_ref,
-    odd_ref,
-    prior_ref,
-    early_mine,
-    early_got,
-    late_mine,
-    late_got,
-    *rest,
-):
-    finals = rest[:chunks]
-    new_ref, map_ref, cur_out, moments, sems = rest[chunks:]
+def energy_kernel(vector_total, chunks, even_ref, odd_ref, prior_ref, early_mine, early_got, *rest):
+    lates, finals = rest[:4], rest[4 : 4 + chunks]
+    new_ref, map_out, cur_out, fresh, held, sems = rest[4 + chunks :]
+    count, halves, moments, group, lanes = prior_ref.shape
     vecs = finals[0].shape[0]
     copies = [
-        pltpu.make_async_copy(finals[c], cur_out.at[pl.ds(c * vecs, vecs)], sems.at[c])
+        pltpu.make_async_copy(
+            finals[c], cur_out.at[pl.ds(c * vecs, vecs)], sems.at[count * halves + c]
+        )
         for c in range(chunks)
     ]
-    step = pl.program_id(0) * pl.num_programs(1) + pl.program_id(1)
-
-    @pl.when(step == 0)
-    def _():
-        for copy in copies:
+    for copy in copies:
+        copy.start()
+    early = early_mine.shape[0]
+    steps = new_ref.shape[0]
+    scale = 1.0 / vector_total
+    new_ref[0:early] = (early_mine[...] + early_got[...]) * scale
+    new_ref[early] = ((lates[0][...] + lates[1][...]) + (lates[2][...] + lates[3][...])) * scale
+    half = even_ref.shape[0]
+    pairs = moments // 2
+    flip = 7 - lax.broadcasted_iota(jnp.int32, (8, lanes), 0)
+    for i in range(count):
+        for h in range(halves):
+            slot = i * halves + h
+            rows = slice(i * group, (i + 1) * group)
+            columns = slice(h * lanes, (h + 1) * lanes)
+            old = prior_ref.at[i, h].reshape(moments * group, lanes)
+            tail = (8 * 2 - steps) * group
+            fresh[slot, 0:tail] = jnp.zeros((tail, lanes), F32)
+            fresh[slot, tail:] = new_ref[:, rows, columns].reshape(steps * group, lanes)
+            flat = held.at[slot].reshape(2 * half * group, lanes)
+            for b in range(0, group, 2):
+                sums = []
+                for parity, table in ((0, even_ref), (1, odd_ref)):
+                    pair = []
+                    for j in range(2):
+                        start = parity * group + b + j
+                        value = old[pl.ds(start, pairs, stride=2 * group)]
+                        added = fresh[slot, pl.ds(start, 8, stride=2 * group)]
+                        pair.append(
+                            jnp.concatenate([value[: pairs - 8], value[pairs - 8 :] + added], axis=0)
+                        )
+                    high, low = split(jnp.concatenate(pair, axis=1))
+                    sums.append(dot(table[...], jnp.concatenate([high, high, low, low], axis=0)))
+                plus = sums[0] + sums[1]
+                minus = sums[0] - sums[1]
+                for j in range(2):
+                    side = slice(j * lanes, (j + 1) * lanes)
+                    flat[pl.ds(b + j, half, stride=group)] = plus[:, side]
+                    for r in range(0, half, 8):
+                        turned = jnp.take_along_axis(minus[r : r + 8, side], flip, axis=0)
+                        top = 2 * half - 8 - r
+                        flat[pl.ds(top * group + b + j, 8, stride=group)] = turned
+            copy = pltpu.make_async_copy(
+                held.at[slot],
+                map_out.at[:, pl.ds(i * group, group), pl.ds(h * lanes, lanes)],
+                sems.at[slot],
+            )
             copy.start()
-
-    prior_count, group, lanes = prior_ref.shape
-    early, late = early_mine.shape[0], late_mine.shape[0]
-    steps = early + late
-    half = even_ref.shape[0]
-    pairs = (prior_count + steps) // 2
-    new_ref[0:early] = (early_mine[...] + early_got[...]) * (1.0 / vector_total)
-    new_ref[early:steps] = (late_mine[...] + late_got[...]) * (1.0 / vector_total)
-    moments[0 : prior_count * group] = prior_ref[...].reshape(prior_count * group, lanes)
-    moments[prior_count * group :] = new_ref[...].reshape(steps * group, lanes)
-    flat = map_ref.reshape(2 * half * group, lanes)
-    flip = 7 - lax.broadcasted_iota(jnp.int32, (8, lanes), 0)
-    for b in range(0, group, 2):
-        sums = []
-        for parity, table in ((0, even_ref), (1, odd_ref)):
-            pair = [
-                moments[pl.ds(parity * group + b + i, pairs, stride=2 * group)] for i in range(2)
-            ]
-            high, low = split(jnp.concatenate(pair, axis=1))
-            sums.append(dot(table[...], jnp.concatenate([high, high, low, low], axis=0)))
-        plus = sums[0] + sums[1]
-        minus = sums[0] - sums[1]
-        for i in range(2):
-            columns = slice(i * lanes, (i + 1) * lanes)
-            flat[pl.ds(b + i, half, stride=group)] = plus[:, columns]
-            for r in range(0, half, 8):
-                turned = jnp.take_along_axis(minus[r : r + 8, columns], flip, axis=0)
-                top = 2 * half - 8 - r
-                flat[pl.ds(top * group + b + i, 8, stride=group)] = turned
-
-    @pl.when(step == pl.num_programs(0) * pl.num_programs(1) - 1)
-    def _():
-        for copy in copies:
-            copy.wait()
+            copies.append(copy)
+    for copy in copies:
+        copy.wait()
 
 
 def per_device(
@@ -351,6 +384,8 @@
     send_lists,
     tile_cols,
 ):
+    group, lanes = 8, 128
+    moment_count = prior_moments.shape[0] + STEPS
     vec_dev, blocks, width = cheb_cur.shape
     kind_count = hop_kinds.shape[0]
     groups = lax.axis_size("vec")
@@ -440,7 +475,6 @@
 
     partials = []
     buffers = []
-    reduced = []
     for s in range(STEPS):
         last = s == STEPS - 1
         partial = None
@@ -449,10 +483,14 @@
             args += [current[c][0], previous[c][0], probe_held, *received[c]]
             specs = [smem()] + [vmem()] * (len(args) - 1)
             fold = c == chunks - 1 and s >= STEPS - 2
-            older = len(partials) if fold else 0
-            extra = ([] if partial is None else [partial]) + (partials if fold else [])
+            older = 0 if last or not fold else len(partials)
+            extra = ([] if partial is None else [partial]) + partials[:older]
             args += extra
             specs += [vmem()] * len(extra)
+            fetch = s == STEPS - 2 and c == 0
+            if fetch:
+                args.append(stay(prior_moments))
+                specs.append(hbm())
             aliases = {len(args) + i: 2 + i for i in range(len(buffers))}
             args += buffers
             specs += [any_space()] * len(buffers)
@@ -467,8 +505,17 @@
                 scratch.append(pltpu.SemaphoreType.DMA)
             else:
                 outs += [rows, rows]
-            if fold:
+            if fold and last:
+                outs += [jax.ShapeDtypeStruct((quarter, width), F32)] * 4
+            elif fold:
                 outs += [jax.ShapeDtypeStruct((older + 1, groups // 2, quarter, width), F32)] * 2
+            if fetch:
+                outs.append(
+                    jax.ShapeDtypeStruct(
+                        (quarter // group, width // lanes, moment_count, group, lanes), F32
+                    )
+                )
+                scratch.append(pltpu.SemaphoreType.DMA((quarter // group * (width // lanes),)))
             out_specs += [vmem()] * (len(outs) - len(out_specs))
             cfg = (
                 vecs,
@@ -479,6 +526,7 @@
                 partial is not None,
                 older,
                 fold,
+                fetch,
                 len(buffers),
             )
             result = list(
@@ -499,21 +547,20 @@
                 buffers = [result.pop(0)]
             else:
                 received[c] = exchange(result.pop(0), result.pop(0))
-            if fold:
-                reduced.append(reduce(*result))
+            if fetch:
+                prior_held = result.pop(0)
+            if fold and last:
+                lates = [result[0]]
+                for flip in (2, 3, 1):
+                    pairs = [(i, i ^ flip) for i in range(groups)]
+                    lates.append(lax.ppermute(result[flip], "vec", pairs))
+            elif fold:
+                early = reduce(*result)
         partials.append(partial)
-        if fold:
-            partials = []
-
-    prior_count = prior_moments.shape[0]
-    moment_count = prior_count + STEPS
-    even_table, odd_table = jackson_split(moment_count, ENERGIES)
-    group, lanes = 8, 128
-
-    def small(count):
-        return pl.BlockSpec((count, group, lanes), lambda i, h: (0, i, h))
-
-    terms = [x for pair in reduced for x in pair]
+
+    tables = [jnp.asarray(x) for x in jackson_split(moment_count, ENERGIES)]
+    tiles = quarter // group * (width // lanes)
+    args = [*tables, prior_held, *early, *lates, *[current[c][0] for c in range(chunks)]]
     new_moments, energy_map, next_cur = pl.pallas_call(
         functools.partial(energy_kernel, vec_dev * groups, chunks),
         out_shape=[
@@ -521,33 +568,17 @@
             jax.ShapeDtypeStruct((ENERGIES, quarter, width), F32),
             full_shape,
         ],
-        grid=(quarter // group, width // lanes),
-        in_specs=[
-            pl.BlockSpec(even_table.shape, lambda i, h: (0, 0)),
-            pl.BlockSpec(odd_table.shape, lambda i, h: (0, 0)),
-            pl.BlockSpec((prior_count, group, lanes), lambda i, h: (0, i, h)),
-            *[small(x.shape[0]) for x in terms],
-            *[vmem()] * chunks,
-        ],
-        out_specs=[
-            small(STEPS),
-            pl.BlockSpec((ENERGIES, group, lanes), lambda i, h: (0, i, h)),
-            any_space(),
-        ],
+        in_specs=[vmem()] * len(args),
+        out_specs=[vmem(), any_space(), any_space()],
         scratch_shapes=[
-            pltpu.VMEM((moment_count * group, lanes), F32),
-            pltpu.SemaphoreType.DMA((chunks,)),
+            pltpu.VMEM((tiles, 16 * group, lanes), F32),
+            pltpu.VMEM((tiles, ENERGIES, group, lanes), F32),
+            pltpu.SemaphoreType.DMA((tiles + chunks,)),
         ],
         compiler_params=params(),
         cost_estimate=cost(4e9, 2.2e7),
         name="energy",
-    )(
-        jnp.asarray(even_table),
-        jnp.asarray(odd_table),
-        prior_moments,
-        *terms,
-        *[current[c][0] for c in range(chunks)],
-    )
+    )(*args)
     return buffers[0], next_cur, new_moments, energy_map
 
 

time: 77.5 us -> 76.7 us (0.990)
  waiting for transfers between devices: 6.11 us -> 4.04 us
  starting transfers between devices: 28.6 us -> 30 us
    ppermute x2 -> x1, waiting for transfers between devices: 3.33 us -> 0.01 us  [reduce(): lax.ppermute(give, 'vec', [(i, i ^ 2) for i in range(groups)])]
    ppermute x0 -> x3, waiting for transfers between devices: none -> 2.72 us  [per_device(): lates.append(lax.ppermute(result[flip], 'vec', pairs))]
    ppermute x0 -> x3, starting transfers between devices: none -> 2.21 us  [per_device(): lates.append(lax.ppermute(result[flip], 'vec', pairs))]
    pallas_call x8, Pallas kernels: 26.6 us -> 28.7 us  [per_device(): pl.pallas_call(functools.partial(step_kernel, cfg), out_shape=outs, in_sp...]
    pallas_call x1, Pallas kernels: 9.07 us -> 7.44 us  [per_device(): pl.pallas_call(functools.partial(energy_kernel, vec_dev * groups, chunks)...]
    ppermute x8, waiting for transfers between devices: 2.75 us -> 1.29 us  [exchange(): got_b = lax.ppermute(b, 'dom', swap_b)]
    ppermute x2 -> x1, starting transfers between devices: 2.24 us -> 1.58 us  [reduce(): lax.ppermute(give, 'vec', [(i, i ^ 2) for i in range(groups)])]
  transfers between devices with their start and end apart: 20 -> 21, of which waited for: 2 -> 3; matrix products, arithmetic and copies ran while one was open for 0% -> 0% of each run, Pallas kernels for 39% -> 42%
where the time goes in v3:
time: 76.7 us; the launch traced here: 76.5 us
  Pallas kernels  41.5 us (54%)
  starting transfers between devices  30 us (39%)
  waiting for transfers between devices  4.04 us (5%)
  between operations  0.98 us (1%)
    pallas_call x8, Pallas kernels, per_device(): pl.pallas_call(functools.partial(step_kernel, cfg), out_shape=outs, in_sp...  28.7 us
    ppermute x8, starting transfers between devices, exchange(): got_b = lax.ppermute(b, 'dom', swap_b)  20.8 us
    pallas_call x1, Pallas kernels, per_device(): pl.pallas_call(functools.partial(energy_kernel, vec_dev * groups, chunks)...  7.44 us
    ppermute x8, starting transfers between devices, exchange(): got_a = lax.ppermute(a, 'dom', swap_a)  5.4 us
    ppermute x3, waiting for transfers between devices, per_device(): lates.append(lax.ppermute(result[flip], 'vec', pairs))  2.72 us
    pallas_call x1, Pallas kernels, per_device(): pl.pallas_call(functools.partial(prep_kernel, rim), out_shape=[jax.ShapeD...  2.56 us
    pallas_call x1, Pallas kernels, per_device(): pl.pallas_call(functools.partial(first_kernel, rim, vecs), out_shape=[jax...  2.21 us
    ppermute x3, starting transfers between devices, per_device(): lates.append(lax.ppermute(result[flip], 'vec', pairs))  2.21 us
  transfers between devices with their start and end apart: 21, of which 3 were waited for; matrix products, arithmetic and copies ran while one was open for 0% of the time, Pallas kernels for 42%

profile of v3, /device:TPU:0, one launch (start us, length us, event | category | flops | bytes accessed | tf_op | source)
XLA Modules:
  0.0 76.5 jit_solution(12434191745349822400)
XLA Ops:
  0.7 0.1 pad_add_fusion.index_ref
  0.7 2.2 %first_sends.1 = (bf16[96,256]{1,0:T(8,128)(2,1)S(1)}, f32[4,128,256]{2,1,0:T(8,128)S(1)}, f32[48,512]{1,0:T(8,128)S(1)}, f32[48,512]{1,0:T(8,128)S(1)}, f32[48,512]{1,0:T(8,128)S(1)}, /*index=5*/f32[48,512]{1,0:T(8,128)S(1)}) custom-call(s32[3]{0:T(128)S(1)} %pad_add_fusion.index_ref, s32[1,2,48]{2,1,0:T(2,128)} %lists_hbm.1, f32[4,128,256]{2,1,0:T(8,128)} %cur_hbm.1), custom_call_target="tpu_custom_call" | custom-call | flops 100000000 | bytes 1000000 | tf_op jit(solution)/shard_map/first_sends/pallas_call | solution.py:406
  2.9 3.0 %collective-permute-start.2 = (f32[48,512]{1,0:T(8,128)S(1)}, f32[48,512]{1,0:T(8,128)S(1)}, u32[]{:S(2)}, u32[]{:S(2)}) collective-permute-start(f32[48,512]{1,0:T(8,128)S(1)} %get-tuple-element.66), channel_id=1, source_target_pairs={{0,1},{1,0},{2,3},{3,2},{4,5},{5,4},{6,7},{7,6},{8,9},{9,8},{10,11... | collective-permute-start | bytes 294920 | tf_op jit(solution)/shard_map/ppermute | solution.py:424
  6.0 3.6 %collective-permute-start.3 = (f32[48,512]{1,0:T(8,128)S(1)}, f32[48,512]{1,0:T(8,128)S(1)}, u32[]{:S(2)}, u32[]{:S(2)}) collective-permute-start(f32[48,512]{1,0:T(8,128)S(1)} %get-tuple-element.67), channel_id=1, source_target_pairs={{0,7},{1,2},{2,1},{3,4},{4,3},{5,6},{6,5},{7,0},{8,15},{9,10},{10,... | collective-permute-start | bytes 294920 | tf_op jit(solution)/shard_map/ppermute | solution.py:423
  9.6 1.9 %collective-permute-start.1 = (f32[48,512]{1,0:T(8,128)S(1)}, f32[48,512]{1,0:T(8,128)S(1)}, u32[]{:S(2)}, u32[]{:S(2)}) collective-permute-start(f32[48,512]{1,0:T(8,128)S(1)} %get-tuple-element.65), channel_id=1, source_target_pairs={{0,7},{1,2},{2,1},{3,4},{4,3},{5,6},{6,5},{7,0},{8,15},{9,10},{10,... | collective-permute-start | bytes 294920 | tf_op jit(solution)/shard_map/ppermute | solution.py:423
  11.5 2.6 %tables.1 = (bf16[1024,512]{1,0:T(8,128)(2,1)S(1)}, bf16[2048,256]{1,0:T(8,128)(2,1)S(1)}, bf16[2048,256]{1,0:T(8,128)(2,1)S(1)}, f32[4,128,256]{2,1,0:T(8,128)S...) custom-call(s32[3]{0:T(128)S(1)} %pad_add_fusion.index_ref, s32[4,128]{1,0:T(4,128)} %bitcast.5, ...), custom_call_target="tpu_custom_call" | custom-call | flops 10000000 | bytes 8000000 | tf_op jit(solution)/shard_map/tables/pallas_call | solution.py:429
  14.1 3.2 %shard_map.138 = (f32[2,128,256]{2,1,0:T(8,128)S(1)}, f32[128,256]{1,0:T(8,128)S(1)}, f32[48,512]{1,0:T(8,128)S(1)}, f32[48,512]{1,0:T(8,128)S(1)}) custom-call(s32[3]{0:T(128)S(1)} %pad_add_fusion.index_ref, bf16[1024,512]{1,0:T(8,128)(2,1)S(1)} %get-tuple-element.56.mix_ref, bf16[2048,256]{1,0:T(8,128)(2,1)S(1)} %get-tuple-element.57.high_ref, ...), custom_call_target="tpu_custom_call" | custom-call | flops 1500000000 | bytes 5000000 | tf_op jit(solution)/shard_map/pallas_call | solution.py:533
  17.3 0.7 collective-permute-start.6
  17.9 4.6 %collective-permute-start.7 = (f32[48,512]{1,0:T(8,128)S(1)}, f32[48,512]{1,0:T(8,128)S(1)}, u32[]{:S(2)}, u32[]{:S(2)}) collective-permute-start(f32[48,512]{1,0:T(8,128)S(1)} %get-tuple-element.74), channel_id=1, source_target_pairs={{0,7},{1,2},{2,1},{3,4},{4,3},{5,6},{6,5},{7,0},{8,15},{9,10},{10,... | collective-permute-start | bytes 294920 | tf_op jit(solution)/shard_map/ppermute | solution.py:423
  22.5 3.2 %shard_map.139 = (f32[2,128,256]{2,1,0:T(8,128)S(1)}, f32[128,256]{1,0:T(8,128)S(1)}, f32[48,512]{1,0:T(8,128)S(1)}, f32[48,512]{1,0:T(8,128)S(1)}) custom-call(s32[3]{0:T(128)S(1)} %pad_add_fusion.index_ref, bf16[1024,512]{1,0:T(8,128)(2,1)S(1)} %get-tuple-element.56.mix_ref, bf16[2048,256]{1,0:T(8,128)(2,1)S(1)} %get-tuple-element.57.high_ref, ...), custom_call_target="tpu_custom_call" | custom-call | flops 1500000000 | bytes 5000000 | tf_op jit(solution)/shard_map/pallas_call | solution.py:533
  25.8 1.4 %collective-permute-start.5 = (f32[48,512]{1,0:T(8,128)S(1)}, f32[48,512]{1,0:T(8,128)S(1)}, u32[]{:S(2)}, u32[]{:S(2)}) collective-permute-start(f32[48,512]{1,0:T(8,128)S(1)} %get-tuple-element.71), channel_id=1, source_target_pairs={{0,7},{1,2},{2,1},{3,4},{4,3},{5,6},{6,5},{7,0},{8,15},{9,10},{10,... | collective-permute-start | bytes 294920 | tf_op jit(solution)/shard_map/ppermute | solution.py:423
  27.2 3.2 %shard_map.140 = (f32[2,128,256]{2,1,0:T(8,128)S(1)}, f32[128,256]{1,0:T(8,128)S(1)}, f32[48,512]{1,0:T(8,128)S(1)}, f32[48,512]{1,0:T(8,128)S(1)}) custom-call(s32[3]{0:T(128)S(1)} %pad_add_fusion.index_ref, bf16[1024,512]{1,0:T(8,128)(2,1)S(1)} %get-tuple-element.56.mix_ref, bf16[2048,256]{1,0:T(8,128)(2,1)S(1)} %get-tuple-element.57.high_ref, ...), custom_call_target="tpu_custom_call" | custom-call | flops 1500000000 | bytes 5000000 | tf_op jit(solution)/shard_map/pallas_call | solution.py:533
  30.3 1.1 %collective-permute-start.10 = (f32[48,512]{1,0:T(8,128)S(1)}, f32[48,512]{1,0:T(8,128)S(1)}, u32[]{:S(2)}, u32[]{:S(2)}) collective-permute-start(f32[48,512]{1,0:T(8,128)S(1)} %get-tuple-element.80), channel_id=1, source_target_pairs={{0,1},{1,0},{2,3},{3,2},{4,5},{5,4},{6,7},{7,6},{8,9},{9,8},{10,11... | collective-permute-start | bytes 294920 | tf_op jit(solution)/shard_map/ppermute | solution.py:424
  31.5 2.4 %collective-permute-start.11 = (f32[48,512]{1,0:T(8,128)S(1)}, f32[48,512]{1,0:T(8,128)S(1)}, u32[]{:S(2)}, u32[]{:S(2)}) collective-permute-start(f32[48,512]{1,0:T(8,128)S(1)} %get-tuple-element.81), channel_id=1, source_target_pairs={{0,7},{1,2},{2,1},{3,4},{4,3},{5,6},{6,5},{7,0},{8,15},{9,10},{10,... | collective-permute-start | bytes 294920 | tf_op jit(solution)/shard_map/ppermute | solution.py:423
  33.9 3.2 %shard_map.141 = (f32[2,128,256]{2,1,0:T(8,128)S(1)}, f32[128,256]{1,0:T(8,128)S(1)}, f32[48,512]{1,0:T(8,128)S(1)}, f32[48,512]{1,0:T(8,128)S(1)}) custom-call(s32[3]{0:T(128)S(1)} %pad_add_fusion.index_ref, bf16[1024,512]{1,0:T(8,128)(2,1)S(1)} %get-tuple-element.56.mix_ref, bf16[2048,256]{1,0:T(8,128)(2,1)S(1)} %get-tuple-element.57.high_ref, ...), custom_call_target="tpu_custom_call" | custom-call | flops 1500000000 | bytes 5000000 | tf_op jit(solution)/shard_map/pallas_call | solution.py:533
  37.1 0.4 collective-permute-start.8
  37.5 2.1 %collective-permute-start.9 = (f32[48,512]{1,0:T(8,128)S(1)}, f32[48,512]{1,0:T(8,128)S(1)}, u32[]{:S(2)}, u32[]{:S(2)}) collective-permute-start(f32[48,512]{1,0:T(8,128)S(1)} %get-tuple-element.78), channel_id=1, source_target_pairs={{0,7},{1,2},{2,1},{3,4},{4,3},{5,6},{6,5},{7,0},{8,15},{9,10},{10,... | collective-permute-start | bytes 294920 | tf_op jit(solution)/shard_map/ppermute | solution.py:423
  39.5 5.3 %shard_map.142 = (f32[2,128,256]{2,1,0:T(8,128)S(1)}, f32[128,256]{1,0:T(8,128)S(1)}, f32[48,512]{1,0:T(8,128)S(1)}, f32[48,512]{1,0:T(8,128)S(1)}, f32[4,2,128,8,128]{4,3,2,1,0:T(8,128)S(1)}) custom-call(s32[3]{0:T(128)S(1)} %pad_add_fusion.index_ref, bf16[1024,512]{1,0:T(8,128)(2,1)S(1)} %get-tuple-element.56.mix_ref, ...), custom_call_target="tpu_custom_call" | custom-call | flops 1500000000 | bytes 5000000 | tf_op jit(solution)/shard_map/pallas_call | solution.py:533
  44.9 3.6 %collective-permute-start.15 = (f32[48,512]{1,0:T(8,128)S(1)}, f32[48,512]{1,0:T(8,128)S(1)}, u32[]{:S(2)}, u32[]{:S(2)}) collective-permute-start(f32[48,512]{1,0:T(8,128)S(1)} %get-tuple-element.90), channel_id=1, source_target_pairs={{0,7},{1,2},{2,1},{3,4},{4,3},{5,6},{6,5},{7,0},{8,15},{9,10},{10,... | collective-permute-start | bytes 294920 | tf_op jit(solution)/shard_map/ppermute | solution.py:423
  48.5 3.9 %shard_map.143 = (f32[2,128,256]{2,1,0:T(8,128)S(1)}, f32[128,256]{1,0:T(8,128)}, f32[48,512]{1,0:T(8,128)S(1)}, f32[48,512]{1,0:T(8,128)S(1)}, f32[3,2,32,256]{...) custom-call(s32[3]{0:T(128)S(1)} %pad_add_fusion.index_ref, bf16[1024,512]{1,0:T(8,128)(2,1)S(1)} %get-tuple-element.56.mix_ref, ...), custom_call_target="tpu_custom_call" | custom-call | flops 1500000000 | bytes 5000000 | tf_op jit(solution)/shard_map/pallas_call | solution.py:533
  52.4 0.1 collective-permute-start.12
  52.4 1.3 %collective-permute-start.13 = (f32[48,512]{1,0:T(8,128)S(1)}, f32[48,512]{1,0:T(8,128)S(1)}, u32[]{:S(2)}, u32[]{:S(2)}) collective-permute-start(f32[48,512]{1,0:T(8,128)S(1)} %get-tuple-element.87), channel_id=1, source_target_pairs={{0,7},{1,2},{2,1},{3,4},{4,3},{5,6},{6,5},{7,0},{8,15},{9,10},{10,... | collective-permute-start | bytes 294920 | tf_op jit(solution)/shard_map/ppermute | solution.py:423
  53.8 3.0 %shard_map.144 = (f32[2,128,256]{2,1,0:T(8,128)S(1)}, f32[128,256]{1,0:T(8,128)S(1)}, f32[4,128,256]{2,1,0:T(8,128)}) custom-call(s32[3]{0:T(128)S(1)} %pad_add_fusion.index_ref, bf16[1024,512]{1,0:T(8,128)(2,1)S(1)} %get-tuple-element.56.mix_ref, bf16[2048,256]{1,0:T(8,128)(2,1)S(1)} %get-tuple-element.57.high_ref, ...), custom_call_target="tpu_custom_call" | custom-call | flops 1500000000 | bytes 5000000 | tf_op jit(solution)/shard_map/pallas_call | solution.py:533
  56.8 0.6 fold.1
  57.4 1.6 %collective-permute-start.17 = (f32[3,32,256]{2,1,0:T(8,128)S(1)}, f32[3,32,256]{2,1,0:T(8,128)S(1)}, u32[]{:S(2)}, u32[]{:S(2)}) collective-permute-start(f32[3,32,256]{2,1,0:T(8,128)S(1)} %get-tuple-element.98), channel_id=1, source_target_pairs={{0,16},{8,24},{16,0},{24,8},{1,17},{9,25},{17,1},{25,9},{2,18},{10... | collective-permute-start | bytes 294920 | tf_op jit(solution)/shard_map/ppermute | solution.py:474
  59.0 1.3 %collective-permute-done.13.recv_b = f32[48,512]{1,0:T(8,128)S(1)} collective-permute-done((f32[48,512]{1,0:T(8,128)S(1)}, f32[48,512]{1,0:T(8,128)S(1)}, u32[]{:S(2)}, u32[]{:S(2)}) %collective-permute-start.13) | collective-permute-done | bytes 98336 | tf_op jit(solution)/shard_map/ppermute | solution.py:423
  60.3 3.7 %shard_map.145 = (f32[2,128,256]{2,1,0:T(8,128)S(1)}, f32[128,256]{1,0:T(8,128)}, f32[4,128,256]{2,1,0:T(8,128)}, f32[32,256]{1,0:T(8,128)S(1)}, f32[32,256]{1,0...) custom-call(s32[3]{0:T(128)S(1)} %pad_add_fusion.index_ref, ...), custom_call_target="tpu_custom_call", output_to_operand_aliasing={{2}: (12, {})} | custom-call | flops 1500000000 | bytes 5000000 | tf_op jit(solution)/shard_map/pallas_call | solution.py:533
  64.0 1.6 %collective-permute-start.18 = (f32[32,256]{1,0:T(8,128)S(1)}, f32[32,256]{1,0:T(8,128)S(1)}, u32[]{:S(2)}, u32[]{:S(2)}) collective-permute-start(f32[32,256]{1,0:T(8,128)S(1)} %get-tuple-element.100), channel_id=1, source_target_pairs={{0,16},{8,24},{16,0},{24,8},{1,17},{9,25},{17,1},{25,9},{2,18},{10... | collective-permute-start | bytes 98312 | tf_op jit(solution)/shard_map/ppermute | solution.py:556
  65.6 0.6 collective-permute-start.20
  66.2 1.8 %collective-permute-done.18.rest_1_ = f32[32,256]{1,0:T(8,128)S(1)} collective-permute-done((f32[32,256]{1,0:T(8,128)S(1)}, f32[32,256]{1,0:T(8,128)S(1)}, u32[]{:S(2)}, u32[]{:S(2)}) %collective-permute-start.18) | collective-permute-done | bytes 32800 | tf_op jit(solution)/shard_map/ppermute | solution.py:556
  68.0 0.9 %collective-permute-done.19.rest_2_ = f32[32,256]{1,0:T(8,128)S(1)} collective-permute-done((f32[32,256]{1,0:T(8,128)S(1)}, f32[32,256]{1,0:T(8,128)S(1)}, u32[]{:S(2)}, u32[]{:S(2)}) %collective-permute-start.19) | collective-permute-done | bytes 32800 | tf_op jit(solution)/shard_map/ppermute | solution.py:556
  68.9 7.4 %energy.1 = (f32[4,32,256]{2,1,0:T(8,128)}, f32[512,32,256]{2,1,0:T(8,128)}, f32[4,128,256]{2,1,0:T(8,128)}) custom-call(bf16[256,256]{1,0:T(8,128)(2,1)S(1)} %copy-done.1, bf16[256,256]{1,0:T(8,128)(2,1)S(1)} %copy-done, f32[4,2,128,8,128]{4,3,2,1,0:T(8,128)S(1)} %get-tuple-element.94.prior_ref, f32[3,32,256]{2,1,0:T(8,128)S(1)} %get-tuple-element.97.early_mine, ...), custom_call_target="tpu_custom_call" | custom-call | flops 4000000000 | bytes 22000000 | tf_op jit(solution)/shard_map/energy/pallas_call | solution.py:564
  (27 shorter events, 0.2 us)
Async XLA Ops:
  2.9 11.1 %collective-permute-start.2 = (f32[48,512]{1,0:T(8,128)S(1)}, f32[48,512]{1,0:T(8,128)S(1)}, u32[]{:S(2)}, u32[]{:S(2)}) collective-permute-start(f32[48,512]{1,0:T(8,128)S(1)} %get-tuple-element.66), channel_id=1, source_target_pairs={{0,1},{1,0},{2,3},{3,2},{4,5},{5,4},{6,7},{7,6},{8,9},{9,8},{10,11... | collective-permute-start | bytes 294920 | tf_op jit(solution)/shard_map/ppermute | solution.py:424
  6.0 8.1 %collective-permute-start.3 = (f32[48,512]{1,0:T(8,128)S(1)}, f32[48,512]{1,0:T(8,128)S(1)}, u32[]{:S(2)}, u32[]{:S(2)}) collective-permute-start(f32[48,512]{1,0:T(8,128)S(1)} %get-tuple-element.67), channel_id=1, source_target_pairs={{0,7},{1,2},{2,1},{3,4},{4,3},{5,6},{6,5},{7,0},{8,15},{9,10},{10,... | collective-permute-start | bytes 294920 | tf_op jit(solution)/shard_map/ppermute | solution.py:423
  9.6 12.9 %collective-permute-start = (f32[48,512]{1,0:T(8,128)S(1)}, f32[48,512]{1,0:T(8,128)S(1)}, u32[]{:S(2)}, u32[]{:S(2)}) collective-permute-start(f32[48,512]{1,0:T(8,128)S(1)} %get-tuple-element.64), channel_id=1, source_target_pairs={{0,1},{1,0},{2,3},{3,2},{4,5},{5,4},{6,7},{7,6},{8,9},{9,8},{10,11... | collective-permute-start | bytes 294920 | tf_op jit(solution)/shard_map/ppermute | solution.py:424
  9.6 12.9 %collective-permute-start.1 = (f32[48,512]{1,0:T(8,128)S(1)}, f32[48,512]{1,0:T(8,128)S(1)}, u32[]{:S(2)}, u32[]{:S(2)}) collective-permute-start(f32[48,512]{1,0:T(8,128)S(1)} %get-tuple-element.65), channel_id=1, source_target_pairs={{0,7},{1,2},{2,1},{3,4},{4,3},{5,6},{6,5},{7,0},{8,15},{9,10},{10,... | collective-permute-start | bytes 294920 | tf_op jit(solution)/shard_map/ppermute | solution.py:423
  17.3 9.9 %collective-permute-start.6 = (f32[48,512]{1,0:T(8,128)S(1)}, f32[48,512]{1,0:T(8,128)S(1)}, u32[]{:S(2)}, u32[]{:S(2)}) collective-permute-start(f32[48,512]{1,0:T(8,128)S(1)} %get-tuple-element.73), channel_id=1, source_target_pairs={{0,1},{1,0},{2,3},{3,2},{4,5},{5,4},{6,7},{7,6},{8,9},{9,8},{10,11... | collective-permute-start | bytes 294920 | tf_op jit(solution)/shard_map/ppermute | solution.py:424
  17.9 9.2 %collective-permute-start.7 = (f32[48,512]{1,0:T(8,128)S(1)}, f32[48,512]{1,0:T(8,128)S(1)}, u32[]{:S(2)}, u32[]{:S(2)}) collective-permute-start(f32[48,512]{1,0:T(8,128)S(1)} %get-tuple-element.74), channel_id=1, source_target_pairs={{0,7},{1,2},{2,1},{3,4},{4,3},{5,6},{6,5},{7,0},{8,15},{9,10},{10,... | collective-permute-start | bytes 294920 | tf_op jit(solution)/shard_map/ppermute | solution.py:423
  25.7 8.2 %collective-permute-start.4 = (f32[48,512]{1,0:T(8,128)S(1)}, f32[48,512]{1,0:T(8,128)S(1)}, u32[]{:S(2)}, u32[]{:S(2)}) collective-permute-start(f32[48,512]{1,0:T(8,128)S(1)} %get-tuple-element.70), channel_id=1, source_target_pairs={{0,1},{1,0},{2,3},{3,2},{4,5},{5,4},{6,7},{7,6},{8,9},{9,8},{10,11... | collective-permute-start | bytes 294920 | tf_op jit(solution)/shard_map/ppermute | solution.py:424
  25.8 8.1 %collective-permute-start.5 = (f32[48,512]{1,0:T(8,128)S(1)}, f32[48,512]{1,0:T(8,128)S(1)}, u32[]{:S(2)}, u32[]{:S(2)}) collective-permute-start(f32[48,512]{1,0:T(8,128)S(1)} %get-tuple-element.71), channel_id=1, source_target_pairs={{0,7},{1,2},{2,1},{3,4},{4,3},{5,6},{6,5},{7,0},{8,15},{9,10},{10,... | collective-permute-start | bytes 294920 | tf_op jit(solution)/shard_map/ppermute | solution.py:423
  30.3 9.2 %collective-permute-start.10 = (f32[48,512]{1,0:T(8,128)S(1)}, f32[48,512]{1,0:T(8,128)S(1)}, u32[]{:S(2)}, u32[]{:S(2)}) collective-permute-start(f32[48,512]{1,0:T(8,128)S(1)} %get-tuple-element.80), channel_id=1, source_target_pairs={{0,1},{1,0},{2,3},{3,2},{4,5},{5,4},{6,7},{7,6},{8,9},{9,8},{10,11... | collective-permute-start | bytes 294920 | tf_op jit(solution)/shard_map/ppermute | solution.py:424
  31.5 8.1 %collective-permute-start.11 = (f32[48,512]{1,0:T(8,128)S(1)}, f32[48,512]{1,0:T(8,128)S(1)}, u32[]{:S(2)}, u32[]{:S(2)}) collective-permute-start(f32[48,512]{1,0:T(8,128)S(1)} %get-tuple-element.81), channel_id=1, source_target_pairs={{0,7},{1,2},{2,1},{3,4},{4,3},{5,6},{6,5},{7,0},{8,15},{9,10},{10,... | collective-permute-start | bytes 294920 | tf_op jit(solution)/shard_map/ppermute | solution.py:423
  37.1 11.3 %collective-permute-start.8 = (f32[48,512]{1,0:T(8,128)S(1)}, f32[48,512]{1,0:T(8,128)S(1)}, u32[]{:S(2)}, u32[]{:S(2)}) collective-permute-start(f32[48,512]{1,0:T(8,128)S(1)} %get-tuple-element.77), channel_id=1, source_target_pairs={{0,1},{1,0},{2,3},{3,2},{4,5},{5,4},{6,7},{7,6},{8,9},{9,8},{10,11... | collective-permute-start | bytes 294920 | tf_op jit(solution)/shard_map/ppermute | solution.py:424
  37.5 11.0 %collective-permute-start.9 = (f32[48,512]{1,0:T(8,128)S(1)}, f32[48,512]{1,0:T(8,128)S(1)}, u32[]{:S(2)}, u32[]{:S(2)}) collective-permute-start(f32[48,512]{1,0:T(8,128)S(1)} %get-tuple-element.78), channel_id=1, source_target_pairs={{0,7},{1,2},{2,1},{3,4},{4,3},{5,6},{6,5},{7,0},{8,15},{9,10},{10,... | collective-permute-start | bytes 294920 | tf_op jit(solution)/shard_map/ppermute | solution.py:423
  44.8 8.9 %collective-permute-start.14 = (f32[48,512]{1,0:T(8,128)S(1)}, f32[48,512]{1,0:T(8,128)S(1)}, u32[]{:S(2)}, u32[]{:S(2)}) collective-permute-start(f32[48,512]{1,0:T(8,128)S(1)} %get-tuple-element.89), channel_id=1, source_target_pairs={{0,1},{1,0},{2,3},{3,2},{4,5},{5,4},{6,7},{7,6},{8,9},{9,8},{10,11... | collective-permute-start | bytes 294920 | tf_op jit(solution)/shard_map/ppermute | solution.py:424
  44.9 8.9 %collective-permute-start.15 = (f32[48,512]{1,0:T(8,128)S(1)}, f32[48,512]{1,0:T(8,128)S(1)}, u32[]{:S(2)}, u32[]{:S(2)}) collective-permute-start(f32[48,512]{1,0:T(8,128)S(1)} %get-tuple-element.90), channel_id=1, source_target_pairs={{0,7},{1,2},{2,1},{3,4},{4,3},{5,6},{6,5},{7,0},{8,15},{9,10},{10,... | collective-permute-start | bytes 294920 | tf_op jit(solution)/shard_map/ppermute | solution.py:423
  52.4 4.5 %collective-permute-start.16 = (f32[3,2,32,256]{3,2,1,0:T(8,128)S(1)}, f32[3,2,32,256]{3,2,1,0:T(8,128)S(1)}, u32[]{:S(2)}, u32[]{:S(2)}) collective-permute-start(f32[3,2,32,256]{3,2,1,0:T(8,128)S(1)} %get-tuple-element.96), channel_id=1, source_target_pairs={{0,8},{8,0},{16,24},{24,16},{1,9},{9,1},{17,25},{25,17},{2,10},{10... | collective-permute-start | bytes 589832 | tf_op jit(solution)/shard_map/ppermute | solution.py:463
  52.4 6.6 %collective-permute-start.12 = (f32[48,512]{1,0:T(8,128)S(1)}, f32[48,512]{1,0:T(8,128)S(1)}, u32[]{:S(2)}, u32[]{:S(2)}) collective-permute-start(f32[48,512]{1,0:T(8,128)S(1)} %get-tuple-element.86), channel_id=1, source_target_pairs={{0,1},{1,0},{2,3},{3,2},{4,5},{5,4},{6,7},{7,6},{8,9},{9,8},{10,11... | collective-permute-start | bytes 294920 | tf_op jit(solution)/shard_map/ppermute | solution.py:424
  52.4 7.8 %collective-permute-start.13 = (f32[48,512]{1,0:T(8,128)S(1)}, f32[48,512]{1,0:T(8,128)S(1)}, u32[]{:S(2)}, u32[]{:S(2)}) collective-permute-start(f32[48,512]{1,0:T(8,128)S(1)} %get-tuple-element.87), channel_id=1, source_target_pairs={{0,7},{1,2},{2,1},{3,4},{4,3},{5,6},{6,5},{7,0},{8,15},{9,10},{10,... | collective-permute-start | bytes 294920 | tf_op jit(solution)/shard_map/ppermute | solution.py:423
  56.8 12.1 %copy-start = (bf16[256,256]{1,0:T(8,128)(2,1)S(1)}, bf16[256,256]{1,0:T(8,128)(2,1)}, u32[]{:S(2)}) copy-start(bf16[256,256]{1,0:T(8,128)(2,1)} %constant.41.clone.odd_ref) | copy-start | bytes 393220
  56.8 12.1 %copy-start.1 = (bf16[256,256]{1,0:T(8,128)(2,1)S(1)}, bf16[256,256]{1,0:T(8,128)(2,1)}, u32[]{:S(2)}) copy-start(bf16[256,256]{1,0:T(8,128)(2,1)} %constant.40.clone.even_ref) | copy-start | bytes 393220
  57.4 11.5 %collective-permute-start.17 = (f32[3,32,256]{2,1,0:T(8,128)S(1)}, f32[3,32,256]{2,1,0:T(8,128)S(1)}, u32[]{:S(2)}, u32[]{:S(2)}) collective-permute-start(f32[3,32,256]{2,1,0:T(8,128)S(1)} %get-tuple-element.98), channel_id=1, source_target_pairs={{0,16},{8,24},{16,0},{24,8},{1,17},{9,25},{17,1},{25,9},{2,18},{10... | collective-permute-start | bytes 294920 | tf_op jit(solution)/shard_map/ppermute | solution.py:474
  64.0 4.0 %collective-permute-start.18 = (f32[32,256]{1,0:T(8,128)S(1)}, f32[32,256]{1,0:T(8,128)S(1)}, u32[]{:S(2)}, u32[]{:S(2)}) collective-permute-start(f32[32,256]{1,0:T(8,128)S(1)} %get-tuple-element.100), channel_id=1, source_target_pairs={{0,16},{8,24},{16,0},{24,8},{1,17},{9,25},{17,1},{25,9},{2,18},{10... | collective-permute-start | bytes 98312 | tf_op jit(solution)/shard_map/ppermute | solution.py:556
  65.6 3.3 %collective-permute-start.19 = (f32[32,256]{1,0:T(8,128)S(1)}, f32[32,256]{1,0:T(8,128)S(1)}, u32[]{:S(2)}, u32[]{:S(2)}) collective-permute-start(f32[32,256]{1,0:T(8,128)S(1)} %get-tuple-element.101), channel_id=1, source_target_pairs={{0,24},{8,16},{16,8},{24,0},{1,25},{9,17},{17,9},{25,1},{2,26},{10... | collective-permute-start | bytes 98312 | tf_op jit(solution)/shard_map/ppermute | solution.py:556
  65.6 3.3 %collective-permute-start.20 = (f32[32,256]{1,0:T(8,128)S(1)}, f32[32,256]{1,0:T(8,128)S(1)}, u32[]{:S(2)}, u32[]{:S(2)}) collective-permute-start(f32[32,256]{1,0:T(8,128)S(1)} %get-tuple-element.102), channel_id=1, source_target_pairs={{0,8},{8,0},{16,24},{24,16},{1,9},{9,1},{17,25},{25,17},{2,10},{10... | collective-permute-start | bytes 98312 | tf_op jit(solution)/shard_map/ppermute | solution.py:556

commit v4 on v3

--- a/solution.py
+++ b/solution.py
@@ -77,8 +77,14 @@
     return pltpu.with_memory_space_constraint(x, pltpu.HBM)
 
 
-def first_kernel(rim, vecs, index_ref, lists_hbm, cur_hbm, pick_ref, cur_ref, *rest):
-    sends, (lists_ref, sems) = rest[:-2], rest[-2:]
+def emit_sends(pick, value, columns, send_a, send_b):
+    rim = send_a.shape[0]
+    got = gather_rows(pick, value)
+    send_a[:, columns] = got[:rim]
+    send_b[:, columns] = got[rim:]
+
+
+def first_kernel(rim, index_ref, lists_hbm, cur_hbm, pick_ref, cur_ref, send_a, send_b, lists_ref, sems):
     count, blocks, width = cur_ref.shape
     list_copy = pltpu.make_async_copy(lists_hbm, lists_ref, sems.at[count])
     list_copy.start()
@@ -102,13 +108,8 @@
         pick_ref[pl.ds(half * rim, rim), blocks : 2 * blocks] = onehot
     pick = pick_ref[...]
     for v in range(count):
-        chunk, place = divmod(v, vecs)
         copies[v].wait()
-        got = gather_rows(pick, cur_ref[v])
-        for half in range(2):
-            sends[2 * chunk + half][:, place * width : (place + 1) * width] = got[
-                half * rim : (half + 1) * rim
-            ]
+        emit_sends(pick, cur_ref[v], slice(v * width, (v + 1) * width), send_a, send_b)
 
 
 def prep_kernel(
@@ -116,7 +117,9 @@
     index_ref,
     cols_hbm,
     ids_hbm,
+    pick_ref,
     kinds_hbm,
+    cur_hbm,
     prev_hbm,
     probe_hbm,
     site_hbm,
@@ -126,6 +129,9 @@
     prev_ref,
     probe_ref,
     site_ref,
+    cur_ref,
+    send_a,
+    send_b,
     cols_ref,
     ids_ref,
     kinds,
@@ -142,6 +148,14 @@
         pltpu.make_async_copy(cols_hbm, cols_ref, sems.at[kind_count + 3]),
         pltpu.make_async_copy(ids_hbm, ids_ref, sems.at[kind_count + 4]),
     ]
+    vecs = cur_ref.shape[0]
+    first = cur_hbm.shape[0] - vecs
+    for v in range(vecs):
+        small.append(
+            pltpu.make_async_copy(
+                cur_hbm.at[first + v], cur_ref.at[v], sems.at[kind_count + 5 + v]
+            )
+        )
     for copy in small:
         copy.start()
     for i, (source, target) in enumerate(fetched):
@@ -169,6 +183,8 @@
         ).astype(BF16)
         mix_ref[n * blocks : (n + 1) * blocks, 0:padded] = turned
         mix_ref[n * blocks : (n + 1) * blocks, padded : 2 * padded] = turned
+    for v in range(vecs):
+        emit_sends(pick_ref[...], cur_ref[v], slice(v * width, (v + 1) * width), send_a, send_b)
     for n in range(kind_count):
         copies[n].wait()
         high, low = split(2.0 * kinds[n])
@@ -197,7 +213,7 @@
     rest = list(rest)
     partial_in = rest.pop(0) if add_partial else None
     olders = [rest.pop(0) for _ in range(older)]
-    prior_hbm = rest.pop(0) if fetch else None
+    prior_hbm = rest.pop(0) if fetch is not None else None
     rest = rest[aliased:]
     out_ref, partial_out = rest[:2]
     rest = rest[2:]
@@ -209,7 +225,7 @@
         pieces_out = [rest.pop(0) for _ in range(4)]
     elif fold:
         keep_ref, give_ref = rest.pop(0), rest.pop(0)
-    if fetch:
+    if fetch is not None:
         prior_ref = rest.pop(0)
     source, mixed = rest[:2]
     blocks, width = cur_ref.shape[1:]
@@ -224,22 +240,22 @@
                 cur_ref.at[pl.ds(cur_at, vecs)], prev_out.at[pl.ds(own_at, vecs)], rest[2]
             )
         ]
-    if fetch:
-        count, halves, moments, group, lanes = prior_ref.shape
+    if fetch is not None:
+        halves, _, moments, group, lanes = prior_ref.shape
         known = prior_hbm.shape[0]
         copies = [
             pltpu.make_async_copy(
-                prior_hbm.at[:, pl.ds(i * group, group), pl.ds(h * lanes, lanes)],
-                prior_ref.at[i, h, pl.ds(0, known)],
-                rest[2].at[i * halves + h],
+                prior_hbm.at[:, p, pl.ds(fetch * group, group), pl.ds(h * lanes, lanes)],
+                prior_ref.at[h, p, pl.ds(0, known)],
+                rest[2].at[2 * h + p],
             )
-            for i in range(count)
             for h in range(halves)
+            for p in range(2)
         ]
     for copy in copies:
         copy.start()
-    if fetch:
-        prior_ref[:, :, known:] = jnp.zeros((count, halves, moments - known, group, lanes), F32)
+    if fetch is not None:
+        prior_ref[:, :, known:] = jnp.zeros((halves, 2, moments - known, group, lanes), F32)
     for v in range(vecs):
         columns = slice(v * width, (v + 1) * width)
         pieces = [cur_ref[cur_at + v], recv_a[:, columns], recv_b[:, columns]]
@@ -276,9 +292,8 @@
         term = probe_ref[own_at + v] * following
         partial = term if partial is None else partial + term
         if not last:
-            got = gather_rows(pick_ref[...], following)
-            send_a[:, v * width : (v + 1) * width] = got[:rim]
-            send_b[:, v * width : (v + 1) * width] = got[rim:]
+            columns = slice(v * width, (v + 1) * width)
+            emit_sends(pick_ref[...], following, columns, send_a, send_b)
     partial_out[...] = partial
     if fold and last:
         quarter = pieces_out[0].shape[0]
@@ -309,10 +324,11 @@
     give_ref[...] = keep_ref[:, 1 - y] + got_ref[:, 1 - y]
 
 
-def energy_kernel(vector_total, chunks, even_ref, odd_ref, prior_ref, early_mine, early_got, *rest):
+def energy_kernel(vector_total, chunks, count, even_ref, odd_ref, early_mine, early_got, *rest):
+    priors, rest = rest[:count], rest[count:]
     lates, finals = rest[:4], rest[4 : 4 + chunks]
     new_ref, map_out, cur_out, fresh, held, sems = rest[4 + chunks :]
-    count, halves, moments, group, lanes = prior_ref.shape
+    halves, _, pairs, group, lanes = priors[0].shape
     vecs = finals[0].shape[0]
     copies = [
         pltpu.make_async_copy(
@@ -328,26 +344,26 @@
     new_ref[0:early] = (early_mine[...] + early_got[...]) * scale
     new_ref[early] = ((lates[0][...] + lates[1][...]) + (lates[2][...] + lates[3][...])) * scale
     half = even_ref.shape[0]
-    pairs = moments // 2
     flip = 7 - lax.broadcasted_iota(jnp.int32, (8, lanes), 0)
     for i in range(count):
         for h in range(halves):
             slot = i * halves + h
             rows = slice(i * group, (i + 1) * group)
             columns = slice(h * lanes, (h + 1) * lanes)
-            old = prior_ref.at[i, h].reshape(moments * group, lanes)
-            tail = (8 * 2 - steps) * group
-            fresh[slot, 0:tail] = jnp.zeros((tail, lanes), F32)
-            fresh[slot, tail:] = new_ref[:, rows, columns].reshape(steps * group, lanes)
+            for p in range(2):
+                fresh[slot, p, 0 : 8 - steps // 2] = jnp.zeros((8 - steps // 2, group, lanes), F32)
+                for m in range(p, steps, 2):
+                    fresh[slot, p, 8 - steps // 2 + m // 2] = new_ref[m, rows, columns]
             flat = held.at[slot].reshape(2 * half * group, lanes)
             for b in range(0, group, 2):
                 sums = []
                 for parity, table in ((0, even_ref), (1, odd_ref)):
                     pair = []
                     for j in range(2):
-                        start = parity * group + b + j
-                        value = old[pl.ds(start, pairs, stride=2 * group)]
-                        added = fresh[slot, pl.ds(start, 8, stride=2 * group)]
+                        old = priors[i].at[h, parity].reshape(pairs * group, lanes)
+                        value = old[pl.ds(b + j, pairs, stride=group)]
+                        extra = fresh.at[slot, parity].reshape(8 * group, lanes)
+                        added = extra[pl.ds(b + j, 8, stride=group)]
                         pair.append(
                             jnp.concatenate([value[: pairs - 8], value[pairs - 8 :] + added], axis=0)
                         )
@@ -403,30 +419,28 @@
     rows = jax.ShapeDtypeStruct((rim, vecs * width), F32)
     full_shape = jax.ShapeDtypeStruct((vec_dev, blocks, width), F32)
     chunk_shape = jax.ShapeDtypeStruct((vecs, blocks, width), F32)
-    first = pl.pallas_call(
-        functools.partial(first_kernel, rim, vecs),
-        out_shape=[jax.ShapeDtypeStruct((2 * rim, 2 * blocks), BF16), full_shape]
-        + [rows] * (2 * chunks),
+    pick, cur_first, *sends = pl.pallas_call(
+        functools.partial(first_kernel, rim),
+        out_shape=[jax.ShapeDtypeStruct((2 * rim, 2 * blocks), BF16), chunk_shape, rows, rows],
         in_specs=[smem(), hbm(), hbm()],
-        out_specs=[vmem()] * (2 + 2 * chunks),
+        out_specs=[vmem()] * 4,
         scratch_shapes=[
             pltpu.VMEM(send_lists.shape, jnp.int32),
-            pltpu.SemaphoreType.DMA((vec_dev + 1,)),
+            pltpu.SemaphoreType.DMA((vecs + 1,)),
         ],
         compiler_params=params(),
         cost_estimate=cost(1e8, 1e6),
         name="first_sends",
     )(index, stay(send_lists), stay(cheb_cur))
-    pick, cur_held, sends = first[0], first[1], list(first[2:])
 
     def exchange(a, b):
+        got_a = lax.ppermute(a, "dom", swap_a)
         got_b = lax.ppermute(b, "dom", swap_b)
-        got_a = lax.ppermute(a, "dom", swap_a)
         return got_a, got_b
 
-    received = [exchange(sends[2 * c], sends[2 * c + 1]) for c in range(chunks)]
-
-    mix, high, low, prev_held, probe_held, site_held = pl.pallas_call(
+    received = [exchange(*sends)]
+    links = tile_cols.shape[1]
+    mix, high, low, prev_held, probe_held, site_held, cur_second, *sends = pl.pallas_call(
         functools.partial(prep_kernel, rim),
         out_shape=[
             jax.ShapeDtypeStruct((kind_count * blocks, 2 * padded), BF16),
@@ -435,28 +449,32 @@
             full_shape,
             full_shape,
             jax.ShapeDtypeStruct(site_terms.shape, F32),
+            chunk_shape,
+            rows,
+            rows,
         ],
-        in_specs=[smem()] + [hbm()] * 6,
-        out_specs=[vmem()] * 6,
+        in_specs=[smem(), hbm(), hbm(), vmem()] + [hbm()] * 5,
+        out_specs=[vmem()] * 9,
         scratch_shapes=[
-            pltpu.VMEM(tile_cols.shape[::-1], jnp.int32),
-            pltpu.VMEM(tile_cols.shape[::-1], jnp.int32),
+            pltpu.VMEM((links, blocks), jnp.int32),
+            pltpu.VMEM((links, blocks), jnp.int32),
             pltpu.VMEM(hop_kinds.shape, F32),
-            pltpu.SemaphoreType.DMA((kind_count + 5,)),
+            pltpu.SemaphoreType.DMA((kind_count + 5 + vecs,)),
         ],
         compiler_params=params(),
         cost_estimate=cost(1e7, 8e6),
         name="tables",
     )(
         index,
-        *[
-            stay(x)
-            for x in (tile_cols.T, tile_kind_ids.T, hop_kinds, cheb_prev, probe, site_terms)
-        ],
+        stay(tile_cols.T),
+        stay(tile_kind_ids.T),
+        pick,
+        *[stay(x) for x in (hop_kinds, cheb_cur, cheb_prev, probe, site_terms)],
     )
+    received.append(exchange(*sends))
 
     partial_shape = jax.ShapeDtypeStruct((blocks, width), F32)
-    current = [(cur_held, c * vecs) for c in range(chunks)]
+    current = [(cur_first, 0), (cur_second, 0)]
     previous = [(prev_held, c * vecs) for c in range(chunks)]
 
     def reduce(keep, give):
@@ -475,6 +493,8 @@
 
     partials = []
     buffers = []
+    prior_held = []
+    prior_pairs = prior_moments.reshape(prior_moments.shape[0] // 2, 2, quarter, width)
     for s in range(STEPS):
         last = s == STEPS - 1
         partial = None
@@ -487,9 +507,10 @@
             extra = ([] if partial is None else [partial]) + partials[:older]
             args += extra
             specs += [vmem()] * len(extra)
-            fetch = s == STEPS - 2 and c == 0
-            if fetch:
-                args.append(stay(prior_moments))
+            place = s * chunks + c
+            fetch = place if place < quarter // group else None
+            if fetch is not None:
+                args.append(stay(prior_pairs))
                 specs.append(hbm())
             aliases = {len(args) + i: 2 + i for i in range(len(buffers))}
             args += buffers
@@ -509,13 +530,11 @@
                 outs += [jax.ShapeDtypeStruct((quarter, width), F32)] * 4
             elif fold:
                 outs += [jax.ShapeDtypeStruct((older + 1, groups // 2, quarter, width), F32)] * 2
-            if fetch:
+            if fetch is not None:
                 outs.append(
-                    jax.ShapeDtypeStruct(
-                        (quarter // group, width // lanes, moment_count, group, lanes), F32
-                    )
+                    jax.ShapeDtypeStruct((width // lanes, 2, moment_count // 2, group, lanes), F32)
                 )
-                scratch.append(pltpu.SemaphoreType.DMA((quarter // group * (width // lanes),)))
+                scratch.append(pltpu.SemaphoreType.DMA((2 * (width // lanes),)))
             out_specs += [vmem()] * (len(outs) - len(out_specs))
             cfg = (
                 vecs,
@@ -537,7 +556,7 @@
                     out_specs=out_specs,
                     scratch_shapes=scratch,
                     input_output_aliases=aliases,
-                    compiler_params=params(),
+                    compiler_params=pltpu.CompilerParams(vmem_limit_bytes=VMEM_LIMIT),
                     cost_estimate=cost(1.5e9, 5e6),
                 )(*args)
             )
@@ -547,8 +566,8 @@
                 buffers = [result.pop(0)]
             else:
                 received[c] = exchange(result.pop(0), result.pop(0))
-            if fetch:
-                prior_held = result.pop(0)
+            if fetch is not None:
+                prior_held.append(result.pop(0))
             if fold and last:
                 lates = [result[0]]
                 for flip in (2, 3, 1):
@@ -560,9 +579,9 @@
 
     tables = [jnp.asarray(x) for x in jackson_split(moment_count, ENERGIES)]
     tiles = quarter // group * (width // lanes)
-    args = [*tables, prior_held, *early, *lates, *[current[c][0] for c in range(chunks)]]
+    args = [*tables, *early, *prior_held, *lates, *[current[c][0] for c in range(chunks)]]
     new_moments, energy_map, next_cur = pl.pallas_call(
-        functools.partial(energy_kernel, vec_dev * groups, chunks),
+        functools.partial(energy_kernel, vec_dev * groups, chunks, len(prior_held)),
         out_shape=[
             jax.ShapeDtypeStruct((STEPS, quarter, width), F32),
             jax.ShapeDtypeStruct((ENERGIES, quarter, width), F32),
@@ -571,7 +590,7 @@
         in_specs=[vmem()] * len(args),
         out_specs=[vmem(), any_space(), any_space()],
         scratch_shapes=[
-            pltpu.VMEM((tiles, 16 * group, lanes), F32),
+            pltpu.VMEM((tiles, 2, 8, group, lanes), F32),
             pltpu.VMEM((tiles, ENERGIES, group, lanes), F32),
             pltpu.SemaphoreType.DMA((tiles + chunks,)),
         ],

time: 76.7 us -> 77.6 us (1.012)
  Pallas kernels: 41.5 us -> 44.1 us
  starting transfers between devices: 30 us -> 28.9 us
    pallas_call x8, Pallas kernels: 28.7 us -> 31.5 us  [per_device(): pl.pallas_call(functools.partial(step_kernel, cfg), out_shape=outs, in_sp...]
    ppermute x8, starting transfers between devices: 20.8 us -> 19.1 us  [exchange(): got_b = lax.ppermute(b, 'dom', swap_b)]
  transfers between devices with their start and end apart: 21 -> 21, of which waited for: 3 -> 3; matrix products, arithmetic and copies ran while one was open for 0% -> 0% of each run, Pallas kernels for 42% -> 45%
where the time goes in v4:
time: 77.6 us; the launch traced here: 77.4 us
  Pallas kernels  44.1 us (57%)
  starting transfers between devices  28.9 us (37%)
  waiting for transfers between devices  3.38 us (4%)
  between operations  0.97 us (1%)
    pallas_call x8, Pallas kernels, per_device(): pl.pallas_call(functools.partial(step_kernel, cfg), out_shape=outs, in_sp...  31.5 us
    ppermute x8, starting transfers between devices, exchange(): got_b = lax.ppermute(b, 'dom', swap_b)  19.1 us
    pallas_call x1, Pallas kernels, per_device(): pl.pallas_call(functools.partial(energy_kernel, vec_dev * groups, chunks,...  7.28 us
    ppermute x8, starting transfers between devices, exchange(): got_a = lax.ppermute(a, 'dom', swap_a)  6.02 us
    pallas_call x1, Pallas kernels, per_device(): pl.pallas_call(functools.partial(prep_kernel, rim), out_shape=[jax.ShapeD...  2.89 us
    ppermute x3, waiting for transfers between devices, per_device(): lates.append(lax.ppermute(result[flip], 'vec', pairs))  2.72 us
    ppermute x3, starting transfers between devices, per_device(): lates.append(lax.ppermute(result[flip], 'vec', pairs))  2.21 us
    pallas_call x1, Pallas kernels, per_device(): pl.pallas_call(functools.partial(first_kernel, rim), out_shape=[jax.Shape...  1.84 us
  transfers between devices with their start and end apart: 21, of which 3 were waited for; matrix products, arithmetic and copies ran while one was open for 0% of the time, Pallas kernels for 45%

profile of v4, /device:TPU:0, one launch (start us, length us, event | category | flops | bytes accessed | tf_op | source)
XLA Modules:
  0.0 77.4 jit_solution(11430004071301068725)
XLA Ops:
  0.7 1.8 %first_sends.1 = (bf16[96,256]{1,0:T(8,128)(2,1)S(1)}, f32[2,128,256]{2,1,0:T(8,128)S(1)}, f32[48,512]{1,0:T(8,128)S(1)}, f32[48,512]{1,0:T(8,128)S(1)}) custom-call(s32[3]{0:T(128)S(1)} %pad_add_fusion.index_ref, s32[1,2,48]{2,1,0:T(2,128)} %lists_hbm.1, f32[4,128,256]{2,1,0:T(8,128)} %cur_hbm.3), custom_call_target="tpu_custom_call" | custom-call | flops 100000000 | bytes 1000000 | tf_op jit(solution)/shard_map/first_sends/pallas_call | solution.py:422
  2.6 3.0 %collective-permute-start.2 = (f32[48,512]{1,0:T(8,128)S(1)}, f32[48,512]{1,0:T(8,128)S(1)}, u32[]{:S(2)}, u32[]{:S(2)}) collective-permute-start(f32[48,512]{1,0:T(8,128)S(1)} %get-tuple-element.71), channel_id=1, source_target_pairs={{0,1},{1,0},{2,3},{3,2},{4,5},{5,4},{6,7},{7,6},{8,9},{9,8},{10,11... | collective-permute-start | bytes 294920 | tf_op jit(solution)/shard_map/ppermute | solution.py:437
  5.6 3.6 %collective-permute-start.3 = (f32[48,512]{1,0:T(8,128)S(1)}, f32[48,512]{1,0:T(8,128)S(1)}, u32[]{:S(2)}, u32[]{:S(2)}) collective-permute-start(f32[48,512]{1,0:T(8,128)S(1)} %get-tuple-element.72), channel_id=1, source_target_pairs={{0,7},{1,2},{2,1},{3,4},{4,3},{5,6},{6,5},{7,0},{8,15},{9,10},{10,... | collective-permute-start | bytes 294920 | tf_op jit(solution)/shard_map/ppermute | solution.py:438
  9.2 2.9 %tables.1 = (bf16[1024,512]{1,0:T(8,128)(2,1)S(1)}, bf16[2048,256]{1,0:T(8,128)(2,1)S(1)}, bf16[2048,256]{1,0:T(8,128)(2,1)S(1)}, f32[4,128,256]{2,1,0:T(8,128)S...) custom-call(s32[3]{0:T(128)S(1)} %pad_add_fusion.index_ref, ...), custom_call_target="tpu_custom_call" | custom-call | flops 10000000 | bytes 8000000 | tf_op jit(solution)/shard_map/tables/pallas_call | solution.py:443
  12.2 1.9 %collective-permute-start.1 = (f32[48,512]{1,0:T(8,128)S(1)}, f32[48,512]{1,0:T(8,128)S(1)}, u32[]{:S(2)}, u32[]{:S(2)}) collective-permute-start(f32[48,512]{1,0:T(8,128)S(1)} %get-tuple-element.69), channel_id=1, source_target_pairs={{0,7},{1,2},{2,1},{3,4},{4,3},{5,6},{6,5},{7,0},{8,15},{9,10},{10,... | collective-permute-start | bytes 294920 | tf_op jit(solution)/shard_map/ppermute | solution.py:438
  14.1 4.4 %shard_map.138 = (f32[2,128,256]{2,1,0:T(8,128)S(1)}, f32[128,256]{1,0:T(8,128)S(1)}, f32[48,512]{1,0:T(8,128)S(1)}, f32[48,512]{1,0:T(8,128)S(1)}, f32[2,2,64,8,128]{4,3,2,1,0:T(8,128)S(1)}) custom-call(s32[3]{0:T(128)S(1)} %pad_add_fusion.index_ref, bf16[1024,512]{1,0:T(8,128)(2,1)S(1)} %get-tuple-element.61.mix_ref, ...), custom_call_target="tpu_custom_call" | custom-call | flops 1500000000 | bytes 5000000 | tf_op jit(solution)/shard_map/pallas_call | solution.py:552
  18.5 0.7 collective-permute-start.6
  19.1 2.4 %collective-permute-start.7 = (f32[48,512]{1,0:T(8,128)S(1)}, f32[48,512]{1,0:T(8,128)S(1)}, u32[]{:S(2)}, u32[]{:S(2)}) collective-permute-start(f32[48,512]{1,0:T(8,128)S(1)} %get-tuple-element.79), channel_id=1, source_target_pairs={{0,7},{1,2},{2,1},{3,4},{4,3},{5,6},{6,5},{7,0},{8,15},{9,10},{10,... | collective-permute-start | bytes 294920 | tf_op jit(solution)/shard_map/ppermute | solution.py:438
  21.5 4.4 %shard_map.139 = (f32[2,128,256]{2,1,0:T(8,128)S(1)}, f32[128,256]{1,0:T(8,128)S(1)}, f32[48,512]{1,0:T(8,128)S(1)}, f32[48,512]{1,0:T(8,128)S(1)}, f32[2,2,64,8,128]{4,3,2,1,0:T(8,128)S(1)}) custom-call(s32[3]{0:T(128)S(1)} %pad_add_fusion.index_ref, bf16[1024,512]{1,0:T(8,128)(2,1)S(1)} %get-tuple-element.61.mix_ref, ...), custom_call_target="tpu_custom_call" | custom-call | flops 1500000000 | bytes 5000000 | tf_op jit(solution)/shard_map/pallas_call | solution.py:552
  25.9 0.7 collective-permute-start.4
  26.7 1.8 %collective-permute-start.5 = (f32[48,512]{1,0:T(8,128)S(1)}, f32[48,512]{1,0:T(8,128)S(1)}, u32[]{:S(2)}, u32[]{:S(2)}) collective-permute-start(f32[48,512]{1,0:T(8,128)S(1)} %get-tuple-element.76), channel_id=1, source_target_pairs={{0,7},{1,2},{2,1},{3,4},{4,3},{5,6},{6,5},{7,0},{8,15},{9,10},{10,... | collective-permute-start | bytes 294920 | tf_op jit(solution)/shard_map/ppermute | solution.py:438
  28.4 4.4 %shard_map.140 = (f32[2,128,256]{2,1,0:T(8,128)S(1)}, f32[128,256]{1,0:T(8,128)S(1)}, f32[48,512]{1,0:T(8,128)S(1)}, f32[48,512]{1,0:T(8,128)S(1)}, f32[2,2,64,8,128]{4,3,2,1,0:T(8,128)S(1)}) custom-call(s32[3]{0:T(128)S(1)} %pad_add_fusion.index_ref, bf16[1024,512]{1,0:T(8,128)(2,1)S(1)} %get-tuple-element.61.mix_ref, ...), custom_call_target="tpu_custom_call" | custom-call | flops 1500000000 | bytes 5000000 | tf_op jit(solution)/shard_map/pallas_call | solution.py:552
  32.9 3.5 %collective-permute-start.11 = (f32[48,512]{1,0:T(8,128)S(1)}, f32[48,512]{1,0:T(8,128)S(1)}, u32[]{:S(2)}, u32[]{:S(2)}) collective-permute-start(f32[48,512]{1,0:T(8,128)S(1)} %get-tuple-element.86), channel_id=1, source_target_pairs={{0,7},{1,2},{2,1},{3,4},{4,3},{5,6},{6,5},{7,0},{8,15},{9,10},{10,... | collective-permute-start | bytes 294920 | tf_op jit(solution)/shard_map/ppermute | solution.py:438
  36.4 4.4 %shard_map.141 = (f32[2,128,256]{2,1,0:T(8,128)S(1)}, f32[128,256]{1,0:T(8,128)S(1)}, f32[48,512]{1,0:T(8,128)S(1)}, f32[48,512]{1,0:T(8,128)S(1)}, f32[2,2,64,8,128]{4,3,2,1,0:T(8,128)S(1)}) custom-call(s32[3]{0:T(128)S(1)} %pad_add_fusion.index_ref, bf16[1024,512]{1,0:T(8,128)(2,1)S(1)} %get-tuple-element.61.mix_ref, ...), custom_call_target="tpu_custom_call" | custom-call | flops 1500000000 | bytes 5000000 | tf_op jit(solution)/shard_map/pallas_call | solution.py:552
  40.8 0.1 collective-permute-start.8
  41.0 1.8 %collective-permute-start.9 = (f32[48,512]{1,0:T(8,128)S(1)}, f32[48,512]{1,0:T(8,128)S(1)}, u32[]{:S(2)}, u32[]{:S(2)}) collective-permute-start(f32[48,512]{1,0:T(8,128)S(1)} %get-tuple-element.83), channel_id=1, source_target_pairs={{0,7},{1,2},{2,1},{3,4},{4,3},{5,6},{6,5},{7,0},{8,15},{9,10},{10,... | collective-permute-start | bytes 294920 | tf_op jit(solution)/shard_map/ppermute | solution.py:438
  42.8 3.2 %shard_map.142 = (f32[2,128,256]{2,1,0:T(8,128)S(1)}, f32[128,256]{1,0:T(8,128)S(1)}, f32[48,512]{1,0:T(8,128)S(1)}, f32[48,512]{1,0:T(8,128)S(1)}) custom-call(s32[3]{0:T(128)S(1)} %pad_add_fusion.index_ref, bf16[1024,512]{1,0:T(8,128)(2,1)S(1)} %get-tuple-element.61.mix_ref, bf16[2048,256]{1,0:T(8,128)(2,1)S(1)} %get-tuple-element.62.high_ref, ...), custom_call_target="tpu_custom_call" | custom-call | flops 1500000000 | bytes 5000000 | tf_op jit(solution)/shard_map/pallas_call | solution.py:552
  46.0 0.7 collective-permute-start.14
  46.7 2.4 %collective-permute-start.15 = (f32[48,512]{1,0:T(8,128)S(1)}, f32[48,512]{1,0:T(8,128)S(1)}, u32[]{:S(2)}, u32[]{:S(2)}) collective-permute-start(f32[48,512]{1,0:T(8,128)S(1)} %get-tuple-element.95), channel_id=1, source_target_pairs={{0,7},{1,2},{2,1},{3,4},{4,3},{5,6},{6,5},{7,0},{8,15},{9,10},{10,... | collective-permute-start | bytes 294920 | tf_op jit(solution)/shard_map/ppermute | solution.py:438
  49.1 3.9 %shard_map.143 = (f32[2,128,256]{2,1,0:T(8,128)S(1)}, f32[128,256]{1,0:T(8,128)}, f32[48,512]{1,0:T(8,128)S(1)}, f32[48,512]{1,0:T(8,128)S(1)}, f32[3,2,32,256]{...) custom-call(s32[3]{0:T(128)S(1)} %pad_add_fusion.index_ref, bf16[1024,512]{1,0:T(8,128)(2,1)S(1)} %get-tuple-element.61.mix_ref, ...), custom_call_target="tpu_custom_call" | custom-call | flops 1500000000 | bytes 5000000 | tf_op jit(solution)/shard_map/pallas_call | solution.py:552
  53.0 0.7 collective-permute-start.12
  53.6 1.8 %collective-permute-start.13 = (f32[48,512]{1,0:T(8,128)S(1)}, f32[48,512]{1,0:T(8,128)S(1)}, u32[]{:S(2)}, u32[]{:S(2)}) collective-permute-start(f32[48,512]{1,0:T(8,128)S(1)} %get-tuple-element.92), channel_id=1, source_target_pairs={{0,7},{1,2},{2,1},{3,4},{4,3},{5,6},{6,5},{7,0},{8,15},{9,10},{10,... | collective-permute-start | bytes 294920 | tf_op jit(solution)/shard_map/ppermute | solution.py:438
  55.4 3.0 %shard_map.144 = (f32[2,128,256]{2,1,0:T(8,128)S(1)}, f32[128,256]{1,0:T(8,128)S(1)}, f32[4,128,256]{2,1,0:T(8,128)}) custom-call(s32[3]{0:T(128)S(1)} %pad_add_fusion.index_ref, bf16[1024,512]{1,0:T(8,128)(2,1)S(1)} %get-tuple-element.61.mix_ref, bf16[2048,256]{1,0:T(8,128)(2,1)S(1)} %get-tuple-element.62.high_ref, ...), custom_call_target="tpu_custom_call" | custom-call | flops 1500000000 | bytes 5000000 | tf_op jit(solution)/shard_map/pallas_call | solution.py:552
  58.5 0.6 fold.1
  59.1 1.6 %collective-permute-start.17 = (f32[3,32,256]{2,1,0:T(8,128)S(1)}, f32[3,32,256]{2,1,0:T(8,128)S(1)}, u32[]{:S(2)}, u32[]{:S(2)}) collective-permute-start(f32[3,32,256]{2,1,0:T(8,128)S(1)} %get-tuple-element.102), channel_id=1, source_target_pairs={{0,16},{8,24},{16,0},{24,8},{1,17},{9,25},{17,1},{25,9},{2,18},{10... | collective-permute-start | bytes 294920 | tf_op jit(solution)/shard_map/ppermute | solution.py:492
  60.6 0.6 collective-permute-done.13.recv_b
  61.3 3.7 %shard_map.145 = (f32[2,128,256]{2,1,0:T(8,128)S(1)}, f32[128,256]{1,0:T(8,128)}, f32[4,128,256]{2,1,0:T(8,128)}, f32[32,256]{1,0:T(8,128)S(1)}, f32[32,256]{1,0...) custom-call(s32[3]{0:T(128)S(1)} %pad_add_fusion.index_ref, ...), custom_call_target="tpu_custom_call", output_to_operand_aliasing={{2}: (12, {})} | custom-call | flops 1500000000 | bytes 5000000 | tf_op jit(solution)/shard_map/pallas_call | solution.py:552
  65.0 1.6 %collective-permute-start.18 = (f32[32,256]{1,0:T(8,128)S(1)}, f32[32,256]{1,0:T(8,128)S(1)}, u32[]{:S(2)}, u32[]{:S(2)}) collective-permute-start(f32[32,256]{1,0:T(8,128)S(1)} %get-tuple-element.108), channel_id=1, source_target_pairs={{0,16},{8,24},{16,0},{24,8},{1,17},{9,25},{17,1},{25,9},{2,18},{10... | collective-permute-start | bytes 98312 | tf_op jit(solution)/shard_map/ppermute | solution.py:575
  66.6 0.6 collective-permute-start.20
  67.2 1.8 %collective-permute-done.18.rest_5_ = f32[32,256]{1,0:T(8,128)S(1)} collective-permute-done((f32[32,256]{1,0:T(8,128)S(1)}, f32[32,256]{1,0:T(8,128)S(1)}, u32[]{:S(2)}, u32[]{:S(2)}) %collective-permute-start.18) | collective-permute-done | bytes 32800 | tf_op jit(solution)/shard_map/ppermute | solution.py:575
  69.0 0.9 %collective-permute-done.19.rest_6_ = f32[32,256]{1,0:T(8,128)S(1)} collective-permute-done((f32[32,256]{1,0:T(8,128)S(1)}, f32[32,256]{1,0:T(8,128)S(1)}, u32[]{:S(2)}, u32[]{:S(2)}) %collective-permute-start.19) | collective-permute-done | bytes 32800 | tf_op jit(solution)/shard_map/ppermute | solution.py:575
  69.9 7.3 %energy.1 = (f32[4,32,256]{2,1,0:T(8,128)}, f32[512,32,256]{2,1,0:T(8,128)}, f32[4,128,256]{2,1,0:T(8,128)}) custom-call(bf16[256,256]{1,0:T(8,128)(2,1)S(1)} %copy-done.1, bf16[256,256]{1,0:T(8,128)(2,1)S(1)} %copy-done, f32[3,32,256]{2,1,0:T(8,128)S(1)} %get-tuple-element.101.early_mine, f32[3,32,256]{2,1,0:T(8,128)S(1)} %collective-permute-done.17.early_got, ...), custom_call_target="tpu_custom_call" | custom-call | flops 4000000000 | bytes 22000000 | tf_op jit(solution)/shard_map/energy/pallas_call | solution.py:583
  (27 shorter events, 0.3 us)
Async XLA Ops:
  2.6 11.5 %collective-permute-start.2 = (f32[48,512]{1,0:T(8,128)S(1)}, f32[48,512]{1,0:T(8,128)S(1)}, u32[]{:S(2)}, u32[]{:S(2)}) collective-permute-start(f32[48,512]{1,0:T(8,128)S(1)} %get-tuple-element.71), channel_id=1, source_target_pairs={{0,1},{1,0},{2,3},{3,2},{4,5},{5,4},{6,7},{7,6},{8,9},{9,8},{10,11... | collective-permute-start | bytes 294920 | tf_op jit(solution)/shard_map/ppermute | solution.py:437
  5.6 8.5 %collective-permute-start.3 = (f32[48,512]{1,0:T(8,128)S(1)}, f32[48,512]{1,0:T(8,128)S(1)}, u32[]{:S(2)}, u32[]{:S(2)}) collective-permute-start(f32[48,512]{1,0:T(8,128)S(1)} %get-tuple-element.72), channel_id=1, source_target_pairs={{0,7},{1,2},{2,1},{3,4},{4,3},{5,6},{6,5},{7,0},{8,15},{9,10},{10,... | collective-permute-start | bytes 294920 | tf_op jit(solution)/shard_map/ppermute | solution.py:438
  12.1 9.4 %collective-permute-start = (f32[48,512]{1,0:T(8,128)S(1)}, f32[48,512]{1,0:T(8,128)S(1)}, u32[]{:S(2)}, u32[]{:S(2)}) collective-permute-start(f32[48,512]{1,0:T(8,128)S(1)} %get-tuple-element.68), channel_id=1, source_target_pairs={{0,1},{1,0},{2,3},{3,2},{4,5},{5,4},{6,7},{7,6},{8,9},{9,8},{10,11... | collective-permute-start | bytes 294920 | tf_op jit(solution)/shard_map/ppermute | solution.py:437
  12.2 9.4 %collective-permute-start.1 = (f32[48,512]{1,0:T(8,128)S(1)}, f32[48,512]{1,0:T(8,128)S(1)}, u32[]{:S(2)}, u32[]{:S(2)}) collective-permute-start(f32[48,512]{1,0:T(8,128)S(1)} %get-tuple-element.69), channel_id=1, source_target_pairs={{0,7},{1,2},{2,1},{3,4},{4,3},{5,6},{6,5},{7,0},{8,15},{9,10},{10,... | collective-permute-start | bytes 294920 | tf_op jit(solution)/shard_map/ppermute | solution.py:438
  18.5 10.0 %collective-permute-start.6 = (f32[48,512]{1,0:T(8,128)S(1)}, f32[48,512]{1,0:T(8,128)S(1)}, u32[]{:S(2)}, u32[]{:S(2)}) collective-permute-start(f32[48,512]{1,0:T(8,128)S(1)} %get-tuple-element.78), channel_id=1, source_target_pairs={{0,1},{1,0},{2,3},{3,2},{4,5},{5,4},{6,7},{7,6},{8,9},{9,8},{10,11... | collective-permute-start | bytes 294920 | tf_op jit(solution)/shard_map/ppermute | solution.py:437
  19.1 9.3 %collective-permute-start.7 = (f32[48,512]{1,0:T(8,128)S(1)}, f32[48,512]{1,0:T(8,128)S(1)}, u32[]{:S(2)}, u32[]{:S(2)}) collective-permute-start(f32[48,512]{1,0:T(8,128)S(1)} %get-tuple-element.79), channel_id=1, source_target_pairs={{0,7},{1,2},{2,1},{3,4},{4,3},{5,6},{6,5},{7,0},{8,15},{9,10},{10,... | collective-permute-start | bytes 294920 | tf_op jit(solution)/shard_map/ppermute | solution.py:438
  25.9 10.5 %collective-permute-start.4 = (f32[48,512]{1,0:T(8,128)S(1)}, f32[48,512]{1,0:T(8,128)S(1)}, u32[]{:S(2)}, u32[]{:S(2)}) collective-permute-start(f32[48,512]{1,0:T(8,128)S(1)} %get-tuple-element.75), channel_id=1, source_target_pairs={{0,1},{1,0},{2,3},{3,2},{4,5},{5,4},{6,7},{7,6},{8,9},{9,8},{10,11... | collective-permute-start | bytes 294920 | tf_op jit(solution)/shard_map/ppermute | solution.py:437
  26.7 9.8 %collective-permute-start.5 = (f32[48,512]{1,0:T(8,128)S(1)}, f32[48,512]{1,0:T(8,128)S(1)}, u32[]{:S(2)}, u32[]{:S(2)}) collective-permute-start(f32[48,512]{1,0:T(8,128)S(1)} %get-tuple-element.76), channel_id=1, source_target_pairs={{0,7},{1,2},{2,1},{3,4},{4,3},{5,6},{6,5},{7,0},{8,15},{9,10},{10,... | collective-permute-start | bytes 294920 | tf_op jit(solution)/shard_map/ppermute | solution.py:438
  32.9 10.0 %collective-permute-start.10 = (f32[48,512]{1,0:T(8,128)S(1)}, f32[48,512]{1,0:T(8,128)S(1)}, u32[]{:S(2)}, u32[]{:S(2)}) collective-permute-start(f32[48,512]{1,0:T(8,128)S(1)} %get-tuple-element.85), channel_id=1, source_target_pairs={{0,1},{1,0},{2,3},{3,2},{4,5},{5,4},{6,7},{7,6},{8,9},{9,8},{10,11... | collective-permute-start | bytes 294920 | tf_op jit(solution)/shard_map/ppermute | solution.py:437
  32.9 9.9 %collective-permute-start.11 = (f32[48,512]{1,0:T(8,128)S(1)}, f32[48,512]{1,0:T(8,128)S(1)}, u32[]{:S(2)}, u32[]{:S(2)}) collective-permute-start(f32[48,512]{1,0:T(8,128)S(1)} %get-tuple-element.86), channel_id=1, source_target_pairs={{0,7},{1,2},{2,1},{3,4},{4,3},{5,6},{6,5},{7,0},{8,15},{9,10},{10,... | collective-permute-start | bytes 294920 | tf_op jit(solution)/shard_map/ppermute | solution.py:438
  40.8 8.2 %collective-permute-start.8 = (f32[48,512]{1,0:T(8,128)S(1)}, f32[48,512]{1,0:T(8,128)S(1)}, u32[]{:S(2)}, u32[]{:S(2)}) collective-permute-start(f32[48,512]{1,0:T(8,128)S(1)} %get-tuple-element.82), channel_id=1, source_target_pairs={{0,1},{1,0},{2,3},{3,2},{4,5},{5,4},{6,7},{7,6},{8,9},{9,8},{10,11... | collective-permute-start | bytes 294920 | tf_op jit(solution)/shard_map/ppermute | solution.py:437
  41.0 8.1 %collective-permute-start.9 = (f32[48,512]{1,0:T(8,128)S(1)}, f32[48,512]{1,0:T(8,128)S(1)}, u32[]{:S(2)}, u32[]{:S(2)}) collective-permute-start(f32[48,512]{1,0:T(8,128)S(1)} %get-tuple-element.83), channel_id=1, source_target_pairs={{0,7},{1,2},{2,1},{3,4},{4,3},{5,6},{6,5},{7,0},{8,15},{9,10},{10,... | collective-permute-start | bytes 294920 | tf_op jit(solution)/shard_map/ppermute | solution.py:438
  46.0 9.4 %collective-permute-start.14 = (f32[48,512]{1,0:T(8,128)S(1)}, f32[48,512]{1,0:T(8,128)S(1)}, u32[]{:S(2)}, u32[]{:S(2)}) collective-permute-start(f32[48,512]{1,0:T(8,128)S(1)} %get-tuple-element.94), channel_id=1, source_target_pairs={{0,1},{1,0},{2,3},{3,2},{4,5},{5,4},{6,7},{7,6},{8,9},{9,8},{10,11... | collective-permute-start | bytes 294920 | tf_op jit(solution)/shard_map/ppermute | solution.py:437
  46.7 8.7 %collective-permute-start.15 = (f32[48,512]{1,0:T(8,128)S(1)}, f32[48,512]{1,0:T(8,128)S(1)}, u32[]{:S(2)}, u32[]{:S(2)}) collective-permute-start(f32[48,512]{1,0:T(8,128)S(1)} %get-tuple-element.95), channel_id=1, source_target_pairs={{0,7},{1,2},{2,1},{3,4},{4,3},{5,6},{6,5},{7,0},{8,15},{9,10},{10,... | collective-permute-start | bytes 294920 | tf_op jit(solution)/shard_map/ppermute | solution.py:438
  53.0 5.5 %collective-permute-start.16 = (f32[3,2,32,256]{3,2,1,0:T(8,128)S(1)}, f32[3,2,32,256]{3,2,1,0:T(8,128)S(1)}, u32[]{:S(2)}, u32[]{:S(2)}) collective-permute-start(f32[3,2,32,256]{3,2,1,0:T(8,128)S(1)} %get-tuple-element.100), channel_id=1, source_target_pairs={{0,8},{8,0},{16,24},{24,16},{1,9},{9,1},{17,25},{25,17},{2,10},{10... | collective-permute-start | bytes 589832 | tf_op jit(solution)/shard_map/ppermute | solution.py:481
  53.0 7.7 %collective-permute-start.12 = (f32[48,512]{1,0:T(8,128)S(1)}, f32[48,512]{1,0:T(8,128)S(1)}, u32[]{:S(2)}, u32[]{:S(2)}) collective-permute-start(f32[48,512]{1,0:T(8,128)S(1)} %get-tuple-element.91), channel_id=1, source_target_pairs={{0,1},{1,0},{2,3},{3,2},{4,5},{5,4},{6,7},{7,6},{8,9},{9,8},{10,11... | collective-permute-start | bytes 294920 | tf_op jit(solution)/shard_map/ppermute | solution.py:437
  53.6 7.6 %collective-permute-start.13 = (f32[48,512]{1,0:T(8,128)S(1)}, f32[48,512]{1,0:T(8,128)S(1)}, u32[]{:S(2)}, u32[]{:S(2)}) collective-permute-start(f32[48,512]{1,0:T(8,128)S(1)} %get-tuple-element.92), channel_id=1, source_target_pairs={{0,7},{1,2},{2,1},{3,4},{4,3},{5,6},{6,5},{7,0},{8,15},{9,10},{10,... | collective-permute-start | bytes 294920 | tf_op jit(solution)/shard_map/ppermute | solution.py:438
  58.4 11.5 %copy-start = (bf16[256,256]{1,0:T(8,128)(2,1)S(1)}, bf16[256,256]{1,0:T(8,128)(2,1)}, u32[]{:S(2)}) copy-start(bf16[256,256]{1,0:T(8,128)(2,1)} %constant.41.clone.odd_ref) | copy-start | bytes 393220
  58.5 11.5 %copy-start.1 = (bf16[256,256]{1,0:T(8,128)(2,1)S(1)}, bf16[256,256]{1,0:T(8,128)(2,1)}, u32[]{:S(2)}) copy-start(bf16[256,256]{1,0:T(8,128)(2,1)} %constant.40.clone.even_ref) | copy-start | bytes 393220
  59.1 10.8 %collective-permute-start.17 = (f32[3,32,256]{2,1,0:T(8,128)S(1)}, f32[3,32,256]{2,1,0:T(8,128)S(1)}, u32[]{:S(2)}, u32[]{:S(2)}) collective-permute-start(f32[3,32,256]{2,1,0:T(8,128)S(1)} %get-tuple-element.102), channel_id=1, source_target_pairs={{0,16},{8,24},{16,0},{24,8},{1,17},{9,25},{17,1},{25,9},{2,18},{10... | collective-permute-start | bytes 294920 | tf_op jit(solution)/shard_map/ppermute | solution.py:492
  65.0 4.0 %collective-permute-start.18 = (f32[32,256]{1,0:T(8,128)S(1)}, f32[32,256]{1,0:T(8,128)S(1)}, u32[]{:S(2)}, u32[]{:S(2)}) collective-permute-start(f32[32,256]{1,0:T(8,128)S(1)} %get-tuple-element.108), channel_id=1, source_target_pairs={{0,16},{8,24},{16,0},{24,8},{1,17},{9,25},{17,1},{25,9},{2,18},{10... | collective-permute-start | bytes 98312 | tf_op jit(solution)/shard_map/ppermute | solution.py:575
  66.6 3.3 %collective-permute-start.19 = (f32[32,256]{1,0:T(8,128)S(1)}, f32[32,256]{1,0:T(8,128)S(1)}, u32[]{:S(2)}, u32[]{:S(2)}) collective-permute-start(f32[32,256]{1,0:T(8,128)S(1)} %get-tuple-element.109), channel_id=1, source_target_pairs={{0,24},{8,16},{16,8},{24,0},{1,25},{9,17},{17,9},{25,1},{2,26},{10... | collective-permute-start | bytes 98312 | tf_op jit(solution)/shard_map/ppermute | solution.py:575
  66.6 3.3 %collective-permute-start.20 = (f32[32,256]{1,0:T(8,128)S(1)}, f32[32,256]{1,0:T(8,128)S(1)}, u32[]{:S(2)}, u32[]{:S(2)}) collective-permute-start(f32[32,256]{1,0:T(8,128)S(1)} %get-tuple-element.110), channel_id=1, source_target_pairs={{0,8},{8,0},{16,24},{24,16},{1,9},{9,1},{17,25},{25,17},{2,10},{10... | collective-permute-start | bytes 98312 | tf_op jit(solution)/shard_map/ppermute | solution.py:575

commit v5 on v4

--- a/solution.py
+++ b/solution.py
@@ -48,16 +48,18 @@
     return pl.BlockSpec(memory_space=pltpu.VMEM)
 
 
-def smem():
-    return pl.BlockSpec(memory_space=pltpu.SMEM)
-
-
 def params(limit=VMEM_LIMIT):
     return pltpu.CompilerParams(vmem_limit_bytes=limit)
 
 
 def cost(flops, size):
     return pl.CostEstimate(flops=int(flops), bytes_accessed=int(size), transcendentals=0)
+
+
+def choose(index_ref, which, when_zero, when_one):
+    rows, width = when_zero.shape
+    bit = jnp.broadcast_to(index_ref[which, 0:1, 0:1], (rows, width))
+    return jnp.where(bit == 0, when_zero, when_one)
 
 
 def gather_rows(onehot, value):
@@ -93,14 +95,13 @@
         copy.start()
     list_copy.wait()
     lists = lists_ref[0]
-    even = index_ref[0] == 0
     rows = lax.broadcasted_iota(jnp.int32, (rim, rim), 0)
     lanes = lax.broadcasted_iota(jnp.int32, (rim, rim), 1)
     slots = lax.broadcasted_iota(jnp.int32, (rim, blocks), 1)
     for half in range(2):
         mine = lists[half : half + 1]
         other = lists[1 - half : 2 - half]
-        chosen = jnp.where(even, mine, other)
+        chosen = choose(index_ref, 0, mine, other)
         spread = jnp.where(rows == lanes, chosen, 0).astype(F32)
         column = jnp.sum(spread, axis=1, keepdims=True).astype(jnp.int32)
         onehot = jnp.where(slots == column, 1.0, 0.0).astype(BF16)
@@ -162,7 +163,6 @@
         copies.append(pltpu.make_async_copy(source, target, sems.at[kind_count + i]))
     for copy in copies:
         copy.start()
-    even = index_ref[0] == 0
     rows = lax.broadcasted_iota(jnp.int32, (padded, blocks), 0)
     corner = lax.broadcasted_iota(jnp.int32, (blocks, blocks), 0)
     diagonal = corner == lax.broadcasted_iota(jnp.int32, (blocks, blocks), 1)
@@ -171,7 +171,7 @@
         copy.wait()
     e = cols_ref[...]
     crossed = jnp.where(e < blocks + rim, e + rim, e - rim)
-    e = jnp.where(jnp.logical_and(even, e >= blocks), crossed, e)
+    e = choose(index_ref, 0, jnp.where(e >= blocks, crossed, e), e)
     ids = ids_ref[...]
     for n in range(kind_count):
         mine = jnp.where(ids == n, e, -1)
@@ -295,33 +295,31 @@
             columns = slice(v * width, (v + 1) * width)
             emit_sends(pick_ref[...], following, columns, send_a, send_b)
     partial_out[...] = partial
-    if fold and last:
-        quarter = pieces_out[0].shape[0]
-        for flip, piece in enumerate(pieces_out):
-            core = index_ref[1] if flip % 2 == 0 else 1 - index_ref[1]
-            chip = index_ref[2] if flip < 2 else 1 - index_ref[2]
-            at = pl.multiple_of((2 * chip + core) * quarter, quarter)
-            piece[...] = partial_out[pl.ds(at, quarter)]
-    elif fold:
-        cores = 2
-        quarter = keep_ref.shape[2]
-        core = index_ref[1]
+    if fold:
+        quarter = blocks // 4
         for s in range(older + 1):
             ref = olders[s] if s < older else partial_out
-            for y in range(keep_ref.shape[1]):
-                base = y * cores * quarter
-                keep_ref[s, y] = ref[pl.ds(pl.multiple_of(base + core * quarter, quarter), quarter)]
-                give_ref[s, y] = ref[
-                    pl.ds(pl.multiple_of(base + (1 - core) * quarter, quarter), quarter)
-                ]
+            parts = [ref[i * quarter : (i + 1) * quarter] for i in range(4)]
+            keep = [choose(index_ref, 1, *parts[2 * y : 2 * y + 2]) for y in range(2)]
+            give = [choose(index_ref, 1, *parts[2 * y : 2 * y + 2][::-1]) for y in range(2)]
+            if last:
+                pieces_out[0][...] = choose(index_ref, 2, *keep)
+                pieces_out[1][...] = choose(index_ref, 2, *give)
+                pieces_out[2][...] = choose(index_ref, 2, *keep[::-1])
+                pieces_out[3][...] = choose(index_ref, 2, *give[::-1])
+            else:
+                for y in range(2):
+                    keep_ref[s, y] = keep[y]
+                    give_ref[s, y] = give[y]
     for copy in copies:
         copy.wait()
 
 
 def fold_kernel(index_ref, keep_ref, got_ref, mine_ref, give_ref):
-    y = index_ref[2]
-    mine_ref[...] = keep_ref[:, y] + got_ref[:, y]
-    give_ref[...] = keep_ref[:, 1 - y] + got_ref[:, 1 - y]
+    for s in range(keep_ref.shape[0]):
+        sums = [keep_ref[s, y] + got_ref[s, y] for y in range(2)]
+        mine_ref[s] = choose(index_ref, 2, *sums)
+        give_ref[s] = choose(index_ref, 2, *sums[::-1])
 
 
 def energy_kernel(vector_total, chunks, count, even_ref, odd_ref, early_mine, early_got, *rest):
@@ -415,6 +413,7 @@
     swap_b = [(i, (i + 1) % domains if i % 2 else (i - 1) % domains) for i in range(domains)]
     vec_index = lax.axis_index("vec")
     index = jnp.stack([lax.axis_index("dom") % 2, vec_index % 2, vec_index // 2]).astype(jnp.int32)
+    index = jnp.broadcast_to(index[:, None, None], (3, 8, 128))
 
     rows = jax.ShapeDtypeStruct((rim, vecs * width), F32)
     full_shape = jax.ShapeDtypeStruct((vec_dev, blocks, width), F32)
@@ -422,7 +421,7 @@
     pick, cur_first, *sends = pl.pallas_call(
         functools.partial(first_kernel, rim),
         out_shape=[jax.ShapeDtypeStruct((2 * rim, 2 * blocks), BF16), chunk_shape, rows, rows],
-        in_specs=[smem(), hbm(), hbm()],
+        in_specs=[vmem(), hbm(), hbm()],
         out_specs=[vmem()] * 4,
         scratch_shapes=[
             pltpu.VMEM(send_lists.shape, jnp.int32),
@@ -453,7 +452,7 @@
             rows,
             rows,
         ],
-        in_specs=[smem(), hbm(), hbm(), vmem()] + [hbm()] * 5,
+        in_specs=[vmem(), hbm(), hbm(), vmem()] + [hbm()] * 5,
         out_specs=[vmem()] * 9,
         scratch_shapes=[
             pltpu.VMEM((links, blocks), jnp.int32),
@@ -483,8 +482,8 @@
         mine, give = pl.pallas_call(
             fold_kernel,
             out_shape=[piece, piece],
-            in_specs=[smem(), vmem(), vmem()],
-            out_specs=[vmem(), vmem()],
+            in_specs=[vmem()] * 3,
+            out_specs=[vmem()] * 2,
             compiler_params=params(),
             cost_estimate=cost(1e5, 1e6),
             name="fold",
@@ -501,7 +500,7 @@
         for c in range(chunks):
             args = [index, mix, high, low, pick, site_held]
             args += [current[c][0], previous[c][0], probe_held, *received[c]]
-            specs = [smem()] + [vmem()] * (len(args) - 1)
+            specs = [vmem()] * len(args)
             fold = c == chunks - 1 and s >= STEPS - 2
             older = 0 if last or not fold else len(partials)
             extra = ([] if partial is None else [partial]) + partials[:older]

time: 77.6 us -> 73.1 us (0.942)
  Pallas kernels: 44.1 us -> 38.3 us
  waiting for transfers between devices: 3.38 us -> 4.92 us
    pallas_call x8, Pallas kernels: 31.5 us -> 27.2 us  [per_device(): pl.pallas_call(functools.partial(step_kernel, cfg), out_shape=outs, in_sp...]
    ppermute x8, waiting for transfers between devices: 0.63 us -> 2.16 us  [exchange(): got_b = lax.ppermute(b, 'dom', swap_b)]
  transfers between devices with their start and end apart: 21 -> 21, of which waited for: 3 -> 4; matrix products, arithmetic and copies ran while one was open for 0% -> 0% of each run, Pallas kernels for 45% -> 41%
where the time goes in v5:
time: 73.1 us; the launch traced here: 72.9 us
  Pallas kernels  38.3 us (52%)
  starting transfers between devices  28.5 us (39%)
  waiting for transfers between devices  4.92 us (7%)
  between operations  0.97 us (1%)
    pallas_call x8, Pallas kernels, per_device(): pl.pallas_call(functools.partial(step_kernel, cfg), out_shape=outs, in_sp...  27.2 us
    ppermute x8, starting transfers between devices, exchange(): got_b = lax.ppermute(b, 'dom', swap_b)  18.9 us
    pallas_call x1, Pallas kernels, per_device(): pl.pallas_call(functools.partial(energy_kernel, vec_dev * groups, chunks,...  7.29 us
    ppermute x8, starting transfers between devices, exchange(): got_a = lax.ppermute(a, 'dom', swap_a)  5.79 us
    ppermute x3, waiting for transfers between devices, per_device(): lates.append(lax.ppermute(result[flip], 'vec', pairs))  2.73 us
    pallas_call x1, Pallas kernels, per_device(): pl.pallas_call(functools.partial(prep_kernel, rim), out_shape=[jax.ShapeD...  2.48 us
    ppermute x3, starting transfers between devices, per_device(): lates.append(lax.ppermute(result[flip], 'vec', pairs))  2.21 us
    ppermute x8, waiting for transfers between devices, exchange(): got_b = lax.ppermute(b, 'dom', swap_b)  2.16 us
  transfers between devices with their start and end apart: 21, of which 4 were waited for; matrix products, arithmetic and copies ran while one was open for 0% of the time, Pallas kernels for 41%

profile of v5, /device:TPU:0, one launch (start us, length us, event | category | flops | bytes accessed | tf_op | source)
XLA Modules:
  0.0 72.9 jit_solution(7368161675447227052)
XLA Ops:
  0.8 1.3 %first_sends.1 = (bf16[96,256]{1,0:T(8,128)(2,1)S(1)}, f32[2,128,256]{2,1,0:T(8,128)S(1)}, f32[48,512]{1,0:T(8,128)S(1)}, f32[48,512]{1,0:T(8,128)S(1)}) custom-call(s32[3,8,128]{2,1,0:T(8,128)S(1)} %broadcast_in_dim.2.index_ref, s32[1,2,48]{2,1,0:T(2,128)} %lists_hbm.1, f32[4,128,256]{2,1,0:T(8,128)} %cur_hbm.3), custom_call_target="tpu_custom_call" | custom-call | flops 100000000 | bytes 1000000 | tf_op jit(solution)/shard_map/first_sends/pallas_call | solution.py:421
  2.1 3.0 %collective-permute-start.2 = (f32[48,512]{1,0:T(8,128)S(1)}, f32[48,512]{1,0:T(8,128)S(1)}, u32[]{:S(2)}, u32[]{:S(2)}) collective-permute-start(f32[48,512]{1,0:T(8,128)S(1)} %get-tuple-element.71), channel_id=1, source_target_pairs={{0,1},{1,0},{2,3},{3,2},{4,5},{5,4},{6,7},{7,6},{8,9},{9,8},{10,11... | collective-permute-start | bytes 294920 | tf_op jit(solution)/shard_map/ppermute | solution.py:436
  5.1 3.6 %collective-permute-start.3 = (f32[48,512]{1,0:T(8,128)S(1)}, f32[48,512]{1,0:T(8,128)S(1)}, u32[]{:S(2)}, u32[]{:S(2)}) collective-permute-start(f32[48,512]{1,0:T(8,128)S(1)} %get-tuple-element.72), channel_id=1, source_target_pairs={{0,7},{1,2},{2,1},{3,4},{4,3},{5,6},{6,5},{7,0},{8,15},{9,10},{10,... | collective-permute-start | bytes 294920 | tf_op jit(solution)/shard_map/ppermute | solution.py:437
  8.7 2.5 %tables.1 = (bf16[1024,512]{1,0:T(8,128)(2,1)S(1)}, bf16[2048,256]{1,0:T(8,128)(2,1)S(1)}, bf16[2048,256]{1,0:T(8,128)(2,1)S(1)}, f32[4,128,256]{2,1,0:T(8,128)S...) custom-call(s32[3,8,128]{2,1,0:T(8,128)S(1)} %broadcast_in_dim.2.ind, ...), custom_call_target="tpu_custom_call" | custom-call | flops 10000000 | bytes 8000000 | tf_op jit(solution)/shard_map/tables/pallas_call | solution.py:442
  11.3 1.9 %collective-permute-start.1 = (f32[48,512]{1,0:T(8,128)S(1)}, f32[48,512]{1,0:T(8,128)S(1)}, u32[]{:S(2)}, u32[]{:S(2)}) collective-permute-start(f32[48,512]{1,0:T(8,128)S(1)} %get-tuple-element.69), channel_id=1, source_target_pairs={{0,7},{1,2},{2,1},{3,4},{4,3},{5,6},{6,5},{7,0},{8,15},{9,10},{10,... | collective-permute-start | bytes 294920 | tf_op jit(solution)/shard_map/ppermute | solution.py:437
  13.2 3.9 %shard_map.138 = (f32[2,128,256]{2,1,0:T(8,128)S(1)}, f32[128,256]{1,0:T(8,128)S(1)}, f32[48,512]{1,0:T(8,128)S(1)}, f32[48,512]{1,0:T(8,128)S(1)}, f32[2,2,64,8,128]{4,3,2,1,0:T(8,128)S(1)}) custom-call(s32[3,8,128]{2,1,0:T(8,128)S(1)} %broadcast_in_dim.2.index_ref, bf16[1024,512]{1,0:T(8,128)(2,1)S(1)} %get-tuple-element.61.mix_ref, ...), custom_call_target="tpu_custom_call" | custom-call | flops 1500000000 | bytes 5000000 | tf_op jit(solution)/shard_map/pallas_call | solution.py:551
  17.1 0.7 collective-permute-start.6
  17.7 2.4 %collective-permute-start.7 = (f32[48,512]{1,0:T(8,128)S(1)}, f32[48,512]{1,0:T(8,128)S(1)}, u32[]{:S(2)}, u32[]{:S(2)}) collective-permute-start(f32[48,512]{1,0:T(8,128)S(1)} %get-tuple-element.79), channel_id=1, source_target_pairs={{0,7},{1,2},{2,1},{3,4},{4,3},{5,6},{6,5},{7,0},{8,15},{9,10},{10,... | collective-permute-start | bytes 294920 | tf_op jit(solution)/shard_map/ppermute | solution.py:437
  20.1 3.9 %shard_map.139 = (f32[2,128,256]{2,1,0:T(8,128)S(1)}, f32[128,256]{1,0:T(8,128)S(1)}, f32[48,512]{1,0:T(8,128)S(1)}, f32[48,512]{1,0:T(8,128)S(1)}, f32[2,2,64,8,128]{4,3,2,1,0:T(8,128)S(1)}) custom-call(s32[3,8,128]{2,1,0:T(8,128)S(1)} %broadcast_in_dim.2.index_ref, bf16[1024,512]{1,0:T(8,128)(2,1)S(1)} %get-tuple-element.61.mix_ref, ...), custom_call_target="tpu_custom_call" | custom-call | flops 1500000000 | bytes 5000000 | tf_op jit(solution)/shard_map/pallas_call | solution.py:551
  24.0 0.7 %collective-permute-start.4 = (f32[48,512]{1,0:T(8,128)S(1)}, f32[48,512]{1,0:T(8,128)S(1)}, u32[]{:S(2)}, u32[]{:S(2)}) collective-permute-start(f32[48,512]{1,0:T(8,128)S(1)} %get-tuple-element.75), channel_id=1, source_target_pairs={{0,1},{1,0},{2,3},{3,2},{4,5},{5,4},{6,7},{7,6},{8,9},{9,8},{10,11... | collective-permute-start | bytes 294920 | tf_op jit(solution)/shard_map/ppermute | solution.py:436
  24.7 1.8 %collective-permute-start.5 = (f32[48,512]{1,0:T(8,128)S(1)}, f32[48,512]{1,0:T(8,128)S(1)}, u32[]{:S(2)}, u32[]{:S(2)}) collective-permute-start(f32[48,512]{1,0:T(8,128)S(1)} %get-tuple-element.76), channel_id=1, source_target_pairs={{0,7},{1,2},{2,1},{3,4},{4,3},{5,6},{6,5},{7,0},{8,15},{9,10},{10,... | collective-permute-start | bytes 294920 | tf_op jit(solution)/shard_map/ppermute | solution.py:437
  26.5 3.9 %shard_map.140 = (f32[2,128,256]{2,1,0:T(8,128)S(1)}, f32[128,256]{1,0:T(8,128)S(1)}, f32[48,512]{1,0:T(8,128)S(1)}, f32[48,512]{1,0:T(8,128)S(1)}, f32[2,2,64,8,128]{4,3,2,1,0:T(8,128)S(1)}) custom-call(s32[3,8,128]{2,1,0:T(8,128)S(1)} %broadcast_in_dim.2.index_ref, bf16[1024,512]{1,0:T(8,128)(2,1)S(1)} %get-tuple-element.61.mix_ref, ...), custom_call_target="tpu_custom_call" | custom-call | flops 1500000000 | bytes 5000000 | tf_op jit(solution)/shard_map/pallas_call | solution.py:551
  30.5 3.5 %collective-permute-start.11 = (f32[48,512]{1,0:T(8,128)S(1)}, f32[48,512]{1,0:T(8,128)S(1)}, u32[]{:S(2)}, u32[]{:S(2)}) collective-permute-start(f32[48,512]{1,0:T(8,128)S(1)} %get-tuple-element.86), channel_id=1, source_target_pairs={{0,7},{1,2},{2,1},{3,4},{4,3},{5,6},{6,5},{7,0},{8,15},{9,10},{10,... | collective-permute-start | bytes 294920 | tf_op jit(solution)/shard_map/ppermute | solution.py:437
  33.9 3.9 %shard_map.141 = (f32[2,128,256]{2,1,0:T(8,128)S(1)}, f32[128,256]{1,0:T(8,128)S(1)}, f32[48,512]{1,0:T(8,128)S(1)}, f32[48,512]{1,0:T(8,128)S(1)}, f32[2,2,64,8,128]{4,3,2,1,0:T(8,128)S(1)}) custom-call(s32[3,8,128]{2,1,0:T(8,128)S(1)} %broadcast_in_dim.2.index_ref, bf16[1024,512]{1,0:T(8,128)(2,1)S(1)} %get-tuple-element.61.mix_ref, ...), custom_call_target="tpu_custom_call" | custom-call | flops 1500000000 | bytes 5000000 | tf_op jit(solution)/shard_map/pallas_call | solution.py:551
  37.8 0.2 collective-permute-start.8
  38.0 1.8 %collective-permute-start.9 = (f32[48,512]{1,0:T(8,128)S(1)}, f32[48,512]{1,0:T(8,128)S(1)}, u32[]{:S(2)}, u32[]{:S(2)}) collective-permute-start(f32[48,512]{1,0:T(8,128)S(1)} %get-tuple-element.83), channel_id=1, source_target_pairs={{0,7},{1,2},{2,1},{3,4},{4,3},{5,6},{6,5},{7,0},{8,15},{9,10},{10,... | collective-permute-start | bytes 294920 | tf_op jit(solution)/shard_map/ppermute | solution.py:437
  39.8 2.7 %shard_map.142 = (f32[2,128,256]{2,1,0:T(8,128)S(1)}, f32[128,256]{1,0:T(8,128)S(1)}, f32[48,512]{1,0:T(8,128)S(1)}, f32[48,512]{1,0:T(8,128)S(1)}) custom-call(s32[3,8,128]{2,1,0:T(8,128)S(1)} %broadcast_in_dim.2.index_ref, bf16[1024,512]{1,0:T(8,128)(2,1)S(1)} %get-tuple-element.61.mix_ref, bf16[2048,256]{1,0:T(8,128)(2,1)S(1)} %get-tuple-element.62.high_ref, ...), custom_call_target="tpu_custom_call" | custom-call | flops 1500000000 | bytes 5000000 | tf_op jit(solution)/shard_map/pallas_call | solution.py:551
  42.5 0.7 collective-permute-start.14
  43.1 2.4 %collective-permute-start.15 = (f32[48,512]{1,0:T(8,128)S(1)}, f32[48,512]{1,0:T(8,128)S(1)}, u32[]{:S(2)}, u32[]{:S(2)}) collective-permute-start(f32[48,512]{1,0:T(8,128)S(1)} %get-tuple-element.95), channel_id=1, source_target_pairs={{0,7},{1,2},{2,1},{3,4},{4,3},{5,6},{6,5},{7,0},{8,15},{9,10},{10,... | collective-permute-start | bytes 294920 | tf_op jit(solution)/shard_map/ppermute | solution.py:437
  45.5 0.4 collective-permute-done.9.recv_b
  45.9 3.3 %shard_map.143 = (f32[2,128,256]{2,1,0:T(8,128)S(1)}, f32[128,256]{1,0:T(8,128)}, f32[48,512]{1,0:T(8,128)S(1)}, f32[48,512]{1,0:T(8,128)S(1)}, f32[3,2,32,256]{...) custom-call(s32[3,8,128]{2,1,0:T(8,128)S(1)} %broadcast_in_dim.2.index_ref, ...), custom_call_target="tpu_custom_call" | custom-call | flops 1500000000 | bytes 5000000 | tf_op jit(solution)/shard_map/pallas_call | solution.py:551
  49.2 0.4 collective-permute-start.12
  49.6 1.6 %collective-permute-start.13 = (f32[48,512]{1,0:T(8,128)S(1)}, f32[48,512]{1,0:T(8,128)S(1)}, u32[]{:S(2)}, u32[]{:S(2)}) collective-permute-start(f32[48,512]{1,0:T(8,128)S(1)} %get-tuple-element.92), channel_id=1, source_target_pairs={{0,7},{1,2},{2,1},{3,4},{4,3},{5,6},{6,5},{7,0},{8,15},{9,10},{10,... | collective-permute-start | bytes 294920 | tf_op jit(solution)/shard_map/ppermute | solution.py:437
  51.3 2.5 %shard_map.144 = (f32[2,128,256]{2,1,0:T(8,128)S(1)}, f32[128,256]{1,0:T(8,128)S(1)}, f32[4,128,256]{2,1,0:T(8,128)}) custom-call(s32[3,8,128]{2,1,0:T(8,128)S(1)} %broadcast_in_dim.2.index_ref, bf16[1024,512]{1,0:T(8,128)(2,1)S(1)} %get-tuple-element.61.mix_ref, bf16[2048,256]{1,0:T(8,128)(2,1)S(1)} %get-tuple-element.62.high_ref, ...), custom_call_target="tpu_custom_call" | custom-call | flops 1500000000 | bytes 5000000 | tf_op jit(solution)/shard_map/pallas_call | solution.py:551
  53.9 1.6 %collective-permute-start.17 = (f32[3,32,256]{2,1,0:T(8,128)S(1)}, f32[3,32,256]{2,1,0:T(8,128)S(1)}, u32[]{:S(2)}, u32[]{:S(2)}) collective-permute-start(f32[3,32,256]{2,1,0:T(8,128)S(1)} %get-tuple-element.102), channel_id=1, source_target_pairs={{0,16},{8,24},{16,0},{24,8},{1,17},{9,25},{17,1},{25,9},{2,18},{10... | collective-permute-start | bytes 294920 | tf_op jit(solution)/shard_map/ppermute | solution.py:491
  55.5 1.8 %collective-permute-done.13.recv_b = f32[48,512]{1,0:T(8,128)S(1)} collective-permute-done((f32[48,512]{1,0:T(8,128)S(1)}, f32[48,512]{1,0:T(8,128)S(1)}, u32[]{:S(2)}, u32[]{:S(2)}) %collective-permute-start.13) | collective-permute-done | bytes 98336 | tf_op jit(solution)/shard_map/ppermute | solution.py:437
  57.3 3.2 %shard_map.145 = (f32[2,128,256]{2,1,0:T(8,128)S(1)}, f32[128,256]{1,0:T(8,128)}, f32[4,128,256]{2,1,0:T(8,128)}, f32[32,256]{1,0:T(8,128)S(1)}, f32[32,256]{1,0...) custom-call(s32[3,8,128]{2,1,0:T(8,128)S(1)} %broadcast_in_dim.2.index_ref, ...), custom_call_target="tpu_custom_call", output_to_operand_aliasing={{2}: (12, {})} | custom-call | flops 1500000000 | bytes 5000000 | tf_op jit(solution)/shard_map/pallas_call | solution.py:551
  60.5 1.6 %collective-permute-start.18 = (f32[32,256]{1,0:T(8,128)S(1)}, f32[32,256]{1,0:T(8,128)S(1)}, u32[]{:S(2)}, u32[]{:S(2)}) collective-permute-start(f32[32,256]{1,0:T(8,128)S(1)} %get-tuple-element.108), channel_id=1, source_target_pairs={{0,16},{8,24},{16,0},{24,8},{1,17},{9,25},{17,1},{25,9},{2,18},{10... | collective-permute-start | bytes 98312 | tf_op jit(solution)/shard_map/ppermute | solution.py:574
  62.0 0.6 collective-permute-start.20
  62.7 1.8 %collective-permute-done.18.rest_5_ = f32[32,256]{1,0:T(8,128)S(1)} collective-permute-done((f32[32,256]{1,0:T(8,128)S(1)}, f32[32,256]{1,0:T(8,128)S(1)}, u32[]{:S(2)}, u32[]{:S(2)}) %collective-permute-start.18) | collective-permute-done | bytes 32800 | tf_op jit(solution)/shard_map/ppermute | solution.py:574
  64.4 1.0 %collective-permute-done.19.rest_6_ = f32[32,256]{1,0:T(8,128)S(1)} collective-permute-done((f32[32,256]{1,0:T(8,128)S(1)}, f32[32,256]{1,0:T(8,128)S(1)}, u32[]{:S(2)}, u32[]{:S(2)}) %collective-permute-start.19) | collective-permute-done | bytes 32800 | tf_op jit(solution)/shard_map/ppermute | solution.py:574
  65.4 7.3 %energy.1 = (f32[4,32,256]{2,1,0:T(8,128)}, f32[512,32,256]{2,1,0:T(8,128)}, f32[4,128,256]{2,1,0:T(8,128)}) custom-call(bf16[256,256]{1,0:T(8,128)(2,1)S(1)} %copy-done.1, bf16[256,256]{1,0:T(8,128)(2,1)S(1)} %copy-done, f32[3,32,256]{2,1,0:T(8,128)S(1)} %get-tuple-element.101.early_mine, f32[3,32,256]{2,1,0:T(8,128)S(1)} %collective-permute-done.17.early_got, ...), custom_call_target="tpu_custom_call" | custom-call | flops 4000000000 | bytes 22000000 | tf_op jit(solution)/shard_map/energy/pallas_call | solution.py:582
  (28 shorter events, 0.4 us)
Async XLA Ops:
  2.1 11.1 %collective-permute-start.2 = (f32[48,512]{1,0:T(8,128)S(1)}, f32[48,512]{1,0:T(8,128)S(1)}, u32[]{:S(2)}, u32[]{:S(2)}) collective-permute-start(f32[48,512]{1,0:T(8,128)S(1)} %get-tuple-element.71), channel_id=1, source_target_pairs={{0,1},{1,0},{2,3},{3,2},{4,5},{5,4},{6,7},{7,6},{8,9},{9,8},{10,11... | collective-permute-start | bytes 294920 | tf_op jit(solution)/shard_map/ppermute | solution.py:436
  5.1 8.0 %collective-permute-start.3 = (f32[48,512]{1,0:T(8,128)S(1)}, f32[48,512]{1,0:T(8,128)S(1)}, u32[]{:S(2)}, u32[]{:S(2)}) collective-permute-start(f32[48,512]{1,0:T(8,128)S(1)} %get-tuple-element.72), channel_id=1, source_target_pairs={{0,7},{1,2},{2,1},{3,4},{4,3},{5,6},{6,5},{7,0},{8,15},{9,10},{10,... | collective-permute-start | bytes 294920 | tf_op jit(solution)/shard_map/ppermute | solution.py:437
  11.2 8.9 %collective-permute-start = (f32[48,512]{1,0:T(8,128)S(1)}, f32[48,512]{1,0:T(8,128)S(1)}, u32[]{:S(2)}, u32[]{:S(2)}) collective-permute-start(f32[48,512]{1,0:T(8,128)S(1)} %get-tuple-element.68), channel_id=1, source_target_pairs={{0,1},{1,0},{2,3},{3,2},{4,5},{5,4},{6,7},{7,6},{8,9},{9,8},{10,11... | collective-permute-start | bytes 294920 | tf_op jit(solution)/shard_map/ppermute | solution.py:436
  11.3 8.8 %collective-permute-start.1 = (f32[48,512]{1,0:T(8,128)S(1)}, f32[48,512]{1,0:T(8,128)S(1)}, u32[]{:S(2)}, u32[]{:S(2)}) collective-permute-start(f32[48,512]{1,0:T(8,128)S(1)} %get-tuple-element.69), channel_id=1, source_target_pairs={{0,7},{1,2},{2,1},{3,4},{4,3},{5,6},{6,5},{7,0},{8,15},{9,10},{10,... | collective-permute-start | bytes 294920 | tf_op jit(solution)/shard_map/ppermute | solution.py:437
  17.1 9.4 %collective-permute-start.6 = (f32[48,512]{1,0:T(8,128)S(1)}, f32[48,512]{1,0:T(8,128)S(1)}, u32[]{:S(2)}, u32[]{:S(2)}) collective-permute-start(f32[48,512]{1,0:T(8,128)S(1)} %get-tuple-element.78), channel_id=1, source_target_pairs={{0,1},{1,0},{2,3},{3,2},{4,5},{5,4},{6,7},{7,6},{8,9},{9,8},{10,11... | collective-permute-start | bytes 294920 | tf_op jit(solution)/shard_map/ppermute | solution.py:436
  17.7 8.8 %collective-permute-start.7 = (f32[48,512]{1,0:T(8,128)S(1)}, f32[48,512]{1,0:T(8,128)S(1)}, u32[]{:S(2)}, u32[]{:S(2)}) collective-permute-start(f32[48,512]{1,0:T(8,128)S(1)} %get-tuple-element.79), channel_id=1, source_target_pairs={{0,7},{1,2},{2,1},{3,4},{4,3},{5,6},{6,5},{7,0},{8,15},{9,10},{10,... | collective-permute-start | bytes 294920 | tf_op jit(solution)/shard_map/ppermute | solution.py:437
  24.0 9.9 %collective-permute-start.4 = (f32[48,512]{1,0:T(8,128)S(1)}, f32[48,512]{1,0:T(8,128)S(1)}, u32[]{:S(2)}, u32[]{:S(2)}) collective-permute-start(f32[48,512]{1,0:T(8,128)S(1)} %get-tuple-element.75), channel_id=1, source_target_pairs={{0,1},{1,0},{2,3},{3,2},{4,5},{5,4},{6,7},{7,6},{8,9},{9,8},{10,11... | collective-permute-start | bytes 294920 | tf_op jit(solution)/shard_map/ppermute | solution.py:436
  24.7 9.2 %collective-permute-start.5 = (f32[48,512]{1,0:T(8,128)S(1)}, f32[48,512]{1,0:T(8,128)S(1)}, u32[]{:S(2)}, u32[]{:S(2)}) collective-permute-start(f32[48,512]{1,0:T(8,128)S(1)} %get-tuple-element.76), channel_id=1, source_target_pairs={{0,7},{1,2},{2,1},{3,4},{4,3},{5,6},{6,5},{7,0},{8,15},{9,10},{10,... | collective-permute-start | bytes 294920 | tf_op jit(solution)/shard_map/ppermute | solution.py:437
  30.4 9.4 %collective-permute-start.10 = (f32[48,512]{1,0:T(8,128)S(1)}, f32[48,512]{1,0:T(8,128)S(1)}, u32[]{:S(2)}, u32[]{:S(2)}) collective-permute-start(f32[48,512]{1,0:T(8,128)S(1)} %get-tuple-element.85), channel_id=1, source_target_pairs={{0,1},{1,0},{2,3},{3,2},{4,5},{5,4},{6,7},{7,6},{8,9},{9,8},{10,11... | collective-permute-start | bytes 294920 | tf_op jit(solution)/shard_map/ppermute | solution.py:436
  30.5 9.4 %collective-permute-start.11 = (f32[48,512]{1,0:T(8,128)S(1)}, f32[48,512]{1,0:T(8,128)S(1)}, u32[]{:S(2)}, u32[]{:S(2)}) collective-permute-start(f32[48,512]{1,0:T(8,128)S(1)} %get-tuple-element.86), channel_id=1, source_target_pairs={{0,7},{1,2},{2,1},{3,4},{4,3},{5,6},{6,5},{7,0},{8,15},{9,10},{10,... | collective-permute-start | bytes 294920 | tf_op jit(solution)/shard_map/ppermute | solution.py:437
  37.8 7.7 %collective-permute-start.8 = (f32[48,512]{1,0:T(8,128)S(1)}, f32[48,512]{1,0:T(8,128)S(1)}, u32[]{:S(2)}, u32[]{:S(2)}) collective-permute-start(f32[48,512]{1,0:T(8,128)S(1)} %get-tuple-element.82), channel_id=1, source_target_pairs={{0,1},{1,0},{2,3},{3,2},{4,5},{5,4},{6,7},{7,6},{8,9},{9,8},{10,11... | collective-permute-start | bytes 294920 | tf_op jit(solution)/shard_map/ppermute | solution.py:436
  38.0 7.9 %collective-permute-start.9 = (f32[48,512]{1,0:T(8,128)S(1)}, f32[48,512]{1,0:T(8,128)S(1)}, u32[]{:S(2)}, u32[]{:S(2)}) collective-permute-start(f32[48,512]{1,0:T(8,128)S(1)} %get-tuple-element.83), channel_id=1, source_target_pairs={{0,7},{1,2},{2,1},{3,4},{4,3},{5,6},{6,5},{7,0},{8,15},{9,10},{10,... | collective-permute-start | bytes 294920 | tf_op jit(solution)/shard_map/ppermute | solution.py:437
  42.5 8.8 %collective-permute-start.14 = (f32[48,512]{1,0:T(8,128)S(1)}, f32[48,512]{1,0:T(8,128)S(1)}, u32[]{:S(2)}, u32[]{:S(2)}) collective-permute-start(f32[48,512]{1,0:T(8,128)S(1)} %get-tuple-element.94), channel_id=1, source_target_pairs={{0,1},{1,0},{2,3},{3,2},{4,5},{5,4},{6,7},{7,6},{8,9},{9,8},{10,11... | collective-permute-start | bytes 294920 | tf_op jit(solution)/shard_map/ppermute | solution.py:436
  43.1 8.1 %collective-permute-start.15 = (f32[48,512]{1,0:T(8,128)S(1)}, f32[48,512]{1,0:T(8,128)S(1)}, u32[]{:S(2)}, u32[]{:S(2)}) collective-permute-start(f32[48,512]{1,0:T(8,128)S(1)} %get-tuple-element.95), channel_id=1, source_target_pairs={{0,7},{1,2},{2,1},{3,4},{4,3},{5,6},{6,5},{7,0},{8,15},{9,10},{10,... | collective-permute-start | bytes 294920 | tf_op jit(solution)/shard_map/ppermute | solution.py:437
  49.2 4.6 %collective-permute-start.16 = (f32[3,2,32,256]{3,2,1,0:T(8,128)S(1)}, f32[3,2,32,256]{3,2,1,0:T(8,128)S(1)}, u32[]{:S(2)}, u32[]{:S(2)}) collective-permute-start(f32[3,2,32,256]{3,2,1,0:T(8,128)S(1)} %get-tuple-element.100), channel_id=1, source_target_pairs={{0,8},{8,0},{16,24},{24,16},{1,9},{9,1},{17,25},{25,17},{2,10},{10... | collective-permute-start | bytes 589832 | tf_op jit(solution)/shard_map/ppermute | solution.py:480
  49.2 6.3 %collective-permute-start.12 = (f32[48,512]{1,0:T(8,128)S(1)}, f32[48,512]{1,0:T(8,128)S(1)}, u32[]{:S(2)}, u32[]{:S(2)}) collective-permute-start(f32[48,512]{1,0:T(8,128)S(1)} %get-tuple-element.91), channel_id=1, source_target_pairs={{0,1},{1,0},{2,3},{3,2},{4,5},{5,4},{6,7},{7,6},{8,9},{9,8},{10,11... | collective-permute-start | bytes 294920 | tf_op jit(solution)/shard_map/ppermute | solution.py:436
  49.6 7.6 %collective-permute-start.13 = (f32[48,512]{1,0:T(8,128)S(1)}, f32[48,512]{1,0:T(8,128)S(1)}, u32[]{:S(2)}, u32[]{:S(2)}) collective-permute-start(f32[48,512]{1,0:T(8,128)S(1)} %get-tuple-element.92), channel_id=1, source_target_pairs={{0,7},{1,2},{2,1},{3,4},{4,3},{5,6},{6,5},{7,0},{8,15},{9,10},{10,... | collective-permute-start | bytes 294920 | tf_op jit(solution)/shard_map/ppermute | solution.py:437
  53.8 11.6 %copy-start = (bf16[256,256]{1,0:T(8,128)(2,1)S(1)}, bf16[256,256]{1,0:T(8,128)(2,1)}, u32[]{:S(2)}) copy-start(bf16[256,256]{1,0:T(8,128)(2,1)} %constant.41.clone.odd_ref) | copy-start | bytes 393220
  53.8 11.6 %copy-start.1 = (bf16[256,256]{1,0:T(8,128)(2,1)S(1)}, bf16[256,256]{1,0:T(8,128)(2,1)}, u32[]{:S(2)}) copy-start(bf16[256,256]{1,0:T(8,128)(2,1)} %constant.40.clone.even_ref) | copy-start | bytes 393220
  53.9 11.5 %collective-permute-start.17 = (f32[3,32,256]{2,1,0:T(8,128)S(1)}, f32[3,32,256]{2,1,0:T(8,128)S(1)}, u32[]{:S(2)}, u32[]{:S(2)}) collective-permute-start(f32[3,32,256]{2,1,0:T(8,128)S(1)} %get-tuple-element.102), channel_id=1, source_target_pairs={{0,16},{8,24},{16,0},{24,8},{1,17},{9,25},{17,1},{25,9},{2,18},{10... | collective-permute-start | bytes 294920 | tf_op jit(solution)/shard_map/ppermute | solution.py:491
  60.5 4.0 %collective-permute-start.18 = (f32[32,256]{1,0:T(8,128)S(1)}, f32[32,256]{1,0:T(8,128)S(1)}, u32[]{:S(2)}, u32[]{:S(2)}) collective-permute-start(f32[32,256]{1,0:T(8,128)S(1)} %get-tuple-element.108), channel_id=1, source_target_pairs={{0,16},{8,24},{16,0},{24,8},{1,17},{9,25},{17,1},{25,9},{2,18},{10... | collective-permute-start | bytes 98312 | tf_op jit(solution)/shard_map/ppermute | solution.py:574
  62.0 3.3 %collective-permute-start.19 = (f32[32,256]{1,0:T(8,128)S(1)}, f32[32,256]{1,0:T(8,128)S(1)}, u32[]{:S(2)}, u32[]{:S(2)}) collective-permute-start(f32[32,256]{1,0:T(8,128)S(1)} %get-tuple-element.109), channel_id=1, source_target_pairs={{0,24},{8,16},{16,8},{24,0},{1,25},{9,17},{17,9},{25,1},{2,26},{10... | collective-permute-start | bytes 98312 | tf_op jit(solution)/shard_map/ppermute | solution.py:574
  62.0 3.3 %collective-permute-start.20 = (f32[32,256]{1,0:T(8,128)S(1)}, f32[32,256]{1,0:T(8,128)S(1)}, u32[]{:S(2)}, u32[]{:S(2)}) collective-permute-start(f32[32,256]{1,0:T(8,128)S(1)} %get-tuple-element.110), channel_id=1, source_target_pairs={{0,8},{8,0},{16,24},{24,16},{1,9},{9,1},{17,25},{25,17},{2,10},{10... | collective-permute-start | bytes 98312 | tf_op jit(solution)/shard_map/ppermute | solution.py:574

commit v6 on v5

--- a/solution.py
+++ b/solution.py
@@ -221,7 +221,7 @@
         prev_out = rest.pop(0)
     else:
         send_a, send_b = rest.pop(0), rest.pop(0)
-    if fold and last:
+    if fold and not older:
         pieces_out = [rest.pop(0) for _ in range(4)]
     elif fold:
         keep_ref, give_ref = rest.pop(0), rest.pop(0)
@@ -297,12 +297,11 @@
     partial_out[...] = partial
     if fold:
         quarter = blocks // 4
-        for s in range(older + 1):
-            ref = olders[s] if s < older else partial_out
+        for s, ref in enumerate(olders or [partial_out]):
             parts = [ref[i * quarter : (i + 1) * quarter] for i in range(4)]
             keep = [choose(index_ref, 1, *parts[2 * y : 2 * y + 2]) for y in range(2)]
             give = [choose(index_ref, 1, *parts[2 * y : 2 * y + 2][::-1]) for y in range(2)]
-            if last:
+            if not older:
                 pieces_out[0][...] = choose(index_ref, 2, *keep)
                 pieces_out[1][...] = choose(index_ref, 2, *give)
                 pieces_out[2][...] = choose(index_ref, 2, *keep[::-1])
@@ -501,8 +500,8 @@
             args = [index, mix, high, low, pick, site_held]
             args += [current[c][0], previous[c][0], probe_held, *received[c]]
             specs = [vmem()] * len(args)
-            fold = c == chunks - 1 and s >= STEPS - 2
-            older = 0 if last or not fold else len(partials)
+            fold = last
+            older = len(partials) if fold and c == 0 else 0
             extra = ([] if partial is None else [partial]) + partials[:older]
             args += extra
             specs += [vmem()] * len(extra)
@@ -525,10 +524,10 @@
                 scratch.append(pltpu.SemaphoreType.DMA)
             else:
                 outs += [rows, rows]
-            if fold and last:
+            if fold and not older:
                 outs += [jax.ShapeDtypeStruct((quarter, width), F32)] * 4
             elif fold:
-                outs += [jax.ShapeDtypeStruct((older + 1, groups // 2, quarter, width), F32)] * 2
+                outs += [jax.ShapeDtypeStruct((older, groups // 2, quarter, width), F32)] * 2
             if fetch is not None:
                 outs.append(
                     jax.ShapeDtypeStruct((width // lanes, 2, moment_count // 2, group, lanes), F32)
@@ -567,7 +566,7 @@
                 received[c] = exchange(result.pop(0), result.pop(0))
             if fetch is not None:
                 prior_held.append(result.pop(0))
-            if fold and last:
+            if fold and not older:
                 lates = [result[0]]
                 for flip in (2, 3, 1):
                     pairs = [(i, i ^ flip) for i in range(groups)]

time: 73.1 us -> 76.8 us (1.051)
  waiting for transfers between devices: 4.92 us -> 8.53 us
    ppermute x8, waiting for transfers between devices: 2.16 us -> 4.83 us  [exchange(): got_b = lax.ppermute(b, 'dom', swap_b)]
    ppermute x8, waiting for transfers between devices: 0.02 us -> 0.98 us  [exchange(): got_a = lax.ppermute(a, 'dom', swap_a)]
    ppermute x8, starting transfers between devices: 18.9 us -> 19.8 us  [exchange(): got_b = lax.ppermute(b, 'dom', swap_b)]
  transfers between devices with their start and end apart: 21 -> 21, of which waited for: 4 -> 6; matrix products, arithmetic and copies ran while one was open for 0% -> 0% of each run, Pallas kernels for 41% -> 35%
where the time goes in v6:
time: 76.8 us; the launch traced here: 76.6 us
  Pallas kernels  37.8 us (49%)
  starting transfers between devices  29.1 us (38%)
  waiting for transfers between devices  8.53 us (11%)
  between operations  0.99 us (1%)
    pallas_call x8, Pallas kernels, per_device(): pl.pallas_call(functools.partial(step_kernel, cfg), out_shape=outs, in_sp...  26.6 us
    ppermute x8, starting transfers between devices, exchange(): got_b = lax.ppermute(b, 'dom', swap_b)  19.8 us
    pallas_call x1, Pallas kernels, per_device(): pl.pallas_call(functools.partial(energy_kernel, vec_dev * groups, chunks,...  7.28 us
    ppermute x8, starting transfers between devices, exchange(): got_a = lax.ppermute(a, 'dom', swap_a)  5.45 us
    ppermute x8, waiting for transfers between devices, exchange(): got_b = lax.ppermute(b, 'dom', swap_b)  4.83 us
    ppermute x3, waiting for transfers between devices, per_device(): lates.append(lax.ppermute(result[flip], 'vec', pairs))  2.72 us
    pallas_call x1, Pallas kernels, per_device(): pl.pallas_call(functools.partial(prep_kernel, rim), out_shape=[jax.ShapeD...  2.48 us
    ppermute x3, starting transfers between devices, per_device(): lates.append(lax.ppermute(result[flip], 'vec', pairs))  2.21 us
  transfers between devices with their start and end apart: 21, of which 6 were waited for; matrix products, arithmetic and copies ran while one was open for 0% of the time, Pallas kernels for 35%

profile of v6, /device:TPU:0, one launch (start us, length us, event | category | flops | bytes accessed | tf_op | source)
XLA Modules:
  0.0 76.6 jit_solution(218404838574068165)
XLA Ops:
  0.8 1.3 %first_sends.1 = (bf16[96,256]{1,0:T(8,128)(2,1)S(1)}, f32[2,128,256]{2,1,0:T(8,128)S(1)}, f32[48,512]{1,0:T(8,128)S(1)}, f32[48,512]{1,0:T(8,128)S(1)}) custom-call(s32[3,8,128]{2,1,0:T(8,128)S(1)} %broadcast_in_dim.2.index_ref, s32[1,2,48]{2,1,0:T(2,128)} %lists_hbm.1, f32[4,128,256]{2,1,0:T(8,128)} %cur_hbm.3), custom_call_target="tpu_custom_call" | custom-call | flops 100000000 | bytes 1000000 | tf_op jit(solution)/shard_map/first_sends/pallas_call | solution.py:420
  2.1 3.0 %collective-permute-start.2 = (f32[48,512]{1,0:T(8,128)S(1)}, f32[48,512]{1,0:T(8,128)S(1)}, u32[]{:S(2)}, u32[]{:S(2)}) collective-permute-start(f32[48,512]{1,0:T(8,128)S(1)} %get-tuple-element.72), channel_id=1, source_target_pairs={{0,1},{1,0},{2,3},{3,2},{4,5},{5,4},{6,7},{7,6},{8,9},{9,8},{10,11... | collective-permute-start | bytes 294920 | tf_op jit(solution)/shard_map/ppermute | solution.py:435
  5.1 3.6 %collective-permute-start.3 = (f32[48,512]{1,0:T(8,128)S(1)}, f32[48,512]{1,0:T(8,128)S(1)}, u32[]{:S(2)}, u32[]{:S(2)}) collective-permute-start(f32[48,512]{1,0:T(8,128)S(1)} %get-tuple-element.73), channel_id=1, source_target_pairs={{0,7},{1,2},{2,1},{3,4},{4,3},{5,6},{6,5},{7,0},{8,15},{9,10},{10,... | collective-permute-start | bytes 294920 | tf_op jit(solution)/shard_map/ppermute | solution.py:436
  8.7 2.5 %tables.1 = (bf16[1024,512]{1,0:T(8,128)(2,1)S(1)}, bf16[2048,256]{1,0:T(8,128)(2,1)S(1)}, bf16[2048,256]{1,0:T(8,128)(2,1)S(1)}, f32[4,128,256]{2,1,0:T(8,128)S...) custom-call(s32[3,8,128]{2,1,0:T(8,128)S(1)} %broadcast_in_dim.2.ind, ...), custom_call_target="tpu_custom_call" | custom-call | flops 10000000 | bytes 8000000 | tf_op jit(solution)/shard_map/tables/pallas_call | solution.py:441
  11.3 1.9 %collective-permute-start.1 = (f32[48,512]{1,0:T(8,128)S(1)}, f32[48,512]{1,0:T(8,128)S(1)}, u32[]{:S(2)}, u32[]{:S(2)}) collective-permute-start(f32[48,512]{1,0:T(8,128)S(1)} %get-tuple-element.70), channel_id=1, source_target_pairs={{0,7},{1,2},{2,1},{3,4},{4,3},{5,6},{6,5},{7,0},{8,15},{9,10},{10,... | collective-permute-start | bytes 294920 | tf_op jit(solution)/shard_map/ppermute | solution.py:436
  13.2 3.9 %shard_map.138 = (f32[2,128,256]{2,1,0:T(8,128)S(1)}, f32[128,256]{1,0:T(8,128)S(1)}, f32[48,512]{1,0:T(8,128)S(1)}, f32[48,512]{1,0:T(8,128)S(1)}, f32[2,2,64,8,128]{4,3,2,1,0:T(8,128)S(1)}) custom-call(s32[3,8,128]{2,1,0:T(8,128)S(1)} %broadcast_in_dim.2.index_ref, bf16[1024,512]{1,0:T(8,128)(2,1)S(1)} %get-tuple-element.62.mix_ref, ...), custom_call_target="tpu_custom_call" | custom-call | flops 1500000000 | bytes 5000000 | tf_op jit(solution)/shard_map/pallas_call | solution.py:550
  17.1 0.7 collective-permute-start.6
  17.7 2.4 %collective-permute-start.7 = (f32[48,512]{1,0:T(8,128)S(1)}, f32[48,512]{1,0:T(8,128)S(1)}, u32[]{:S(2)}, u32[]{:S(2)}) collective-permute-start(f32[48,512]{1,0:T(8,128)S(1)} %get-tuple-element.80), channel_id=1, source_target_pairs={{0,7},{1,2},{2,1},{3,4},{4,3},{5,6},{6,5},{7,0},{8,15},{9,10},{10,... | collective-permute-start | bytes 294920 | tf_op jit(solution)/shard_map/ppermute | solution.py:436
  20.1 3.9 %shard_map.139 = (f32[2,128,256]{2,1,0:T(8,128)S(1)}, f32[128,256]{1,0:T(8,128)S(1)}, f32[48,512]{1,0:T(8,128)S(1)}, f32[48,512]{1,0:T(8,128)S(1)}, f32[2,2,64,8,128]{4,3,2,1,0:T(8,128)S(1)}) custom-call(s32[3,8,128]{2,1,0:T(8,128)S(1)} %broadcast_in_dim.2.index_ref, bf16[1024,512]{1,0:T(8,128)(2,1)S(1)} %get-tuple-element.62.mix_ref, ...), custom_call_target="tpu_custom_call" | custom-call | flops 1500000000 | bytes 5000000 | tf_op jit(solution)/shard_map/pallas_call | solution.py:550
  24.0 0.7 collective-permute-start.4
  24.7 1.8 %collective-permute-start.5 = (f32[48,512]{1,0:T(8,128)S(1)}, f32[48,512]{1,0:T(8,128)S(1)}, u32[]{:S(2)}, u32[]{:S(2)}) collective-permute-start(f32[48,512]{1,0:T(8,128)S(1)} %get-tuple-element.77), channel_id=1, source_target_pairs={{0,7},{1,2},{2,1},{3,4},{4,3},{5,6},{6,5},{7,0},{8,15},{9,10},{10,... | collective-permute-start | bytes 294920 | tf_op jit(solution)/shard_map/ppermute | solution.py:436
  26.5 3.9 %shard_map.140 = (f32[2,128,256]{2,1,0:T(8,128)S(1)}, f32[128,256]{1,0:T(8,128)S(1)}, f32[48,512]{1,0:T(8,128)S(1)}, f32[48,512]{1,0:T(8,128)S(1)}, f32[2,2,64,8,128]{4,3,2,1,0:T(8,128)S(1)}) custom-call(s32[3,8,128]{2,1,0:T(8,128)S(1)} %broadcast_in_dim.2.index_ref, bf16[1024,512]{1,0:T(8,128)(2,1)S(1)} %get-tuple-element.62.mix_ref, ...), custom_call_target="tpu_custom_call" | custom-call | flops 1500000000 | bytes 5000000 | tf_op jit(solution)/shard_map/pallas_call | solution.py:550
  30.5 3.5 %collective-permute-start.11 = (f32[48,512]{1,0:T(8,128)S(1)}, f32[48,512]{1,0:T(8,128)S(1)}, u32[]{:S(2)}, u32[]{:S(2)}) collective-permute-start(f32[48,512]{1,0:T(8,128)S(1)} %get-tuple-element.87), channel_id=1, source_target_pairs={{0,7},{1,2},{2,1},{3,4},{4,3},{5,6},{6,5},{7,0},{8,15},{9,10},{10,... | collective-permute-start | bytes 294920 | tf_op jit(solution)/shard_map/ppermute | solution.py:436
  33.9 3.9 %shard_map.141 = (f32[2,128,256]{2,1,0:T(8,128)S(1)}, f32[128,256]{1,0:T(8,128)S(1)}, f32[48,512]{1,0:T(8,128)S(1)}, f32[48,512]{1,0:T(8,128)S(1)}, f32[2,2,64,8,128]{4,3,2,1,0:T(8,128)S(1)}) custom-call(s32[3,8,128]{2,1,0:T(8,128)S(1)} %broadcast_in_dim.2.index_ref, bf16[1024,512]{1,0:T(8,128)(2,1)S(1)} %get-tuple-element.62.mix_ref, ...), custom_call_target="tpu_custom_call" | custom-call | flops 1500000000 | bytes 5000000 | tf_op jit(solution)/shard_map/pallas_call | solution.py:550
  38.0 1.8 %collective-permute-start.9 = (f32[48,512]{1,0:T(8,128)S(1)}, f32[48,512]{1,0:T(8,128)S(1)}, u32[]{:S(2)}, u32[]{:S(2)}) collective-permute-start(f32[48,512]{1,0:T(8,128)S(1)} %get-tuple-element.84), channel_id=1, source_target_pairs={{0,7},{1,2},{2,1},{3,4},{4,3},{5,6},{6,5},{7,0},{8,15},{9,10},{10,... | collective-permute-start | bytes 294920 | tf_op jit(solution)/shard_map/ppermute | solution.py:436
  39.8 2.6 %shard_map.142 = (f32[2,128,256]{2,1,0:T(8,128)S(1)}, f32[128,256]{1,0:T(8,128)S(1)}, f32[48,512]{1,0:T(8,128)S(1)}, f32[48,512]{1,0:T(8,128)S(1)}) custom-call(s32[3,8,128]{2,1,0:T(8,128)S(1)} %broadcast_in_dim.2.index_ref, bf16[1024,512]{1,0:T(8,128)(2,1)S(1)} %get-tuple-element.62.mix_ref, bf16[2048,256]{1,0:T(8,128)(2,1)S(1)} %get-tuple-element.63.high_ref, ...), custom_call_target="tpu_custom_call" | custom-call | flops 1500000000 | bytes 5000000 | tf_op jit(solution)/shard_map/pallas_call | solution.py:550
  42.5 0.7 collective-permute-start.14
  43.1 2.4 %collective-permute-start.15 = (f32[48,512]{1,0:T(8,128)S(1)}, f32[48,512]{1,0:T(8,128)S(1)}, u32[]{:S(2)}, u32[]{:S(2)}) collective-permute-start(f32[48,512]{1,0:T(8,128)S(1)} %get-tuple-element.94), channel_id=1, source_target_pairs={{0,7},{1,2},{2,1},{3,4},{4,3},{5,6},{6,5},{7,0},{8,15},{9,10},{10,... | collective-permute-start | bytes 294920 | tf_op jit(solution)/shard_map/ppermute | solution.py:436
  45.5 0.4 collective-permute-done.9.recv_b
  45.9 2.8 %shard_map.143 = (f32[2,128,256]{2,1,0:T(8,128)S(1)}, f32[128,256]{1,0:T(8,128)S(1)}, f32[48,512]{1,0:T(8,128)S(1)}, f32[48,512]{1,0:T(8,128)S(1)}) custom-call(s32[3,8,128]{2,1,0:T(8,128)S(1)} %broadcast_in_dim.2.index_ref, bf16[1024,512]{1,0:T(8,128)(2,1)S(1)} %get-tuple-element.62.mix_ref, bf16[2048,256]{1,0:T(8,128)(2,1)S(1)} %get-tuple-element.63.high_ref, ...), custom_call_target="tpu_custom_call" | custom-call | flops 1500000000 | bytes 5000000 | tf_op jit(solution)/shard_map/pallas_call | solution.py:550
  48.7 1.7 %collective-permute-done.15.recv_b = f32[48,512]{1,0:T(8,128)S(1)} collective-permute-done((f32[48,512]{1,0:T(8,128)S(1)}, f32[48,512]{1,0:T(8,128)S(1)}, u32[]{:S(2)}, u32[]{:S(2)}) %collective-permute-start.15) | collective-permute-done | bytes 98336 | tf_op jit(solution)/shard_map/ppermute | solution.py:436
  50.4 2.5 %shard_map.144 = (f32[2,128,256]{2,1,0:T(8,128)S(1)}, f32[128,256]{1,0:T(8,128)S(1)}, f32[4,128,256]{2,1,0:T(8,128)}, f32[3,2,32,256]{3,2,1,0:T(8,128)S(1)}, f32[3,2,32,256]{3,2,1,0:T(8,128)S(1)}) custom-call(s32[3,8,128]{2,1,0:T(8,128)S(1)} %broadcast_in_dim.2.index_ref, bf16[1024,512]{1,0:T(8,128)(2,1)S(1)} %get-tuple-element.62.mix_ref, ...), custom_call_target="tpu_custom_call" | custom-call | flops 1500000000 | bytes 5000000 | tf_op jit(solution)/shard_map/pallas_call | solution.py:550
  53.1 2.5 %collective-permute-start.13 = (f32[48,512]{1,0:T(8,128)S(1)}, f32[48,512]{1,0:T(8,128)S(1)}, u32[]{:S(2)}, u32[]{:S(2)}) collective-permute-start(f32[48,512]{1,0:T(8,128)S(1)} %get-tuple-element.91), channel_id=1, source_target_pairs={{0,7},{1,2},{2,1},{3,4},{4,3},{5,6},{6,5},{7,0},{8,15},{9,10},{10,... | collective-permute-start | bytes 294920 | tf_op jit(solution)/shard_map/ppermute | solution.py:436
  55.7 1.6 %collective-permute-start.17 = (f32[3,32,256]{2,1,0:T(8,128)S(1)}, f32[3,32,256]{2,1,0:T(8,128)S(1)}, u32[]{:S(2)}, u32[]{:S(2)}) collective-permute-start(f32[3,32,256]{2,1,0:T(8,128)S(1)} %get-tuple-element.104), channel_id=1, source_target_pairs={{0,16},{8,24},{16,0},{24,8},{1,17},{9,25},{17,1},{25,9},{2,18},{10... | collective-permute-start | bytes 294920 | tf_op jit(solution)/shard_map/ppermute | solution.py:490
  57.3 1.0 %collective-permute-done.12.recv_a = f32[48,512]{1,0:T(8,128)S(1)} collective-permute-done((f32[48,512]{1,0:T(8,128)S(1)}, f32[48,512]{1,0:T(8,128)S(1)}, u32[]{:S(2)}, u32[]{:S(2)}) %collective-permute-start.12) | collective-permute-done | bytes 98336 | tf_op jit(solution)/shard_map/ppermute | solution.py:435
  58.3 2.7 %collective-permute-done.13.recv_b = f32[48,512]{1,0:T(8,128)S(1)} collective-permute-done((f32[48,512]{1,0:T(8,128)S(1)}, f32[48,512]{1,0:T(8,128)S(1)}, u32[]{:S(2)}, u32[]{:S(2)}) %collective-permute-start.13) | collective-permute-done | bytes 98336 | tf_op jit(solution)/shard_map/ppermute | solution.py:436
  61.0 3.2 %shard_map.145 = (f32[2,128,256]{2,1,0:T(8,128)S(1)}, f32[128,256]{1,0:T(8,128)}, f32[4,128,256]{2,1,0:T(8,128)}, f32[32,256]{1,0:T(8,128)S(1)}, f32[32,256]{1,0...) custom-call(s32[3,8,128]{2,1,0:T(8,128)S(1)} %broadcast_in_dim.2.index_ref, ...), custom_call_target="tpu_custom_call", output_to_operand_aliasing={{2}: (12, {})} | custom-call | flops 1500000000 | bytes 5000000 | tf_op jit(solution)/shard_map/pallas_call | solution.py:550
  64.2 1.6 %collective-permute-start.18 = (f32[32,256]{1,0:T(8,128)S(1)}, f32[32,256]{1,0:T(8,128)S(1)}, u32[]{:S(2)}, u32[]{:S(2)}) collective-permute-start(f32[32,256]{1,0:T(8,128)S(1)} %get-tuple-element.110), channel_id=1, source_target_pairs={{0,16},{8,24},{16,0},{24,8},{1,17},{9,25},{17,1},{25,9},{2,18},{10... | collective-permute-start | bytes 98312 | tf_op jit(solution)/shard_map/ppermute | solution.py:573
  65.7 0.6 collective-permute-start.20
  66.4 1.8 %collective-permute-done.18.rest_5_ = f32[32,256]{1,0:T(8,128)S(1)} collective-permute-done((f32[32,256]{1,0:T(8,128)S(1)}, f32[32,256]{1,0:T(8,128)S(1)}, u32[]{:S(2)}, u32[]{:S(2)}) %collective-permute-start.18) | collective-permute-done | bytes 32800 | tf_op jit(solution)/shard_map/ppermute | solution.py:573
  68.1 0.9 %collective-permute-done.19.rest_6_ = f32[32,256]{1,0:T(8,128)S(1)} collective-permute-done((f32[32,256]{1,0:T(8,128)S(1)}, f32[32,256]{1,0:T(8,128)S(1)}, u32[]{:S(2)}, u32[]{:S(2)}) %collective-permute-start.19) | collective-permute-done | bytes 32800 | tf_op jit(solution)/shard_map/ppermute | solution.py:573
  69.1 7.3 %energy.1 = (f32[4,32,256]{2,1,0:T(8,128)}, f32[512,32,256]{2,1,0:T(8,128)}, f32[4,128,256]{2,1,0:T(8,128)}) custom-call(bf16[256,256]{1,0:T(8,128)(2,1)S(1)} %copy-done.1, bf16[256,256]{1,0:T(8,128)(2,1)S(1)} %copy-done, f32[3,32,256]{2,1,0:T(8,128)S(1)} %get-tuple-element.103.early_mine, f32[3,32,256]{2,1,0:T(8,128)S(1)} %collective-permute-done.17.early_got, ...), custom_call_target="tpu_custom_call" | custom-call | flops 4000000000 | bytes 22000000 | tf_op jit(solution)/shard_map/energy/pallas_call | solution.py:581
  (28 shorter events, 0.7 us)
Async XLA Ops:
  2.1 11.1 %collective-permute-start.2 = (f32[48,512]{1,0:T(8,128)S(1)}, f32[48,512]{1,0:T(8,128)S(1)}, u32[]{:S(2)}, u32[]{:S(2)}) collective-permute-start(f32[48,512]{1,0:T(8,128)S(1)} %get-tuple-element.72), channel_id=1, source_target_pairs={{0,1},{1,0},{2,3},{3,2},{4,5},{5,4},{6,7},{7,6},{8,9},{9,8},{10,11... | collective-permute-start | bytes 294920 | tf_op jit(solution)/shard_map/ppermute | solution.py:435
  5.1 8.0 %collective-permute-start.3 = (f32[48,512]{1,0:T(8,128)S(1)}, f32[48,512]{1,0:T(8,128)S(1)}, u32[]{:S(2)}, u32[]{:S(2)}) collective-permute-start(f32[48,512]{1,0:T(8,128)S(1)} %get-tuple-element.73), channel_id=1, source_target_pairs={{0,7},{1,2},{2,1},{3,4},{4,3},{5,6},{6,5},{7,0},{8,15},{9,10},{10,... | collective-permute-start | bytes 294920 | tf_op jit(solution)/shard_map/ppermute | solution.py:436
  11.2 8.9 %collective-permute-start = (f32[48,512]{1,0:T(8,128)S(1)}, f32[48,512]{1,0:T(8,128)S(1)}, u32[]{:S(2)}, u32[]{:S(2)}) collective-permute-start(f32[48,512]{1,0:T(8,128)S(1)} %get-tuple-element.69), channel_id=1, source_target_pairs={{0,1},{1,0},{2,3},{3,2},{4,5},{5,4},{6,7},{7,6},{8,9},{9,8},{10,11... | collective-permute-start | bytes 294920 | tf_op jit(solution)/shard_map/ppermute | solution.py:435
  11.3 8.8 %collective-permute-start.1 = (f32[48,512]{1,0:T(8,128)S(1)}, f32[48,512]{1,0:T(8,128)S(1)}, u32[]{:S(2)}, u32[]{:S(2)}) collective-permute-start(f32[48,512]{1,0:T(8,128)S(1)} %get-tuple-element.70), channel_id=1, source_target_pairs={{0,7},{1,2},{2,1},{3,4},{4,3},{5,6},{6,5},{7,0},{8,15},{9,10},{10,... | collective-permute-start | bytes 294920 | tf_op jit(solution)/shard_map/ppermute | solution.py:436
  17.1 9.4 %collective-permute-start.6 = (f32[48,512]{1,0:T(8,128)S(1)}, f32[48,512]{1,0:T(8,128)S(1)}, u32[]{:S(2)}, u32[]{:S(2)}) collective-permute-start(f32[48,512]{1,0:T(8,128)S(1)} %get-tuple-element.79), channel_id=1, source_target_pairs={{0,1},{1,0},{2,3},{3,2},{4,5},{5,4},{6,7},{7,6},{8,9},{9,8},{10,11... | collective-permute-start | bytes 294920 | tf_op jit(solution)/shard_map/ppermute | solution.py:435
  17.7 8.8 %collective-permute-start.7 = (f32[48,512]{1,0:T(8,128)S(1)}, f32[48,512]{1,0:T(8,128)S(1)}, u32[]{:S(2)}, u32[]{:S(2)}) collective-permute-start(f32[48,512]{1,0:T(8,128)S(1)} %get-tuple-element.80), channel_id=1, source_target_pairs={{0,7},{1,2},{2,1},{3,4},{4,3},{5,6},{6,5},{7,0},{8,15},{9,10},{10,... | collective-permute-start | bytes 294920 | tf_op jit(solution)/shard_map/ppermute | solution.py:436
  24.0 9.9 %collective-permute-start.4 = (f32[48,512]{1,0:T(8,128)S(1)}, f32[48,512]{1,0:T(8,128)S(1)}, u32[]{:S(2)}, u32[]{:S(2)}) collective-permute-start(f32[48,512]{1,0:T(8,128)S(1)} %get-tuple-element.76), channel_id=1, source_target_pairs={{0,1},{1,0},{2,3},{3,2},{4,5},{5,4},{6,7},{7,6},{8,9},{9,8},{10,11... | collective-permute-start | bytes 294920 | tf_op jit(solution)/shard_map/ppermute | solution.py:435
  24.7 9.2 %collective-permute-start.5 = (f32[48,512]{1,0:T(8,128)S(1)}, f32[48,512]{1,0:T(8,128)S(1)}, u32[]{:S(2)}, u32[]{:S(2)}) collective-permute-start(f32[48,512]{1,0:T(8,128)S(1)} %get-tuple-element.77), channel_id=1, source_target_pairs={{0,7},{1,2},{2,1},{3,4},{4,3},{5,6},{6,5},{7,0},{8,15},{9,10},{10,... | collective-permute-start | bytes 294920 | tf_op jit(solution)/shard_map/ppermute | solution.py:436
  30.4 9.4 %collective-permute-start.10 = (f32[48,512]{1,0:T(8,128)S(1)}, f32[48,512]{1,0:T(8,128)S(1)}, u32[]{:S(2)}, u32[]{:S(2)}) collective-permute-start(f32[48,512]{1,0:T(8,128)S(1)} %get-tuple-element.86), channel_id=1, source_target_pairs={{0,1},{1,0},{2,3},{3,2},{4,5},{5,4},{6,7},{7,6},{8,9},{9,8},{10,11... | collective-permute-start | bytes 294920 | tf_op jit(solution)/shard_map/ppermute | solution.py:435
  30.5 9.4 %collective-permute-start.11 = (f32[48,512]{1,0:T(8,128)S(1)}, f32[48,512]{1,0:T(8,128)S(1)}, u32[]{:S(2)}, u32[]{:S(2)}) collective-permute-start(f32[48,512]{1,0:T(8,128)S(1)} %get-tuple-element.87), channel_id=1, source_target_pairs={{0,7},{1,2},{2,1},{3,4},{4,3},{5,6},{6,5},{7,0},{8,15},{9,10},{10,... | collective-permute-start | bytes 294920 | tf_op jit(solution)/shard_map/ppermute | solution.py:436
  37.8 7.7 %collective-permute-start.8 = (f32[48,512]{1,0:T(8,128)S(1)}, f32[48,512]{1,0:T(8,128)S(1)}, u32[]{:S(2)}, u32[]{:S(2)}) collective-permute-start(f32[48,512]{1,0:T(8,128)S(1)} %get-tuple-element.83), channel_id=1, source_target_pairs={{0,1},{1,0},{2,3},{3,2},{4,5},{5,4},{6,7},{7,6},{8,9},{9,8},{10,11... | collective-permute-start | bytes 294920 | tf_op jit(solution)/shard_map/ppermute | solution.py:435
  38.0 7.9 %collective-permute-start.9 = (f32[48,512]{1,0:T(8,128)S(1)}, f32[48,512]{1,0:T(8,128)S(1)}, u32[]{:S(2)}, u32[]{:S(2)}) collective-permute-start(f32[48,512]{1,0:T(8,128)S(1)} %get-tuple-element.84), channel_id=1, source_target_pairs={{0,7},{1,2},{2,1},{3,4},{4,3},{5,6},{6,5},{7,0},{8,15},{9,10},{10,... | collective-permute-start | bytes 294920 | tf_op jit(solution)/shard_map/ppermute | solution.py:436
  42.5 6.2 %collective-permute-start.14 = (f32[48,512]{1,0:T(8,128)S(1)}, f32[48,512]{1,0:T(8,128)S(1)}, u32[]{:S(2)}, u32[]{:S(2)}) collective-permute-start(f32[48,512]{1,0:T(8,128)S(1)} %get-tuple-element.93), channel_id=1, source_target_pairs={{0,1},{1,0},{2,3},{3,2},{4,5},{5,4},{6,7},{7,6},{8,9},{9,8},{10,11... | collective-permute-start | bytes 294920 | tf_op jit(solution)/shard_map/ppermute | solution.py:435
  43.1 7.3 %collective-permute-start.15 = (f32[48,512]{1,0:T(8,128)S(1)}, f32[48,512]{1,0:T(8,128)S(1)}, u32[]{:S(2)}, u32[]{:S(2)}) collective-permute-start(f32[48,512]{1,0:T(8,128)S(1)} %get-tuple-element.94), channel_id=1, source_target_pairs={{0,7},{1,2},{2,1},{3,4},{4,3},{5,6},{6,5},{7,0},{8,15},{9,10},{10,... | collective-permute-start | bytes 294920 | tf_op jit(solution)/shard_map/ppermute | solution.py:436
  53.0 16.1 %copy-start = (bf16[256,256]{1,0:T(8,128)(2,1)S(1)}, bf16[256,256]{1,0:T(8,128)(2,1)}, u32[]{:S(2)}) copy-start(bf16[256,256]{1,0:T(8,128)(2,1)} %constant.41.clone.odd_ref) | copy-start | bytes 393220
  53.0 16.1 %copy-start.1 = (bf16[256,256]{1,0:T(8,128)(2,1)S(1)}, bf16[256,256]{1,0:T(8,128)(2,1)}, u32[]{:S(2)}) copy-start(bf16[256,256]{1,0:T(8,128)(2,1)} %constant.40.clone.even_ref) | copy-start | bytes 393220
  53.0 2.7 %collective-permute-start.16 = (f32[3,2,32,256]{3,2,1,0:T(8,128)S(1)}, f32[3,2,32,256]{3,2,1,0:T(8,128)S(1)}, u32[]{:S(2)}, u32[]{:S(2)}) collective-permute-start(f32[3,2,32,256]{3,2,1,0:T(8,128)S(1)} %get-tuple-element.102), channel_id=1, source_target_pairs={{0,8},{8,0},{16,24},{24,16},{1,9},{9,1},{17,25},{25,17},{2,10},{10... | collective-permute-start | bytes 589832 | tf_op jit(solution)/shard_map/ppermute | solution.py:479
  53.1 5.2 %collective-permute-start.12 = (f32[48,512]{1,0:T(8,128)S(1)}, f32[48,512]{1,0:T(8,128)S(1)}, u32[]{:S(2)}, u32[]{:S(2)}) collective-permute-start(f32[48,512]{1,0:T(8,128)S(1)} %get-tuple-element.90), channel_id=1, source_target_pairs={{0,1},{1,0},{2,3},{3,2},{4,5},{5,4},{6,7},{7,6},{8,9},{9,8},{10,11... | collective-permute-start | bytes 294920 | tf_op jit(solution)/shard_map/ppermute | solution.py:435
  53.1 7.8 %collective-permute-start.13 = (f32[48,512]{1,0:T(8,128)S(1)}, f32[48,512]{1,0:T(8,128)S(1)}, u32[]{:S(2)}, u32[]{:S(2)}) collective-permute-start(f32[48,512]{1,0:T(8,128)S(1)} %get-tuple-element.91), channel_id=1, source_target_pairs={{0,7},{1,2},{2,1},{3,4},{4,3},{5,6},{6,5},{7,0},{8,15},{9,10},{10,... | collective-permute-start | bytes 294920 | tf_op jit(solution)/shard_map/ppermute | solution.py:436
  55.7 13.4 %collective-permute-start.17 = (f32[3,32,256]{2,1,0:T(8,128)S(1)}, f32[3,32,256]{2,1,0:T(8,128)S(1)}, u32[]{:S(2)}, u32[]{:S(2)}) collective-permute-start(f32[3,32,256]{2,1,0:T(8,128)S(1)} %get-tuple-element.104), channel_id=1, source_target_pairs={{0,16},{8,24},{16,0},{24,8},{1,17},{9,25},{17,1},{25,9},{2,18},{10... | collective-permute-start | bytes 294920 | tf_op jit(solution)/shard_map/ppermute | solution.py:490
  64.2 4.0 %collective-permute-start.18 = (f32[32,256]{1,0:T(8,128)S(1)}, f32[32,256]{1,0:T(8,128)S(1)}, u32[]{:S(2)}, u32[]{:S(2)}) collective-permute-start(f32[32,256]{1,0:T(8,128)S(1)} %get-tuple-element.110), channel_id=1, source_target_pairs={{0,16},{8,24},{16,0},{24,8},{1,17},{9,25},{17,1},{25,9},{2,18},{10... | collective-permute-start | bytes 98312 | tf_op jit(solution)/shard_map/ppermute | solution.py:573
  65.7 3.3 %collective-permute-start.19 = (f32[32,256]{1,0:T(8,128)S(1)}, f32[32,256]{1,0:T(8,128)S(1)}, u32[]{:S(2)}, u32[]{:S(2)}) collective-permute-start(f32[32,256]{1,0:T(8,128)S(1)} %get-tuple-element.111), channel_id=1, source_target_pairs={{0,24},{8,16},{16,8},{24,0},{1,25},{9,17},{17,9},{25,1},{2,26},{10... | collective-permute-start | bytes 98312 | tf_op jit(solution)/shard_map/ppermute | solution.py:573
  65.7 3.3 %collective-permute-start.20 = (f32[32,256]{1,0:T(8,128)S(1)}, f32[32,256]{1,0:T(8,128)S(1)}, u32[]{:S(2)}, u32[]{:S(2)}) collective-permute-start(f32[32,256]{1,0:T(8,128)S(1)} %get-tuple-element.112), channel_id=1, source_target_pairs={{0,8},{8,0},{16,24},{24,16},{1,9},{9,1},{17,25},{25,17},{2,10},{10... | collective-permute-start | bytes 98312 | tf_op jit(solution)/shard_map/ppermute | solution.py:573
